TPU v7x, 32 devices: a whole 2x2x4 slice. The times are simulated.
32 devices in a mesh: groups: 2 (over y), seq: 4 (over z), head: 4 (over x, core).
Axes of the slice: x: 2, y: 2, z: 4, core: 2. Of those that a mesh axis runs over, the one named last changes fastest.
Arguments:
- segment_query: bfloat16 [512, 4096], P(('groups', 'seq'), 'head'), parts along dimension 0, may hold values from -8 to 8
- segment_memory: bfloat16 [512, 2, 1024], P(('groups', 'seq'), None, 'head'), parts along dimension 0, may hold values from -8 to 8
- finished_memory: bfloat16 [2048, 2, 1024], P(('groups', 'seq'), None, 'head'), parts along dimension 0, may hold values from -8 to 8
- cache_memory: bfloat16 [32768, 2, 1024], P(('groups', 'seq'), None, 'head'), parts along dimension 0, may hold values from -8 to 8
- block_mask: int32 [4, 128], P('groups', 'seq'), parts along dimension 0, may hold values 0 or 1
- owner_index: int32 [2], P('groups'), parts along dimension 0, may hold values from 0 to 3
- valid_count: int32 [2], P('groups'), parts along dimension 0, may hold values from 1 to 256
- output_weight: bfloat16 [4096, 4096], P('head', 'seq'), may hold values from -0.09375 to 0.09375
Outputs:
- mixed_output: float32 [512, 4096], P(('groups', 'head'), 'seq'), parts along dimension 0
There are 2 independent parts, one for each index of `groups`. A program takes and returns all parts, laid end to end along the dimension named above; an argument that names none is the same for every part. Nothing has to cross between parts.
All inputs are finite; a program needn't handle non-finite values. No bound on the sum of `block_mask` on one device may be relied on, other than what follows from the above.
Results may differ from a plain program's by a relative error of at most 0.0065.
Values may be sent and summed in bfloat16 or wider, within the bound.
No kernel may reach another device: no remote copies, remote signals or barrier semaphores. Data moves between devices by JAX's collectives and lax.ppermute only.
A program may use at most 128 MiB of HBM per device.

v0:
```python
import jax
import jax.numpy as jnp
from jax import lax
from jax.sharding import PartitionSpec as P

HD = 128
BLOCK = 128


floor_value = -1e30


def merged(value, axis, join):
    pieces = jax.tree.map(lambda part: lax.all_gather(part, axis), value)
    head = jax.tree.map(lambda part: part[0], pieces)
    tail = jax.tree.map(lambda part: part[1:], pieces)
    running, _ = lax.scan(lambda running, slab: (join(running, slab), None), head, tail)
    return running


def attend(queries, key_rows, value_rows, valid_mask):
    scores = jnp.einsum(
        "rkgd,tkd->rkgt", queries, key_rows, preferred_element_type=jnp.float32
    ) * queries.shape[-1] ** (-0.5)
    allowed = valid_mask[:, None, None, :]
    scores = jnp.where(allowed, scores, floor_value)
    row_peak = jnp.max(scores, axis=-1)
    weights = jnp.where(allowed, jnp.exp(scores - row_peak[..., None]), 0.0)
    row_total = jnp.sum(weights, axis=-1)
    summed = jnp.einsum(
        "rkgt,tkd->rkgd",
        weights.astype(jnp.bfloat16),
        value_rows,
        preferred_element_type=jnp.float32,
    )
    return (row_peak, row_total, summed)


def join(first_part, second_part):
    row_peak = jnp.maximum(first_part[0], second_part[0])
    first_factor = jnp.exp(first_part[0] - row_peak)
    second_factor = jnp.exp(second_part[0] - row_peak)
    row_total = first_part[1] * first_factor + second_part[1] * second_factor
    summed = first_part[2] * first_factor[..., None] + second_part[2] * second_factor[..., None]
    return (row_peak, row_total, summed)


def per_device(
    segment_query,
    segment_memory,
    finished_memory,
    cache_memory,
    block_mask,
    owner_index,
    valid_count,
    output_weight,
):
    queries_flat, fresh_rows = (
        lax.all_gather(segment_query, "seq", axis=0, tiled=True),
        lax.all_gather(segment_memory, "seq", axis=0, tiled=True),
    )
    segment_len = queries_flat.shape[0]
    kv_local = segment_memory.shape[2] // HD
    group_size = queries_flat.shape[1] // (kv_local * HD)
    queries = queries_flat.reshape(segment_len, kv_local, group_size, HD)
    stat_shape = (segment_len, kv_local, group_size)
    empty_state = (
        jnp.full(stat_shape, floor_value, jnp.float32),
        jnp.zeros(stat_shape, jnp.float32),
        jnp.zeros(stat_shape + (HD,), jnp.float32),
    )

    def recent_part(finished_rows, query_rows):
        pairs = jnp.concatenate([finished_rows, fresh_rows], axis=0)
        key_rows = pairs[:, 0].reshape(-1, kv_local, HD)
        value_rows = pairs[:, 1].reshape(-1, kv_local, HD)
        positions = lax.broadcasted_iota(jnp.int32, (1, 2 * segment_len), 1)
        valid_mask = jnp.broadcast_to(
            positions < segment_len + valid_count[0], (query_rows.shape[0], 2 * segment_len)
        )
        return attend(query_rows, key_rows, value_rows, valid_mask)

    start_state = lax.cond(
        lax.axis_index("seq") == owner_index[0],
        lambda: recent_part(finished_memory, queries),
        lambda: empty_state,
    )
    tile_size = min(512, cache_memory.shape[0])
    tile_count = cache_memory.shape[0] // tile_size
    tile_blocks = tile_size // BLOCK
    query_blocks = segment_len // BLOCK
    cache_tiles = cache_memory.reshape(tile_count, tile_size, 2, kv_local, HD)
    mask_tiles = block_mask.reshape(query_blocks, tile_count, tile_blocks).transpose(1, 0, 2)

    def advance(partial_value, inputs):
        tile_rows, tile_mask = inputs
        expanded = jnp.broadcast_to(
            tile_mask[:, None, :, None] > 0, (query_blocks, BLOCK, tile_blocks, BLOCK)
        ).reshape(segment_len, tile_size)
        return (
            join(partial_value, attend(queries, tile_rows[:, 0], tile_rows[:, 1], expanded)),
            None,
        )

    state, ignored = lax.scan(advance, start_state, (cache_tiles, mask_tiles))
    row_peak, row_total, summed = merged(state, "seq", join)
    attended = (summed / row_total[..., None]).astype(jnp.bfloat16).reshape(segment_len, -1)
    return lax.psum_scatter(
        jnp.dot(attended, output_weight, preferred_element_type=jnp.float32),
        "head",
        scatter_dimension=0,
        tiled=True,
    )


def solution(mesh):
    return jax.shard_map(
        per_device,
        mesh=mesh,
        in_specs=(
            P(("groups", "seq"), "head"),
            P(("groups", "seq"), None, "head"),
            P(("groups", "seq"), None, "head"),
            P(("groups", "seq"), None, "head"),
            P("groups", "seq"),
            P("groups"),
            P("groups"),
            P("head", "seq"),
        ),
        out_specs=P(("groups", "head"), "seq"),
        check_vma=False,
    )
```

profile of v0, /device:TPU:0, one launch (start us, length us, event | category | flops | bytes accessed | tf_op | source)
XLA Modules:
  0.0 266.5 jit_solution(16382702717518910027)
XLA Ops:
  8.1 15.8 %all_gather.24 = bf16[256,2,256]{2,1,0:T(2,128)(2,1)S(1)} all-gather(bf16[64,2,256]{2,1,0:T(2,128)(2,1)} %param.15), channel_id=1, replica_groups=mesh['groups'=2,'seq'=4,'head'=4] {'seq'}, dimensions={0}, use_global_device_ids=true | all-gather | bytes 327680 | tf_op jit(solution)/shard_map/all_gather | solution.py:60
  23.9 16.4 %all_gather.25 = bf16[256,1024]{1,0:T(8,128)(2,1)S(1)} all-gather(bf16[64,1024]{1,0:T(8,128)(2,1)} %param.14), channel_id=1, replica_groups=mesh['groups'=2,'seq'=4,'head'=4] {'seq'}, dimensions={0}, use_global_device_ids=true | all-gather | bytes 655360 | tf_op jit(solution)/shard_map/all_gather | solution.py:59
  40.8 11.7 %reshape.61 = bf16[8,512,2,2,128]{4,3,2,1,0:T(2,128)(2,1)} reshape(bf16[4096,2,256]{2,1,0:T(2,128)(2,1)} %param.17) | data formatting | bytes 8388608 | tf_op jit(solution)/shard_map/reshape | solution.py:92
  52.5 1.7 conditional.1
  54.2 68.9 %while.28 = (s32[]{:T(128)}, f32[256,2,4]{0,2,1:T(4,128)}, f32[256,2,4]{0,2,1:T(4,128)S(1)}, f32[256,2,4,128]{0,3,2,1:T(8,128)}, s32[8,2,4]{2,0,1:T(8,128)S(1)},...) while((s32[]{:T(128)}, f32[256,2,4]{0,2,1:T(4,128)}, ...), condition=%wide.region_7.8_spmd, body=%wide.region_4.7_spmd.sunk | while | flops 551297024 | bytes 18989268 | solution.py:105
  59.4 3.5 %fusion.57 = f32[256,2,4,128]{0,3,2,1:T(8,128)} fusion(f32[2,512,256,4]{2,1,3,0:T(8,128)S(1)} %get-tuple-element.299, f32[256,2,4]{0,2,1:T(4,128)S(1)} %get-tuple-element.300, pred[256,512]{0,1:T(8,128)(4,1)S(1)} %copy.103, f32[256,2,4,128]{0,3,2,1:T(8,128)} %get-tuple-element.335, f32[256,2,4]{0,2,1:T(4,128)S(1)} %bitcast.175, ...), kind=kOutput, calls=%fused_computation.28.clone.1 | convolution fusion | flops 274464768 | bytes 6709248 | tf_op jit(solution)/shard_map/while/body/eval_jaxpr/rkgt,tkd->rkgd/dot_general | solution.py:30
  68.0 3.5 %fusion.57 = f32[256,2,4,128]{0,3,2,1:T(8,128)} fusion(f32[2,512,256,4]{2,1,3,0:T(8,128)S(1)} %get-tuple-element.299, f32[256,2,4]{0,2,1:T(4,128)S(1)} %get-tuple-element.300, pred[256,512]{0,1:T(8,128)(4,1)S(1)} %copy.103, f32[256,2,4,128]{0,3,2,1:T(8,128)} %get-tuple-element.335, f32[256,2,4]{0,2,1:T(4,128)S(1)} %bitcast.175, ...), kind=kOutput, calls=%fused_computation.28.clone.1 | convolution fusion | flops 274464768 | bytes 6709248 | tf_op jit(solution)/shard_map/while/body/eval_jaxpr/rkgt,tkd->rkgd/dot_general | solution.py:30
  76.6 3.5 %fusion.57 = f32[256,2,4,128]{0,3,2,1:T(8,128)} fusion(f32[2,512,256,4]{2,1,3,0:T(8,128)S(1)} %get-tuple-element.299, f32[256,2,4]{0,2,1:T(4,128)S(1)} %get-tuple-element.300, pred[256,512]{0,1:T(8,128)(4,1)S(1)} %copy.103, f32[256,2,4,128]{0,3,2,1:T(8,128)} %get-tuple-element.335, f32[256,2,4]{0,2,1:T(4,128)S(1)} %bitcast.175, ...), kind=kOutput, calls=%fused_computation.28.clone.1 | convolution fusion | flops 274464768 | bytes 6709248 | tf_op jit(solution)/shard_map/while/body/eval_jaxpr/rkgt,tkd->rkgd/dot_general | solution.py:30
  85.2 3.5 %fusion.57 = f32[256,2,4,128]{0,3,2,1:T(8,128)} fusion(f32[2,512,256,4]{2,1,3,0:T(8,128)S(1)} %get-tuple-element.299, f32[256,2,4]{0,2,1:T(4,128)S(1)} %get-tuple-element.300, pred[256,512]{0,1:T(8,128)(4,1)S(1)} %copy.103, f32[256,2,4,128]{0,3,2,1:T(8,128)} %get-tuple-element.335, f32[256,2,4]{0,2,1:T(4,128)S(1)} %bitcast.175, ...), kind=kOutput, calls=%fused_computation.28.clone.1 | convolution fusion | flops 274464768 | bytes 6709248 | tf_op jit(solution)/shard_map/while/body/eval_jaxpr/rkgt,tkd->rkgd/dot_general | solution.py:30
  93.8 3.5 %fusion.57 = f32[256,2,4,128]{0,3,2,1:T(8,128)} fusion(f32[2,512,256,4]{2,1,3,0:T(8,128)S(1)} %get-tuple-element.299, f32[256,2,4]{0,2,1:T(4,128)S(1)} %get-tuple-element.300, pred[256,512]{0,1:T(8,128)(4,1)S(1)} %copy.103, f32[256,2,4,128]{0,3,2,1:T(8,128)} %get-tuple-element.335, f32[256,2,4]{0,2,1:T(4,128)S(1)} %bitcast.175, ...), kind=kOutput, calls=%fused_computation.28.clone.1 | convolution fusion | flops 274464768 | bytes 6709248 | tf_op jit(solution)/shard_map/while/body/eval_jaxpr/rkgt,tkd->rkgd/dot_general | solution.py:30
  102.4 3.5 %fusion.57 = f32[256,2,4,128]{0,3,2,1:T(8,128)} fusion(f32[2,512,256,4]{2,1,3,0:T(8,128)S(1)} %get-tuple-element.299, f32[256,2,4]{0,2,1:T(4,128)S(1)} %get-tuple-element.300, pred[256,512]{0,1:T(8,128)(4,1)S(1)} %copy.103, f32[256,2,4,128]{0,3,2,1:T(8,128)} %get-tuple-element.335, f32[256,2,4]{0,2,1:T(4,128)S(1)} %bitcast.175, ...), kind=kOutput, calls=%fused_computation.28.clone.1 | convolution fusion | flops 274464768 | bytes 6709248 | tf_op jit(solution)/shard_map/while/body/eval_jaxpr/rkgt,tkd->rkgd/dot_general | solution.py:30
  111.0 3.5 %fusion.57 = f32[256,2,4,128]{0,3,2,1:T(8,128)} fusion(f32[2,512,256,4]{2,1,3,0:T(8,128)S(1)} %get-tuple-element.299, f32[256,2,4]{0,2,1:T(4,128)S(1)} %get-tuple-element.300, pred[256,512]{0,1:T(8,128)(4,1)S(1)} %copy.103, f32[256,2,4,128]{0,3,2,1:T(8,128)} %get-tuple-element.335, f32[256,2,4]{0,2,1:T(4,128)S(1)} %bitcast.175, ...), kind=kOutput, calls=%fused_computation.28.clone.1 | convolution fusion | flops 274464768 | bytes 6709248 | tf_op jit(solution)/shard_map/while/body/eval_jaxpr/rkgt,tkd->rkgd/dot_general | solution.py:30
  119.6 3.5 %fusion.57 = f32[256,2,4,128]{0,3,2,1:T(8,128)} fusion(f32[2,512,256,4]{2,1,3,0:T(8,128)S(1)} %get-tuple-element.299, f32[256,2,4]{0,2,1:T(4,128)S(1)} %get-tuple-element.300, pred[256,512]{0,1:T(8,128)(4,1)S(1)} %copy.103, f32[256,2,4,128]{0,3,2,1:T(8,128)} %get-tuple-element.335, f32[256,2,4]{0,2,1:T(4,128)S(1)} %bitcast.175, ...), kind=kOutput, calls=%fused_computation.28.clone.1 | convolution fusion | flops 274464768 | bytes 6709248 | tf_op jit(solution)/shard_map/while/body/eval_jaxpr/rkgt,tkd->rkgd/dot_general | solution.py:30
  123.1 2.5 copy.58
  125.7 20.0 %all-gather = f32[1024,2,4]{0,2,1:T(4,128)S(1)} all-gather(f32[256,2,4]{0,2,1:T(4,128)} %get-tuple-element.100), channel_id=2, replica_groups=mesh['groups'=2,'seq'=4,'head'=4] {'seq'}, dimensions={0}, use_global_device_ids=true | all-gather | bytes 40960 | tf_op jit(solution)/shard_map/all_gather | solution.py:14
  145.7 13.6 %all-gather.1 = f32[1024,2,4]{0,2,1:T(4,128)S(1)} all-gather(f32[256,2,4]{0,2,1:T(4,128)S(1)} %get-tuple-element.101), channel_id=3, replica_groups=mesh['groups'=2,'seq'=4,'head'=4] {'seq'}, dimensions={0}, use_global_device_ids=true | all-gather | bytes 40960 | tf_op jit(solution)/shard_map/all_gather | solution.py:14
  159.3 53.9 %all-gather.5.cloned.1.call-done = f32[1024,2,4,128]{3,2,1,0:T(4,128)} async-done(((f32[256,2,4,128]{3,2,1,0:T(4,128)}), f32[1024,2,4,128]{3,2,1,0:T(4,128)}) %all-gather.5.cloned.1.call-update) | async-done | bytes 4194320 | tf_op jit(solution)/shard_map/all_gather | solution.py:14
  213.2 4.2 %slice.51 = f32[768,2,4,128]{3,2,1,0:T(4,128)} slice(f32[1024,2,4,128]{3,2,1,0:T(4,128)} %all-gather.5.cloned.1.call-done), slice={[256:1024], [0:2], [0:4], [0:128]} | slice | bytes 6291456 | tf_op jit(solution)/shard_map/slice | solution.py:16
  217.4 13.7 %while.29 = (s32[]{:T(128)}, f32[256,2,4]{0,2,1:T(4,128)S(1)}, f32[256,2,4]{0,2,1:T(4,128)S(1)}, f32[256,2,4,128]{3,2,1,0:T(4,128)S(1)}, f32[3,256,2,4]{1,0,3,2:...) while((s32[]{:T(128)}, f32[256,2,4]{0,2,1:T(4,128)S(1)}, ...), condition=%wide.region_9.10_spmd, body=%wide.region_8.9_spmd.sunk | while | flops 798722 | bytes 3293285 | solution.py:17
  218.5 3.5 %fusion.59 = f32[256,2,4,128]{3,2,1,0:T(4,128)S(1)} fusion(f32[3,256,2,4,128]{4,3,2,1,0:T(4,128)} %get-tuple-element.370, s32[]{:T(128)S(6)} %copy.130, f32[256,2,4,128]{3,2,1,0:T(4,128)S(1)} %get-tuple-element.359, f32[256,2,4]{2,1,0:T(2,128)S(1)} %copy.106, f32[256,2,4]{2,1,0:T(2,128)} %copy.107), kind=kLoop, calls=%fused_computation.44.clone.1 | loop fusion | flops 786432 | bytes 3162116 | tf_op jit(solution)/shard_map/while/body/eval_jaxpr/add | solution.py:44
  223.1 3.5 %fusion.59 = f32[256,2,4,128]{3,2,1,0:T(4,128)S(1)} fusion(f32[3,256,2,4,128]{4,3,2,1,0:T(4,128)} %get-tuple-element.370, s32[]{:T(128)S(6)} %copy.130, f32[256,2,4,128]{3,2,1,0:T(4,128)S(1)} %get-tuple-element.359, f32[256,2,4]{2,1,0:T(2,128)S(1)} %copy.106, f32[256,2,4]{2,1,0:T(2,128)} %copy.107), kind=kLoop, calls=%fused_computation.44.clone.1 | loop fusion | flops 786432 | bytes 3162116 | tf_op jit(solution)/shard_map/while/body/eval_jaxpr/add | solution.py:44
  227.7 3.5 %fusion.59 = f32[256,2,4,128]{3,2,1,0:T(4,128)S(1)} fusion(f32[3,256,2,4,128]{4,3,2,1,0:T(4,128)} %get-tuple-element.370, s32[]{:T(128)S(6)} %copy.130, f32[256,2,4,128]{3,2,1,0:T(4,128)S(1)} %get-tuple-element.359, f32[256,2,4]{2,1,0:T(2,128)S(1)} %copy.106, f32[256,2,4]{2,1,0:T(2,128)} %copy.107), kind=kLoop, calls=%fused_computation.44.clone.1 | loop fusion | flops 786432 | bytes 3162116 | tf_op jit(solution)/shard_map/while/body/eval_jaxpr/add | solution.py:44
  234.2 1.7 fusion.39
  235.9 23.8 %reduce-scatter.2.cloned.1.call-done = f32[64,1024]{1,0:T(8,128)} async-done(((f32[256,1024]{1,0:T(8,128)}), f32[64,1024]{1,0:T(8,128)}) %reduce-scatter.2.cloned.1.call-update) | async-done | bytes 262160 | tf_op jit(solution)/shard_map/reduce_scatter | solution.py:108
  (115 shorter events, 50.0 us)
Async XLA Ops:
  6.5 227.6 %copy-start = (bf16[1024,1024]{1,0:T(8,128)(2,1)S(1)}, bf16[1024,1024]{1,0:T(8,128)(2,1)}, u32[]{:S(2)}) copy-start(bf16[1024,1024]{1,0:T(8,128)(2,1)} %param.21) | copy-start | bytes 6291460
  6.5 206.7 %all-gather.5.cloned.1.call-start = ((), (), s32[]{:S(2)}) async-start(), calls=%async_computation.2 | async-start | bytes 5242880 | tf_op jit(solution)/shard_map/all_gather | solution.py:14
  125.7 134.0 %reduce-scatter.2.cloned.1.call-start = ((), (), s32[]{:S(2)}) async-start(), calls=%async_computation.1 | async-start | bytes 1310720 | tf_op jit(solution)/shard_map/reduce_scatter | solution.py:108
  213.2 4.2 %slice-start = ((f32[1024,2,4,128]{3,2,1,0:T(4,128)}), f32[256,2,4,128]{3,2,1,0:T(4,128)S(1)}, s32[]{:S(2)}) async-start(f32[1024,2,4,128]{3,2,1,0:T(4,128)} %all-gather.5.cloned.1.call-done), calls=%async_computation.3 | async-start | bytes 2097152 | tf_op jit(solution)/shard_map/slice | solution.py:15
Sparse Core Ops, SparseCore 0:
  125.8 87.3 all-gather.4
  236.0 23.6 reduce-scatter.1
where the time goes:
time: 269 us; the launch traced here: 267 us
  waiting for transfers between devices  77.7 us (29%)
  blocking collectives  65.8 us (24%)
  local copies, waits for them, and re-layouts  41.9 us (16%)
  matrix products  36 us (13%)
  other arithmetic  30.5 us (11%)
  between operations  14.3 us (5%)
    all_gather x1, waiting for transfers between devices, merged(): pieces = jax.tree.map(lambda part: lax.all_gather(part, axis), value)  53.9 us
    all_gather x2, blocking collectives, merged(): pieces = jax.tree.map(lambda part: lax.all_gather(part, axis), value)  33.6 us
    dot_general x8, matrix products, attend(): jnp.einsum('rkgt,tkd->rkgd', weights.astype(jnp.bfloat16), value_rows, pr...  28 us
    reduce_scatter x1, waiting for transfers between devices, per_device(): lax.psum_scatter(jnp.dot(attended, output_weight, preferred_element_type=...  23.8 us
    all_gather x1, blocking collectives, per_device(): lax.all_gather(segment_query, 'seq', axis=0, tiled=True)  16.4 us
    all_gather x1, blocking collectives, per_device(): lax.all_gather(segment_memory, 'seq', axis=0, tiled=True)  15.8 us
    dynamic_slice x24, local copies, waits for them, and re-layouts, per_device(): state, ignored = lax.scan(advance, start_state, (cache_tiles, mask_tiles))  11.9 us
    reshape x1, local copies, waits for them, and re-layouts, per_device(): cache_tiles = cache_memory.reshape(tile_count, tile_size, 2, kv_local, HD)  11.7 us
  transfers between devices with their start and end apart: 2, of which 2 were waited for; matrix products, arithmetic and copies ran while one was open for 0% of the time, Pallas kernels for 0%

commit v1 on v0

v1 whole, which is shorter than its diff:
```python
import functools
import math

import jax
import jax.numpy as jnp
from jax import lax
from jax.experimental import pallas as pl
from jax.experimental.pallas import tpu as pltpu
from jax.sharding import PartitionSpec as P

HD = 128
BLOCK = 128
LANES = 128
FLOOR = -1e30
LOW_PEAK = -1e29
SCALE = math.log2(math.e) / math.sqrt(HD)
BF = jnp.bfloat16
F32 = jnp.float32


def split_rows(raw, rows, kv, stage, keys_ref, values_ref, start):
    for g in range(kv):
        cols = pl.ds(g * HD, HD)
        stage[g, pl.ds(0, 2 * rows)] = raw[:, :, g * HD : (g + 1) * HD].reshape(2 * rows, HD).astype(F32)
        keys_ref[pl.ds(start, rows), cols] = stage[g, pl.ds(0, rows, stride=2)].astype(BF)
        values_ref[pl.ds(start, rows), cols] = stage[g, pl.ds(1, rows, stride=2)].astype(BF)


def prepare_body(kv, ctx_blocks, fin_blocks, own_rows, mask_ref, cache_ref, fin_ref, own_ref, keys_ref, values_ref, raw, stage, sems):
    def fetch(i):
        return pltpu.make_async_copy(cache_ref.at[pl.ds(i * BLOCK, BLOCK)], raw.at[i], sems.at[i])

    for i in range(ctx_blocks):
        fetch(i).start()
    own_start = (ctx_blocks + fin_blocks) * BLOCK
    pad = BLOCK - own_rows
    for ref in (keys_ref, values_ref):
        ref[pl.ds(own_start, BLOCK)] = jnp.zeros((BLOCK, kv * HD), BF)
    split_rows(own_ref[...], own_rows, kv, stage.at[0], keys_ref, values_ref, own_start)
    for i in range(fin_blocks):
        split_rows(fin_ref[pl.ds(i * BLOCK, BLOCK)], BLOCK, kv, stage.at[(i + 1) % 2], keys_ref, values_ref, (ctx_blocks + i) * BLOCK)

    @pl.loop(0, ctx_blocks)
    def _(i):
        fetch(i).wait()
        used = mask_ref[0, i]
        for q in range(1, mask_ref.shape[0]):
            used = used | mask_ref[q, i]

        @pl.when(used > 0)
        def _():
            split_rows(raw[i], BLOCK, kv, stage.at[i % 2], keys_ref, values_ref, pl.multiple_of(i * BLOCK, BLOCK))


def prepare(mask, cache, finished, own):
    rows, _, width = cache.shape
    kv = width // HD
    ctx_blocks, fin_blocks = rows // BLOCK, finished.shape[0] // BLOCK
    total = (ctx_blocks + fin_blocks + 1) * BLOCK
    vmem = pl.BlockSpec(memory_space=pltpu.VMEM)
    return pl.pallas_call(
        functools.partial(prepare_body, kv, ctx_blocks, fin_blocks, own.shape[0]),
        in_specs=[pl.BlockSpec(memory_space=pltpu.SMEM), pl.BlockSpec(memory_space=pl.ANY), vmem, vmem],
        out_specs=[vmem, vmem],
        out_shape=[jax.ShapeDtypeStruct((total, width), BF)] * 2,
        scratch_shapes=[
            pltpu.VMEM((ctx_blocks, BLOCK, 2, width), BF),
            pltpu.VMEM((2, kv, 2 * BLOCK, HD), F32),
            pltpu.SemaphoreType.DMA((ctx_blocks,)),
        ],
        cost_estimate=pl.CostEstimate(flops=0, bytes_accessed=12 * 1024 * 1024, transcendentals=0),
        compiler_params=pltpu.CompilerParams(vmem_limit_bytes=24 << 20),
        name="prepare",
    )(mask, cache, finished, own)


def attend_body(geometry, shifts, *refs):
    kv, group, tokens, ctx_blocks, fin_blocks, seq_blocks = geometry
    n = len(shifts)
    meta_ref, mask_ref, keys_ref, values_ref = refs[:4]
    query_refs, message_refs = refs[4 : 4 + n], refs[4 + n : 4 + 2 * n]
    blocks_ref, scores, peaks, totals, sums = refs[4 + 2 * n :]
    rows = group * tokens
    own_block = ctx_blocks + fin_blocks
    is_owner, limit = meta_ref[0], meta_ref[1]
    lane = lax.broadcasted_iota(jnp.int32, (1, 2 * BLOCK), 1)
    stat_lane = lax.broadcasted_iota(jnp.int32, (1, LANES), 1)

    for at, (query_ref, message_ref) in enumerate(zip(query_refs, message_refs, strict=True)):
        query_block = meta_ref[2 + at]

        def gather_block(i, count, query_block=query_block):
            blocks_ref[count] = i
            return count + jnp.where(mask_ref[query_block, i] > 0, 1, 0)

        count = lax.fori_loop(0, ctx_blocks, gather_block, jnp.int32(0))
        for i in range(fin_blocks):
            blocks_ref[count] = ctx_blocks + i
            count = count + is_owner
        blocks_ref[count] = own_block
        blocks_ref[count + 1] = own_block
        full = count
        pairs = (count + 2) // 2

        queries = [
            jnp.concatenate(
                [query_ref[:, (g * group + a) * HD : (g * group + a + 1) * HD] for a in range(group)], axis=0
            )
            for g in range(kv)
        ]

        def block_rows(ref, j, g):
            parts = [
                ref[pl.ds(pl.multiple_of(blocks_ref[2 * j + half] * BLOCK, BLOCK), BLOCK), g * HD : (g + 1) * HD]
                for half in range(2)
            ]
            return jnp.concatenate(parts, axis=0)

        def score(j, masked):
            for g in range(kv):
                s = lax.dot_general(
                    queries[g], block_rows(keys_ref, j, g), (((1,), (1,)), ((), ())), preferred_element_type=F32
                )
                if masked:
                    bound = jnp.where(2 * j < full, BLOCK, limit)
                    bound_next = jnp.where(2 * j + 1 < full, BLOCK, jnp.where(2 * j + 1 == full, limit, 0))
                    edge = jnp.where(lane < BLOCK, bound, BLOCK + bound_next)
                    s = s + jnp.where(lane < edge, 0.0, FLOOR)
                scores[j, g] = s
                peaks[g] = jnp.maximum(peaks[g], jnp.maximum(s[:, :BLOCK], s[:, BLOCK:]))

        peaks[...] = jnp.full(peaks.shape, LOW_PEAK, F32)
        pl.loop(0, pairs - 1)(lambda j: score(j, False))
        score(pairs - 1, True)

        shift = []
        for g in range(kv):
            peak = jnp.max(peaks[g], axis=1, keepdims=True) * SCALE
            shift.append(jnp.broadcast_to(peak.astype(BF).astype(F32), (rows, LANES)))
            peaks[g] = shift[g]
        totals[...] = jnp.zeros(totals.shape, F32)
        sums[...] = jnp.zeros(sums.shape, F32)

        @pl.loop(0, pairs)
        def _(j):
            for g in range(kv):
                s = scores[j, g]
                low = jnp.exp2(s[:, :BLOCK] * SCALE - peaks[g])
                high = jnp.exp2(s[:, BLOCK:] * SCALE - peaks[g])
                totals[g] += low + high
                weights = jnp.concatenate([low.astype(BF), high.astype(BF)], axis=1)
                sums[g] += jnp.dot(weights, block_rows(values_ref, j, g), preferred_element_type=F32)

        stats = jnp.zeros((tokens, LANES), F32)
        for g in range(kv):
            total = jnp.broadcast_to(jnp.sum(totals[g], axis=1, keepdims=True), (rows, LANES))
            coarse = total.astype(BF).astype(F32)
            for a in range(group):
                h = g * group + a
                part = slice(a * tokens, (a + 1) * tokens)
                message_ref[:, h * HD : (h + 1) * HD] = sums[g, part].astype(BF)
                stats = jnp.where(stat_lane == 3 * h, peaks[g, part], stats)
                stats = jnp.where(stat_lane == 3 * h + 1, coarse[part], stats)
                stats = jnp.where(stat_lane == 3 * h + 2, total[part] - coarse[part], stats)
        message_ref[:, kv * group * HD :] = stats.astype(BF)


def attend(meta, mask, keys, values, queries, kv, fin_blocks):
    tokens, width = queries[0].shape
    n = len(queries)
    group = width // (kv * HD)
    ctx_blocks = mask.shape[1]
    slots = ctx_blocks + fin_blocks + 2
    rows = group * tokens
    vmem, smem = pl.BlockSpec(memory_space=pltpu.VMEM), pl.BlockSpec(memory_space=pltpu.SMEM)
    geometry = (kv, group, tokens, ctx_blocks, fin_blocks, mask.shape[0])
    pair_count = (slots + 1) // 2
    return pl.pallas_call(
        functools.partial(attend_body, geometry, tuple(range(n))),
        in_specs=[smem, smem] + [vmem] * (2 + n),
        out_specs=[vmem] * n,
        out_shape=[jax.ShapeDtypeStruct((tokens, width + LANES), BF)] * n,
        scratch_shapes=[
            pltpu.SMEM((slots + 1,), jnp.int32),
            pltpu.VMEM((pair_count, kv, rows, 2 * BLOCK), F32),
            pltpu.VMEM((kv, rows, LANES), F32),
            pltpu.VMEM((kv, rows, LANES), F32),
            pltpu.VMEM((kv, rows, HD), F32),
        ],
        cost_estimate=pl.CostEstimate(
            flops=4 * n * rows * kv * HD * BLOCK * slots // 2,
            bytes_accessed=2 * keys.size * 2,
            transcendentals=n * rows * kv * BLOCK * slots // 2,
        ),
        compiler_params=pltpu.CompilerParams(vmem_limit_bytes=28 << 20),
        name="attend",
    )(meta, mask, keys, values, *queries)


def merge_body(heads, *refs):
    *parts, out_ref = refs
    loaded = [part[:, heads * HD :].astype(F32) for part in parts]
    for h in range(heads):
        peaks = [s[:, 3 * h : 3 * h + 1] for s in loaded]
        totals = [s[:, 3 * h + 1 : 3 * h + 2] + s[:, 3 * h + 2 : 3 * h + 3] for s in loaded]
        top = functools.reduce(jnp.maximum, peaks)
        factors = [jnp.exp2(p - top) for p in peaks]
        inverse = 1.0 / sum(f * t for f, t in zip(factors, totals, strict=True))
        cols = slice(h * HD, (h + 1) * HD)
        out_ref[:, cols] = sum(
            part[:, cols].astype(F32) * (f * inverse) for part, f in zip(parts, factors, strict=True)
        ).astype(BF)


def merge(parts, heads):
    tokens = parts[0].shape[0]
    return pl.pallas_call(
        functools.partial(merge_body, heads),
        in_specs=[pl.BlockSpec(memory_space=pltpu.VMEM)] * len(parts),
        out_specs=pl.BlockSpec(memory_space=pltpu.VMEM),
        out_shape=jax.ShapeDtypeStruct((tokens, heads * HD), BF),
        compiler_params=pltpu.CompilerParams(vmem_limit_bytes=16 << 20),
        name="merge",
    )(*parts)


def per_device(
    n_seq,
    n_head,
    segment_query,
    segment_memory,
    finished_memory,
    cache_memory,
    block_mask,
    owner_index,
    valid_count,
    output_weight,
):
    here = lax.axis_index("seq")
    own_tokens, width = segment_query.shape
    heads = width // HD
    kv = segment_memory.shape[2] // HD
    fin_blocks = finished_memory.shape[0] // BLOCK
    direct = n_seq == 4 and n_head == 4

    is_owner = (here == owner_index[0]).astype(jnp.int32)
    limit = jnp.clip(valid_count[0] - here * own_tokens, 0, own_tokens)

    if direct:
        def toward(k):
            return [(i, i ^ k) for i in range(n_seq)]

        queries = [segment_query] + [lax.ppermute(segment_query, "seq", toward(k)) for k in range(1, n_seq)]
        query_blocks = [((here ^ k) * own_tokens) // BLOCK for k in range(n_seq)]
    else:
        gathered = lax.all_gather(segment_query, "seq", axis=0, tiled=True)
        query_blocks = list(range(gathered.shape[0] // BLOCK))
        queries = [gathered[i * BLOCK : (i + 1) * BLOCK] for i in query_blocks]

    meta = jnp.stack([jnp.asarray(x, jnp.int32) for x in [is_owner, limit] + query_blocks])
    keys, values = prepare(block_mask, cache_memory, finished_memory, segment_memory)
    messages = attend(meta, block_mask, keys, values, queries, kv, fin_blocks)

    if direct:
        parts = [messages[0]] + [lax.ppermute(messages[k], "seq", toward(k)) for k in range(1, n_seq)]
        attended = merge(parts, heads)
        shards = [attended] + [lax.ppermute(attended, "seq", toward(k)) for k in range(1, n_seq)]
        stacked = jnp.stack(shards)
        projected = jnp.einsum("ktf,fd->ktd", stacked, output_weight, preferred_element_type=F32)
        head_at = lax.axis_index("head")
        tile = projected.shape[1:]
        core, side = head_at % 2, head_at // 2

        def shard_of(token_shard):
            return lax.dynamic_index_in_dim(projected, token_shard ^ here, 0, keepdims=False)

        mine_core = [shard_of(core), shard_of(2 + core)]
        other_core = jnp.stack([shard_of(1 - core), shard_of(3 - core)]).astype(BF)
        received = lax.ppermute(other_core, "head", [(i, i ^ 1) for i in range(n_head)])
        joined = jnp.stack(mine_core) + received.astype(F32)
        mine = lax.dynamic_index_in_dim(joined, side, 0, keepdims=False)
        other = lax.dynamic_index_in_dim(joined, 1 - side, 0, keepdims=False).astype(BF)
        return mine + lax.ppermute(other, "head", [(i, i ^ 2) for i in range(n_head)]).astype(F32)

    sent = jnp.concatenate(messages, axis=0)
    got = lax.all_to_all(sent, "seq", 0, 0, tiled=True).reshape(n_seq, own_tokens, -1)
    attended = merge([got[i] for i in range(n_seq)], heads)
    attended = lax.all_gather(attended, "seq", axis=0, tiled=True)
    return lax.psum_scatter(
        jnp.dot(attended, output_weight, preferred_element_type=F32), "head", scatter_dimension=0, tiled=True
    )


def solution(mesh):
    return jax.shard_map(
        functools.partial(per_device, mesh.shape["seq"], mesh.shape["head"]),
        mesh=mesh,
        in_specs=(
            P(("groups", "seq"), "head"),
            P(("groups", "seq"), None, "head"),
            P(("groups", "seq"), None, "head"),
            P(("groups", "seq"), None, "head"),
            P("groups", "seq"),
            P("groups"),
            P("groups"),
            P("head", "seq"),
        ),
        out_specs=P(("groups", "head"), "seq"),
        check_vma=False,
    )
```

time: 269 us -> 83.2 us (0.31)
  blocking collectives: 65.8 us -> 0 us
  waiting for transfers between devices: 77.7 us -> 24.2 us
  matrix products: 36 us -> 1.61 us
  local copies, waits for them, and re-layouts: 41.9 us -> 11.6 us
  other arithmetic: 30.5 us -> 1.52 us
  Pallas kernels: 0 us -> 22.8 us
  starting transfers between devices: 0.04 us -> 19.3 us
  between operations: 14.3 us -> 1.45 us
    all_gather x4 -> x0, blocking collectives: 65.8 us -> none  [the longest x2 33.6 us: merged(): pieces = jax.tree.map(lambda part: lax.all_gather(part, axis), value)]
    all_gather x1 -> x0, waiting for transfers between devices: 53.9 us -> none  [merged(): pieces = jax.tree.map(lambda part: lax.all_gather(part, axis), value)]
    dot_general x17 -> x1, matrix products: 36 us -> 1.61 us  [per_device(): jnp.einsum('ktf,fd->ktd', stacked, output_weight, preferred_element_type=...]
    ppermute x0 -> x11, waiting for transfers between devices: none -> 24.2 us  [the longest x3 10.7 us: per_device(): lax.ppermute(messages[k], 'seq', toward(k))]
    reduce_scatter x1 -> x0, waiting for transfers between devices: 23.8 us -> none  [per_device(): lax.psum_scatter(jnp.dot(attended, output_weight, preferred_element_type=...]
    pallas_call x0 -> x3, Pallas kernels: none -> 22.8 us  [the longest x1 12.9 us: attend(): pl.pallas_call(functools.partial(attend_body, geometry, tuple(range(n))),...]
    add x14 -> x2, other arithmetic: 20.9 us -> 0.79 us  [the longest x1 0.73 us: per_device(): mine + lax.ppermute(other, 'head', [(i, i ^ 2) for i in range(n_head)]).a...]
    ppermute x0 -> x11, starting transfers between devices: none -> 19.3 us  [the longest x3 7.5 us: per_device(): lax.ppermute(messages[k], 'seq', toward(k))]
  transfers between devices with their start and end apart: 2 -> 11, of which waited for: 2 -> 6; matrix products, arithmetic and copies ran while one was open for 0% -> 0% of each run, Pallas kernels for 0% -> 11%
where the time goes in v1:
time: 83.2 us; the launch traced here: 82.4 us
  waiting for transfers between devices  24.2 us (29%)
  Pallas kernels  22.8 us (27%)
  starting transfers between devices  19.3 us (23%)
  local copies, waits for them, and re-layouts  11.6 us (14%)
  matrix products  1.61 us (2%)
  other arithmetic  1.52 us (2%)
  between operations  1.45 us (2%)
    pallas_call x1, Pallas kernels, attend(): pl.pallas_call(functools.partial(attend_body, geometry, tuple(range(n))),...  12.9 us
    unnamed x24, local copies, waits for them, and re-layouts  11.4 us
    ppermute x3, waiting for transfers between devices, per_device(): lax.ppermute(messages[k], 'seq', toward(k))  10.7 us
    pallas_call x1, Pallas kernels, prepare(): pl.pallas_call(functools.partial(prepare_body, kv, ctx_blocks, fin_blocks...  9.37 us
    ppermute x3, waiting for transfers between devices, per_device(): lax.ppermute(attended, 'seq', toward(k))  7.83 us
    ppermute x3, starting transfers between devices, per_device(): lax.ppermute(messages[k], 'seq', toward(k))  7.5 us
    ppermute x3, starting transfers between devices, per_device(): lax.ppermute(segment_query, 'seq', toward(k))  5.62 us
    ppermute x3, starting transfers between devices, per_device(): lax.ppermute(attended, 'seq', toward(k))  4.57 us
  transfers between devices with their start and end apart: 11, of which 6 were waited for; matrix products, arithmetic and copies ran while one was open for 0% of the time, Pallas kernels for 11%

profile of v1, /device:TPU:0, one launch (start us, length us, event | category | flops | bytes accessed | tf_op | source)
XLA Modules:
  0.0 82.4 jit_solution(6186869205703139632)
XLA Ops:
  0.0 3.0 %collective-permute-start = (bf16[64,1024]{1,0:T(8,128)(2,1)}, bf16[64,1024]{1,0:T(8,128)(2,1)S(1)}, u32[]{:S(2)}, u32[]{:S(2)}) collective-permute-start(bf16[64,1024]{1,0:T(8,128)(2,1)} %refs_4_.1), channel_id=1, source_target_pairs={{0,4},{4,0},{8,12},{12,8},{1,5},{5,1},{9,13},{13,9},{2,6},{6,2},{1... | collective-permute-start | bytes 393224 | tf_op jit(solution)/shard_map/ppermute | solution.py:253
  3.0 2.6 %collective-permute-start.1 = (bf16[64,1024]{1,0:T(8,128)(2,1)}, bf16[64,1024]{1,0:T(8,128)(2,1)S(1)}, u32[]{:S(2)}, u32[]{:S(2)}) collective-permute-start(bf16[64,1024]{1,0:T(8,128)(2,1)} %refs_4_.1), channel_id=1, source_target_pairs={{0,8},{4,12},{8,0},{12,4},{1,9},{5,13},{9,1},{13,5},{2,10},{6,14},... | collective-permute-start | bytes 393224 | tf_op jit(solution)/shard_map/ppermute | solution.py:253
  7.0 2.2 %copy-done.1 = bf16[4096,2,256]{2,1,0:T(2,128)(2,1)S(1)} copy-done((bf16[4096,2,256]{2,1,0:T(2,128)(2,1)S(1)}, bf16[4096,2,256]{2,1,0:T(2,128)(2,1)}, u32[]{:S(2)}) %copy-start.1) | copy-done | bytes 4194328
  9.1 0.9 %copy-done.2 = bf16[256,2,256]{2,1,0:T(2,128)(2,1)S(1)} copy-done((bf16[256,2,256]{2,1,0:T(2,128)(2,1)S(1)}, bf16[256,2,256]{2,1,0:T(2,128)(2,1)}, u32[]{:S(2)}) %copy-start.2) | copy-done | bytes 262168
  10.1 0.8 %copy-done.3 = bf16[64,2,256]{2,1,0:T(2,128)(2,1)S(1)} copy-done((bf16[64,2,256]{2,1,0:T(2,128)(2,1)S(1)}, bf16[64,2,256]{2,1,0:T(2,128)(2,1)}, u32[]{:S(2)}) %copy-start.3) | copy-done | bytes 65560
  11.6 9.4 %prepare.1 = (bf16[4480,256]{1,0:T(8,128)(2,1)S(1)}, bf16[4480,256]{1,0:T(8,128)(2,1)S(1)}) custom-call(s32[2,32]{1,0:T(2,128)S(1)} %copy-done.4, bf16[4096,2,256]{2,1,0:T(2,128)(2,1)S(1)} %copy-done.1, bf16[256,2,256]{2,1,0:T(2,128)(2,1)S(1)} %copy-done.2, bf16[64,2,256]{2,1,0:T(2,128)(2,1)S(1)} %copy-done.3), custom_call_target="tpu_custom_call" | custom-call | bytes 12582912 | tf_op jit(solution)/shard_map/prepare/pallas_call | solution.py:61
  21.0 1.4 %copy-done.6 = bf16[4480,256]{1,0:T(8,128)(2,1)} copy-done((bf16[4480,256]{1,0:T(8,128)(2,1)}, bf16[4480,256]{1,0:T(8,128)(2,1)S(1)}, u32[]{:S(2)}) %copy-start.6) | copy-done | bytes 2293784
  22.4 1.4 %copy-done.8 = bf16[4480,256]{1,0:T(8,128)(2,1)} copy-done((bf16[4480,256]{1,0:T(8,128)(2,1)}, bf16[4480,256]{1,0:T(8,128)(2,1)S(1)}, u32[]{:S(2)}) %copy-start.8) | copy-done | bytes 2293784
  23.9 1.6 %copy-done.7 = bf16[4480,256]{1,0:T(8,128)(2,1)S(1)} copy-done((bf16[4480,256]{1,0:T(8,128)(2,1)S(1)}, bf16[4480,256]{1,0:T(8,128)(2,1)}, u32[]{:S(2)}) %copy-start.7) | copy-done | bytes 2293784
  25.6 1.6 %copy-done.9 = bf16[4480,256]{1,0:T(8,128)(2,1)S(1)} copy-done((bf16[4480,256]{1,0:T(8,128)(2,1)S(1)}, bf16[4480,256]{1,0:T(8,128)(2,1)}, u32[]{:S(2)}) %copy-start.9) | copy-done | bytes 2293784
  27.2 12.9 %attend.1 = (bf16[64,1152]{1,0:T(8,128)(2,1)S(1)}, bf16[64,1152]{1,0:T(8,128)(2,1)S(1)}, bf16[64,1152]{1,0:T(8,128)(2,1)S(1)}, bf16[64,1152]{1,0:T(8,128)(2,1)S(1)}) custom-call(s32[6]{0:T(128)S(1)} %stack.57.refs_0_, s32[2,32]{1,0:T(2,128)S(1)} %copy-done.5, bf16[4480,256]{1,0:T(8,128)(2,1)S(1)} %copy-done.7, bf16[4480,256]{1,0:T(8,128)(2,1)S(1)} %copy-done.9, ...), custom_call_target="tpu_custom_call" | custom-call | flops 2415919104 | bytes 4587520 | tf_op jit(solution)/shard_map/attend/pallas_call | solution.py:178
  40.1 4.6 %collective-permute-start.3 = (bf16[64,1152]{1,0:T(8,128)(2,1)S(1)}, bf16[64,1152]{1,0:T(8,128)(2,1)S(1)}, u32[]{:S(2)}, u32[]{:S(2)}) collective-permute-start(bf16[64,1152]{1,0:T(8,128)(2,1)S(1)} %get-tuple-element.14), channel_id=1, source_target_pairs={{0,4},{4,0},{8,12},{12,8},{1,5},{5,1},{9,13},{13,9},{2,6},{6,2},{1... | collective-permute-start | bytes 442376 | tf_op jit(solution)/shard_map/ppermute | solution.py:265
  44.8 2.9 %collective-permute-start.4 = (bf16[64,1152]{1,0:T(8,128)(2,1)S(1)}, bf16[64,1152]{1,0:T(8,128)(2,1)S(1)}, u32[]{:S(2)}, u32[]{:S(2)}) collective-permute-start(bf16[64,1152]{1,0:T(8,128)(2,1)S(1)} %get-tuple-element.15), channel_id=1, source_target_pairs={{0,8},{4,12},{8,0},{12,4},{1,9},{5,13},{9,1},{13,5},{2,10},{6,14},... | collective-permute-start | bytes 442376 | tf_op jit(solution)/shard_map/ppermute | solution.py:265
  47.6 1.9 %collective-permute-done.3.refs_1_ = bf16[64,1152]{1,0:T(8,128)(2,1)S(1)} collective-permute-done((bf16[64,1152]{1,0:T(8,128)(2,1)S(1)}, bf16[64,1152]{1,0:T(8,128)(2,1)S(1)}, u32[]{:S(2)}, u32[]{:S(2)}) %collective-permute-start.3) | collective-permute-done | bytes 147488 | tf_op jit(solution)/shard_map/ppermute | solution.py:265
  49.5 8.8 %collective-permute-done.4.refs_2_ = bf16[64,1152]{1,0:T(8,128)(2,1)S(1)} collective-permute-done((bf16[64,1152]{1,0:T(8,128)(2,1)S(1)}, bf16[64,1152]{1,0:T(8,128)(2,1)S(1)}, u32[]{:S(2)}, u32[]{:S(2)}) %collective-permute-start.4) | collective-permute-done | bytes 147488 | tf_op jit(solution)/shard_map/ppermute | solution.py:265
  58.8 3.2 %collective-permute-start.7 = (bf16[64,1024]{1,0:T(8,128)(2,1)S(1)}, bf16[64,1024]{1,0:T(8,128)(2,1)S(1)}, u32[]{:S(2)}, u32[]{:S(2)}) collective-permute-start(bf16[64,1024]{1,0:T(8,128)(2,1)S(1)} %merge.1), channel_id=1, source_target_pairs={{0,8},{4,12},{8,0},{12,4},{1,9},{5,13},{9,1},{13,5},{2,10},{6,14},... | collective-permute-start | bytes 393224 | tf_op jit(solution)/shard_map/ppermute | solution.py:267
  62.0 1.4 %collective-permute-start.8 = (bf16[64,1024]{1,0:T(8,128)(2,1)S(1)}, bf16[64,1024]{1,0:T(8,128)(2,1)S(1)}, u32[]{:S(2)}, u32[]{:S(2)}) collective-permute-start(bf16[64,1024]{1,0:T(8,128)(2,1)S(1)} %merge.1), channel_id=1, source_target_pairs={{0,12},{4,8},{8,4},{12,0},{1,13},{5,9},{9,5},{13,1},{2,14},{6,10},... | collective-permute-start | bytes 393224 | tf_op jit(solution)/shard_map/ppermute | solution.py:267
  63.4 7.4 %collective-permute-done.7 = bf16[64,1024]{1,0:T(8,128)(2,1)S(1)} collective-permute-done((bf16[64,1024]{1,0:T(8,128)(2,1)S(1)}, bf16[64,1024]{1,0:T(8,128)(2,1)S(1)}, u32[]{:S(2)}, u32[]{:S(2)}) %collective-permute-start.7) | collective-permute-done | bytes 131104 | tf_op jit(solution)/shard_map/ppermute | solution.py:267
  71.9 1.6 %fusion = f32[4,64,1024]{2,1,0:T(8,128)S(1)} fusion(bf16[1024,1024]{1,0:T(8,128)(2,1)S(1)} %copy-done, bf16[1,64,1024]{2,1,0:T(8,128)(2,1)S(1)} %bitcast.23, bf16[1,64,1024]{2,1,0:T(8,128)(2,1)S(1)} %bitcast.22, bf16[1,64,1024]{2,1,0:T(8,128)(2,1)} %bitcast.24, bf16[1,64,1024]{2,1,0:T(8,128)(2,1)S(1)} %bitcast.21), kind=kOutput, calls=%fused_computation | convolution fusion | flops 537657344 | bytes 3670016 | tf_op jit(solution)/shard_map/ktf,fd->ktd/dot_general | solution.py:269
  73.5 0.7 pad_maximum_fusion
  74.3 1.7 %collective-permute-done.9 = bf16[2,64,1024]{2,1,0:T(8,128)(2,1)S(1)} collective-permute-done((bf16[2,64,1024]{2,1,0:T(8,128)(2,1)}, bf16[2,64,1024]{2,1,0:T(8,128)(2,1)S(1)}, u32[]{:S(2)}, u32[]{:S(2)}) %collective-permute-start.9) | collective-permute-done | bytes 262176 | tf_op jit(solution)/shard_map/ppermute | solution.py:279
  76.1 1.6 %collective-permute-start.10 = (bf16[64,1024]{1,0:T(8,128)(2,1)S(1)}, bf16[64,1024]{1,0:T(8,128)(2,1)S(1)}, u32[]{:S(2)}, u32[]{:S(2)}) collective-permute-start(bf16[64,1024]{1,0:T(8,128)(2,1)S(1)} %fusion.9), channel_id=1, source_target_pairs={{0,2},{1,3},{2,0},{3,1},{4,6},{5,7},{6,4},{7,5},{8,10},{9,11},{10,... | collective-permute-start | bytes 393224 | tf_op jit(solution)/shard_map/ppermute | solution.py:283
  77.7 4.0 %collective-permute-done.10 = bf16[64,1024]{1,0:T(8,128)(2,1)S(1)} collective-permute-done((bf16[64,1024]{1,0:T(8,128)(2,1)S(1)}, bf16[64,1024]{1,0:T(8,128)(2,1)S(1)}, u32[]{:S(2)}, u32[]{:S(2)}) %collective-permute-start.10) | collective-permute-done | bytes 131104 | tf_op jit(solution)/shard_map/ppermute | solution.py:283
  81.7 0.7 bitcast_add_fusion
  (33 shorter events, 2.6 us)
Async XLA Ops:
  0.0 71.9 %copy-start = (bf16[1024,1024]{1,0:T(8,128)(2,1)S(1)}, bf16[1024,1024]{1,0:T(8,128)(2,1)}, u32[]{:S(2)}) copy-start(bf16[1024,1024]{1,0:T(8,128)(2,1)} %param.15) | copy-start | bytes 6291460
  0.0 23.9 %collective-permute-start = (bf16[64,1024]{1,0:T(8,128)(2,1)}, bf16[64,1024]{1,0:T(8,128)(2,1)S(1)}, u32[]{:S(2)}, u32[]{:S(2)}) collective-permute-start(bf16[64,1024]{1,0:T(8,128)(2,1)} %refs_4_.1), channel_id=1, source_target_pairs={{0,4},{4,0},{8,12},{12,8},{1,5},{5,1},{9,13},{13,9},{2,6},{6,2},{1... | collective-permute-start | bytes 393224 | tf_op jit(solution)/shard_map/ppermute | solution.py:253
  3.0 20.9 %collective-permute-start.1 = (bf16[64,1024]{1,0:T(8,128)(2,1)}, bf16[64,1024]{1,0:T(8,128)(2,1)S(1)}, u32[]{:S(2)}, u32[]{:S(2)}) collective-permute-start(bf16[64,1024]{1,0:T(8,128)(2,1)} %refs_4_.1), channel_id=1, source_target_pairs={{0,8},{4,12},{8,0},{12,4},{1,9},{5,13},{9,1},{13,5},{2,10},{6,14},... | collective-permute-start | bytes 393224 | tf_op jit(solution)/shard_map/ppermute | solution.py:253
  5.6 18.3 %collective-permute-start.2 = (bf16[64,1024]{1,0:T(8,128)(2,1)}, bf16[64,1024]{1,0:T(8,128)(2,1)S(1)}, u32[]{:S(2)}, u32[]{:S(2)}) collective-permute-start(bf16[64,1024]{1,0:T(8,128)(2,1)} %refs_4_.1), channel_id=1, source_target_pairs={{0,12},{4,8},{8,4},{12,0},{1,13},{5,9},{9,5},{13,1},{2,14},{6,10},... | collective-permute-start | bytes 393224 | tf_op jit(solution)/shard_map/ppermute | solution.py:253
  6.9 2.2 %copy-start.1 = (bf16[4096,2,256]{2,1,0:T(2,128)(2,1)S(1)}, bf16[4096,2,256]{2,1,0:T(2,128)(2,1)}, u32[]{:S(2)}) copy-start(bf16[4096,2,256]{2,1,0:T(2,128)(2,1)} %cache_ref.1) | copy-start | bytes 12582916
  9.1 0.9 %copy-start.2 = (bf16[256,2,256]{2,1,0:T(2,128)(2,1)S(1)}, bf16[256,2,256]{2,1,0:T(2,128)(2,1)}, u32[]{:S(2)}) copy-start(bf16[256,2,256]{2,1,0:T(2,128)(2,1)} %fin_ref.1) | copy-start | bytes 786436
  10.1 0.8 %copy-start.3 = (bf16[64,2,256]{2,1,0:T(2,128)(2,1)S(1)}, bf16[64,2,256]{2,1,0:T(2,128)(2,1)}, u32[]{:S(2)}) copy-start(bf16[64,2,256]{2,1,0:T(2,128)(2,1)} %own_ref.1) | copy-start | bytes 196612
  10.9 0.7 copy-start.4
  11.6 12.3 %copy-start.5 = (s32[2,32]{1,0:T(2,128)S(1)}, s32[2,32]{1,0:T(2,128)}, u32[]{:S(2)}) copy-start(s32[2,32]{1,0:T(2,128)} %refs_1_.1) | copy-start | bytes 772
  11.6 12.3 %copy-start.10 = (bf16[64,1024]{1,0:T(8,128)(2,1)S(1)}, bf16[64,1024]{1,0:T(8,128)(2,1)}, u32[]{:S(2)}) copy-start(bf16[64,1024]{1,0:T(8,128)(2,1)} %refs_4_.1) | copy-start | bytes 393220
  21.0 1.4 %copy-start.6 = (bf16[4480,256]{1,0:T(8,128)(2,1)}, bf16[4480,256]{1,0:T(8,128)(2,1)S(1)}, u32[]{:S(2)}) copy-start(bf16[4480,256]{1,0:T(8,128)(2,1)S(1)} %get-tuple-element.11.refs_2_) | copy-start | bytes 6881284
  22.4 1.4 %copy-start.8 = (bf16[4480,256]{1,0:T(8,128)(2,1)}, bf16[4480,256]{1,0:T(8,128)(2,1)S(1)}, u32[]{:S(2)}) copy-start(bf16[4480,256]{1,0:T(8,128)(2,1)S(1)} %get-tuple-element.12.refs_3_) | copy-start | bytes 6881284
  23.9 1.6 %copy-start.7 = (bf16[4480,256]{1,0:T(8,128)(2,1)S(1)}, bf16[4480,256]{1,0:T(8,128)(2,1)}, u32[]{:S(2)}) copy-start(bf16[4480,256]{1,0:T(8,128)(2,1)} %copy-done.6) | copy-start | bytes 6881284
  25.6 1.6 %copy-start.9 = (bf16[4480,256]{1,0:T(8,128)(2,1)S(1)}, bf16[4480,256]{1,0:T(8,128)(2,1)}, u32[]{:S(2)}) copy-start(bf16[4480,256]{1,0:T(8,128)(2,1)} %copy-done.8) | copy-start | bytes 6881284
  40.1 9.4 %collective-permute-start.3 = (bf16[64,1152]{1,0:T(8,128)(2,1)S(1)}, bf16[64,1152]{1,0:T(8,128)(2,1)S(1)}, u32[]{:S(2)}, u32[]{:S(2)}) collective-permute-start(bf16[64,1152]{1,0:T(8,128)(2,1)S(1)} %get-tuple-element.14), channel_id=1, source_target_pairs={{0,4},{4,0},{8,12},{12,8},{1,5},{5,1},{9,13},{13,9},{2,6},{6,2},{1... | collective-permute-start | bytes 442376 | tf_op jit(solution)/shard_map/ppermute | solution.py:265
  44.8 13.5 %collective-permute-start.4 = (bf16[64,1152]{1,0:T(8,128)(2,1)S(1)}, bf16[64,1152]{1,0:T(8,128)(2,1)S(1)}, u32[]{:S(2)}, u32[]{:S(2)}) collective-permute-start(bf16[64,1152]{1,0:T(8,128)(2,1)S(1)} %get-tuple-element.15), channel_id=1, source_target_pairs={{0,8},{4,12},{8,0},{12,4},{1,9},{5,13},{9,1},{13,5},{2,10},{6,14},... | collective-permute-start | bytes 442376 | tf_op jit(solution)/shard_map/ppermute | solution.py:265
  47.6 10.7 %collective-permute-start.5 = (bf16[64,1152]{1,0:T(8,128)(2,1)S(1)}, bf16[64,1152]{1,0:T(8,128)(2,1)S(1)}, u32[]{:S(2)}, u32[]{:S(2)}) collective-permute-start(bf16[64,1152]{1,0:T(8,128)(2,1)S(1)} %get-tuple-element.16), channel_id=1, source_target_pairs={{0,12},{4,8},{8,4},{12,0},{1,13},{5,9},{9,5},{13,1},{2,14},{6,10},... | collective-permute-start | bytes 442376 | tf_op jit(solution)/shard_map/ppermute | solution.py:265
  58.8 12.0 %collective-permute-start.7 = (bf16[64,1024]{1,0:T(8,128)(2,1)S(1)}, bf16[64,1024]{1,0:T(8,128)(2,1)S(1)}, u32[]{:S(2)}, u32[]{:S(2)}) collective-permute-start(bf16[64,1024]{1,0:T(8,128)(2,1)S(1)} %merge.1), channel_id=1, source_target_pairs={{0,8},{4,12},{8,0},{12,4},{1,9},{5,13},{9,1},{13,5},{2,10},{6,14},... | collective-permute-start | bytes 393224 | tf_op jit(solution)/shard_map/ppermute | solution.py:267
  62.0 8.8 %collective-permute-start.8 = (bf16[64,1024]{1,0:T(8,128)(2,1)S(1)}, bf16[64,1024]{1,0:T(8,128)(2,1)S(1)}, u32[]{:S(2)}, u32[]{:S(2)}) collective-permute-start(bf16[64,1024]{1,0:T(8,128)(2,1)S(1)} %merge.1), channel_id=1, source_target_pairs={{0,12},{4,8},{8,4},{12,0},{1,13},{5,9},{9,5},{13,1},{2,14},{6,10},... | collective-permute-start | bytes 393224 | tf_op jit(solution)/shard_map/ppermute | solution.py:267
  63.4 7.8 %collective-permute-start.6 = (bf16[64,1024]{1,0:T(8,128)(2,1)S(1)}, bf16[64,1024]{1,0:T(8,128)(2,1)S(1)}, u32[]{:S(2)}, u32[]{:S(2)}) collective-permute-start(bf16[64,1024]{1,0:T(8,128)(2,1)S(1)} %merge.1), channel_id=1, source_target_pairs={{0,4},{4,0},{8,12},{12,8},{1,5},{5,1},{9,13},{13,9},{2,6},{6,2},{1... | collective-permute-start | bytes 393224 | tf_op jit(solution)/shard_map/ppermute | solution.py:267
  71.2 0.7 copy-start.11
  74.3 1.7 %collective-permute-start.9 = (bf16[2,64,1024]{2,1,0:T(8,128)(2,1)}, bf16[2,64,1024]{2,1,0:T(8,128)(2,1)S(1)}, u32[]{:S(2)}, u32[]{:S(2)}) collective-permute-start(bf16[2,64,1024]{2,1,0:T(8,128)(2,1)} %pad_maximum_fusion), channel_id=1, source_target_pairs={{0,1},{1,0},{2,3},{3,2},{4,5},{5,4},{6,7},{7,6},{8,9},{9,8},{10,11... | collective-permute-start | bytes 786440 | tf_op jit(solution)/shard_map/ppermute | solution.py:279
  76.1 5.6 %collective-permute-start.10 = (bf16[64,1024]{1,0:T(8,128)(2,1)S(1)}, bf16[64,1024]{1,0:T(8,128)(2,1)S(1)}, u32[]{:S(2)}, u32[]{:S(2)}) collective-permute-start(bf16[64,1024]{1,0:T(8,128)(2,1)S(1)} %fusion.9), channel_id=1, source_target_pairs={{0,2},{1,3},{2,0},{3,1},{4,6},{5,7},{6,4},{7,5},{8,10},{9,11},{10,... | collective-permute-start | bytes 393224 | tf_op jit(solution)/shard_map/ppermute | solution.py:283

commit v2 on v1

v2 whole, which is shorter than its diff:
```python
import functools
import math

import jax
import jax.numpy as jnp
from jax import lax
from jax.experimental import pallas as pl
from jax.experimental.pallas import tpu as pltpu
from jax.sharding import PartitionSpec as P

HD = 128
BLOCK = 128
LANES = 128
FLOOR = -1e30
LOW_PEAK = -1e29
SCALE = math.log2(math.e) / math.sqrt(HD)
BF = jnp.bfloat16
F32 = jnp.float32


VMEM_LIMIT = 30 << 20
UNROLL = 4


def params():
    return pltpu.CompilerParams(vmem_limit_bytes=VMEM_LIMIT)


def vmem_spec():
    return pl.BlockSpec(memory_space=pltpu.VMEM)


def smem_spec():
    return pl.BlockSpec(memory_space=pltpu.SMEM)


def prepare_body(ctx_blocks, fin_blocks, own_rows, mask_ref, cache_ref, fin_ref, own_ref, keys_ref, values_ref, used_ref):
    width = keys_ref.shape[1]
    row = lax.broadcasted_iota(jnp.int32, (2 * BLOCK, 2 * BLOCK), 0)
    col = lax.broadcasted_iota(jnp.int32, (2 * BLOCK, 2 * BLOCK), 1)
    source = jnp.where(row < BLOCK, 2 * row, 2 * row - 2 * BLOCK + 1)
    pick = jnp.where(col == source, 1.0, 0.0).astype(BF)

    def take_apart(pairs, start):
        parts = jnp.dot(pick, pairs.reshape(2 * BLOCK, width), preferred_element_type=F32).astype(BF)
        keys_ref[pl.ds(start, BLOCK)] = parts[:BLOCK]
        values_ref[pl.ds(start, BLOCK)] = parts[BLOCK:]

    def note(i, count):
        used_ref[count] = i
        used = mask_ref[0, i]
        for q in range(1, mask_ref.shape[0]):
            used = used | mask_ref[q, i]
        return count + jnp.where(used > 0, 1, 0)

    count = lax.fori_loop(0, ctx_blocks, note, jnp.int32(0))
    for i in range(UNROLL):
        used_ref[count + i] = ctx_blocks - 1

    @pl.loop(0, (count + UNROLL - 1) // UNROLL)
    def _(j):
        for i in range(UNROLL):
            start = pl.multiple_of(used_ref[j * UNROLL + i] * BLOCK, BLOCK)
            take_apart(cache_ref[pl.ds(start, BLOCK)], start)

    for i in range(fin_blocks):
        take_apart(fin_ref[pl.ds(i * BLOCK, BLOCK)], (ctx_blocks + i) * BLOCK)
    own = jnp.concatenate([own_ref[...], jnp.zeros((BLOCK - own_rows, 2, width), BF)], axis=0)
    take_apart(own, (ctx_blocks + fin_blocks) * BLOCK)


def prepare(mask, cache, finished, own):
    rows, _, width = cache.shape
    ctx_blocks, fin_blocks = rows // BLOCK, finished.shape[0] // BLOCK
    total = (ctx_blocks + fin_blocks + 1) * BLOCK
    return pl.pallas_call(
        functools.partial(prepare_body, ctx_blocks, fin_blocks, own.shape[0]),
        in_specs=[smem_spec(), vmem_spec(), vmem_spec(), vmem_spec()],
        out_specs=[vmem_spec(), vmem_spec()],
        out_shape=[jax.ShapeDtypeStruct((total, width), BF)] * 2,
        scratch_shapes=[pltpu.SMEM((ctx_blocks + UNROLL,), jnp.int32)],
        cost_estimate=pl.CostEstimate(flops=0, bytes_accessed=12 * 1024 * 1024, transcendentals=0),
        compiler_params=params(),
        name="prepare",
    )(mask, cache, finished, own)


def attend_body(geometry, *refs):
    kv, group, tokens, ctx_blocks, fin_blocks, n = geometry
    meta_ref, mask_ref, keys_ref, values_ref = refs[:4]
    query_refs, message_refs = refs[4 : 4 + n], refs[4 + n : 4 + 2 * n]
    blocks_ref, scores, peaks, totals, sums = refs[4 + 2 * n :]
    rows = n * group * tokens
    own_block = ctx_blocks + fin_blocks
    is_owner, limit, query_block = meta_ref[0], meta_ref[1], meta_ref[2]
    lane = lax.broadcasted_iota(jnp.int32, (1, 2 * BLOCK), 1)
    stat_lane = lax.broadcasted_iota(jnp.int32, (1, LANES), 1)

    def gather_block(i, count):
        blocks_ref[count] = i
        return count + jnp.where(mask_ref[query_block, i] > 0, 1, 0)

    full = lax.fori_loop(0, ctx_blocks, gather_block, jnp.int32(0))
    for i in range(fin_blocks):
        blocks_ref[full] = ctx_blocks + i
        full = full + is_owner
    blocks_ref[full] = own_block
    blocks_ref[full + 1] = own_block
    pairs = (full + 2) // 2

    def cols(h):
        return slice(h * HD, (h + 1) * HD)

    queries = [
        jnp.concatenate([ref[:, cols(g * group + a)] for ref in query_refs for a in range(group)], axis=0)
        for g in range(kv)
    ]

    def block_rows(ref, j, g, count):
        parts = [
            ref[pl.ds(pl.multiple_of(blocks_ref[2 * j + i] * BLOCK, BLOCK), BLOCK), cols(g)] for i in range(2 * count)
        ]
        return jnp.concatenate(parts, axis=0)

    def score(j, count, masked):
        for g in range(kv):
            top = peaks[g]
            for i in range(count):
                s = lax.dot_general(
                    queries[g], block_rows(keys_ref, j + i, g, 1), (((1,), (1,)), ((), ())), preferred_element_type=F32
                )
                if masked:
                    bound = jnp.where(2 * j < full, BLOCK, limit)
                    bound_next = jnp.where(2 * j + 1 == full, limit, 0)
                    edge = jnp.where(lane < BLOCK, bound, BLOCK + bound_next)
                    s = s + jnp.where(lane < edge, 0.0, FLOOR)
                scores[j + i, g] = s
                top = jnp.maximum(top, jnp.maximum(s[:, :BLOCK], s[:, BLOCK:]))
            peaks[g] = top

    def accumulate(j, count):
        for g in range(kv):
            total, weights = totals[g], []
            for i in range(count):
                s = scores[j + i, g]
                for half in range(2):
                    w = jnp.exp2(s[:, half * BLOCK : (half + 1) * BLOCK] * SCALE - peaks[g])
                    total = total + w
                    weights.append(w.astype(BF))
            totals[g] = total
            sums[g] += jnp.dot(
                jnp.concatenate(weights, axis=1), block_rows(values_ref, j, g, count), preferred_element_type=F32
            )

    def by_twos(total, step):
        pl.loop(0, total // 2)(lambda j: step(2 * j, 2))
        pl.when(total % 2 == 1)(lambda: step(total - 1, 1))

    peaks[...] = jnp.full(peaks.shape, LOW_PEAK, F32)
    by_twos(pairs - 1, lambda j, count: score(j, count, False))
    score(pairs - 1, 1, True)

    for g in range(kv):
        peak = jnp.max(peaks[g], axis=1, keepdims=True) * SCALE
        peaks[g] = jnp.broadcast_to(peak.astype(BF).astype(F32), (rows, LANES))
    totals[...] = jnp.zeros(totals.shape, F32)
    sums[...] = jnp.zeros(sums.shape, F32)
    by_twos(pairs, accumulate)

    stats = [jnp.zeros((tokens, LANES), F32) for _ in range(n)]
    for g in range(kv):
        total = jnp.broadcast_to(jnp.sum(totals[g], axis=1, keepdims=True), (rows, LANES))
        coarse = total.astype(BF).astype(F32)
        for r in range(n):
            for a in range(group):
                h = g * group + a
                part = slice((r * group + a) * tokens, (r * group + a + 1) * tokens)
                message_refs[r][:, cols(h)] = sums[g, part].astype(BF)
                for at, value in enumerate((peaks[g, part], coarse[part], total[part] - coarse[part])):
                    stats[r] = jnp.where(stat_lane == 3 * h + at, value, stats[r])
    for r in range(n):
        message_refs[r][:, kv * group * HD :] = stats[r].astype(BF)


def attend(meta, mask, keys, values, queries, kv, fin_blocks):
    tokens, width = queries[0].shape
    n = len(queries)
    group = width // (kv * HD)
    ctx_blocks = mask.shape[1]
    slots = ctx_blocks + fin_blocks + 2
    rows = n * group * tokens
    return pl.pallas_call(
        functools.partial(attend_body, (kv, group, tokens, ctx_blocks, fin_blocks, n)),
        in_specs=[smem_spec(), smem_spec()] + [vmem_spec()] * (2 + n),
        out_specs=[vmem_spec()] * n,
        out_shape=[jax.ShapeDtypeStruct((tokens, width + LANES), BF)] * n,
        scratch_shapes=[
            pltpu.SMEM((slots + 1,), jnp.int32),
            pltpu.VMEM(((slots + 1) // 2, kv, rows, 2 * BLOCK), F32),
            pltpu.VMEM((kv, rows, LANES), F32),
            pltpu.VMEM((kv, rows, LANES), F32),
            pltpu.VMEM((kv, rows, HD), F32),
        ],
        cost_estimate=pl.CostEstimate(
            flops=4 * rows * kv * HD * BLOCK * slots // 2,
            bytes_accessed=2 * keys.size * 2,
            transcendentals=rows * kv * BLOCK * slots // 2,
        ),
        compiler_params=params(),
        name="attend",
    )(meta, mask, keys, values, *queries)


def merge_body(heads, *refs):
    *parts, out_ref = refs
    loaded = [part[:, heads * HD :].astype(F32) for part in parts]
    for h in range(heads):
        peaks = [s[:, 3 * h : 3 * h + 1] for s in loaded]
        totals = [s[:, 3 * h + 1 : 3 * h + 2] + s[:, 3 * h + 2 : 3 * h + 3] for s in loaded]
        top = functools.reduce(jnp.maximum, peaks)
        factors = [jnp.exp2(p - top) for p in peaks]
        inverse = 1.0 / sum(f * t for f, t in zip(factors, totals, strict=True))
        cols = slice(h * HD, (h + 1) * HD)
        out_ref[:, cols] = sum(
            part[:, cols].astype(F32) * (f * inverse) for part, f in zip(parts, factors, strict=True)
        ).astype(BF)


def merge(parts, heads):
    tokens = parts[0].shape[0]
    return pl.pallas_call(
        functools.partial(merge_body, heads),
        in_specs=[pl.BlockSpec(memory_space=pltpu.VMEM)] * len(parts),
        out_specs=pl.BlockSpec(memory_space=pltpu.VMEM),
        out_shape=jax.ShapeDtypeStruct((tokens, heads * HD), BF),
        compiler_params=params(),
        name="merge",
    )(*parts)


def per_device(
    n_seq,
    n_head,
    segment_query,
    segment_memory,
    finished_memory,
    cache_memory,
    block_mask,
    owner_index,
    valid_count,
    output_weight,
):
    here = lax.axis_index("seq")
    own_tokens, width = segment_query.shape
    heads = width // HD
    kv = segment_memory.shape[2] // HD
    fin_blocks = finished_memory.shape[0] // BLOCK
    direct = n_seq == 4 and n_head == 4 and BLOCK == 2 * own_tokens

    is_owner = (here == owner_index[0]).astype(jnp.int32)
    limit = jnp.clip(valid_count[0] - here * own_tokens, 0, own_tokens)

    if direct:
        def toward(k):
            return [(i, i ^ k) for i in range(n_seq)]

        queries = [segment_query] + [lax.ppermute(segment_query, "seq", toward(k)) for k in range(1, n_seq)]
        per_block = BLOCK // own_tokens
        batches = [(((here ^ k) * own_tokens) // BLOCK, queries[k : k + per_block]) for k in range(0, n_seq, per_block)]
    else:
        gathered = lax.all_gather(segment_query, "seq", axis=0, tiled=True)
        batches = [(i, [gathered[i * BLOCK : (i + 1) * BLOCK]]) for i in range(gathered.shape[0] // BLOCK)]

    keys, values = prepare(block_mask, cache_memory, finished_memory, segment_memory)
    messages = []
    for query_block, queries in batches:
        meta = jnp.stack([is_owner, limit, jnp.asarray(query_block, jnp.int32)])
        messages += attend(meta, block_mask, keys, values, queries, kv, fin_blocks)

    if direct:
        parts = [messages[0]] + [lax.ppermute(messages[k], "seq", toward(k)) for k in range(1, n_seq)]
        attended = merge(parts, heads)
        shards = [attended] + [lax.ppermute(attended, "seq", toward(k)) for k in range(1, n_seq)]
        stacked = jnp.stack(shards)
        projected = jnp.einsum("ktf,fd->ktd", stacked, output_weight, preferred_element_type=F32)
        head_at = lax.axis_index("head")
        tile = projected.shape[1:]
        core, side = head_at % 2, head_at // 2

        def shard_of(token_shard):
            return lax.dynamic_index_in_dim(projected, token_shard ^ here, 0, keepdims=False)

        mine_core = [shard_of(core), shard_of(2 + core)]
        other_core = jnp.stack([shard_of(1 - core), shard_of(3 - core)]).astype(BF)
        received = lax.ppermute(other_core, "head", [(i, i ^ 1) for i in range(n_head)])
        joined = jnp.stack(mine_core) + received.astype(F32)
        mine = lax.dynamic_index_in_dim(joined, side, 0, keepdims=False)
        other = lax.dynamic_index_in_dim(joined, 1 - side, 0, keepdims=False).astype(BF)
        return mine + lax.ppermute(other, "head", [(i, i ^ 2) for i in range(n_head)]).astype(F32)

    sent = jnp.concatenate(messages, axis=0)
    got = lax.all_to_all(sent, "seq", 0, 0, tiled=True).reshape(n_seq, own_tokens, -1)
    attended = merge([got[i] for i in range(n_seq)], heads)
    attended = lax.all_gather(attended, "seq", axis=0, tiled=True)
    return lax.psum_scatter(
        jnp.dot(attended, output_weight, preferred_element_type=F32), "head", scatter_dimension=0, tiled=True
    )


def solution(mesh):
    return jax.shard_map(
        functools.partial(per_device, mesh.shape["seq"], mesh.shape["head"]),
        mesh=mesh,
        in_specs=(
            P(("groups", "seq"), "head"),
            P(("groups", "seq"), None, "head"),
            P(("groups", "seq"), None, "head"),
            P(("groups", "seq"), None, "head"),
            P("groups", "seq"),
            P("groups"),
            P("groups"),
            P("head", "seq"),
        ),
        out_specs=P(("groups", "head"), "seq"),
        check_vma=False,
    )
```

time: 83.2 us -> 61.6 us (0.74)
  Pallas kernels: 22.8 us -> 13.9 us
  local copies, waits for them, and re-layouts: 11.6 us -> 5.43 us
  starting transfers between devices: 19.3 us -> 14.8 us
  waiting for transfers between devices: 24.2 us -> 22.2 us
    pallas_call x2 -> x3, Pallas kernels: 22.3 us -> 13.4 us  [the longest x2 9.81 us: attend(): pl.pallas_call(functools.partial(attend_body, (kv, group, tokens, ctx_blo...]
    unnamed x24 -> x14, local copies, waits for them, and re-layouts: 11.4 us -> 5.32 us
    ppermute x3, starting transfers between devices: 7.5 us -> 3.15 us  [per_device(): lax.ppermute(messages[k], 'seq', toward(k))]
    ppermute x3, waiting for transfers between devices: 10.7 us -> 7.63 us  [per_device(): lax.ppermute(messages[k], 'seq', toward(k))]
    ppermute x3, waiting for transfers between devices: 7.83 us -> 8.86 us  [per_device(): lax.ppermute(attended, 'seq', toward(k))]
  transfers between devices with their start and end apart: 11 -> 11, of which waited for: 6 -> 6; matrix products, arithmetic and copies ran while one was open for 0% -> 0% of each run, Pallas kernels for 11% -> 22%
where the time goes in v2:
time: 61.6 us; the launch traced here: 61 us
  waiting for transfers between devices  22.2 us (36%)
  starting transfers between devices  14.8 us (24%)
  Pallas kernels  13.9 us (23%)
  local copies, waits for them, and re-layouts  5.43 us (9%)
  other arithmetic  1.67 us (3%)
  matrix products  1.61 us (3%)
  between operations  1.42 us (2%)
    pallas_call x2, Pallas kernels, attend(): pl.pallas_call(functools.partial(attend_body, (kv, group, tokens, ctx_blo...  9.81 us
    ppermute x3, waiting for transfers between devices, per_device(): lax.ppermute(attended, 'seq', toward(k))  8.86 us
    ppermute x3, waiting for transfers between devices, per_device(): lax.ppermute(messages[k], 'seq', toward(k))  7.63 us
    ppermute x3, starting transfers between devices, per_device(): lax.ppermute(segment_query, 'seq', toward(k))  5.62 us
    unnamed x14, local copies, waits for them, and re-layouts  5.32 us
    ppermute x3, starting transfers between devices, per_device(): lax.ppermute(attended, 'seq', toward(k))  4.45 us
    ppermute x1, waiting for transfers between devices, per_device(): lax.ppermute(other, 'head', [(i, i ^ 2) for i in range(n_head)]).astype(F32)  4.03 us
    pallas_call x1, Pallas kernels, prepare(): pl.pallas_call(functools.partial(prepare_body, ctx_blocks, fin_blocks, ow...  3.56 us
  transfers between devices with their start and end apart: 11, of which 6 were waited for; matrix products, arithmetic and copies ran while one was open for 0% of the time, Pallas kernels for 22%

profile of v2, /device:TPU:0, one launch (start us, length us, event | category | flops | bytes accessed | tf_op | source)
XLA Modules:
  0.0 61.0 jit_solution(10587859446867660260)
XLA Ops:
  0.0 4.0 %collective-permute-start.2 = (bf16[64,1024]{1,0:T(8,128)(2,1)}, bf16[64,1024]{1,0:T(8,128)(2,1)S(1)}, u32[]{:S(2)}, u32[]{:S(2)}) collective-permute-start(bf16[64,1024]{1,0:T(8,128)(2,1)} %refs_4_.1), channel_id=1, source_target_pairs={{0,8},{4,12},{8,0},{12,4},{1,9},{5,13},{9,1},{13,5},{2,10},{6,14},... | collective-permute-start | bytes 393224 | tf_op jit(solution)/shard_map/ppermute | solution.py:267
  4.0 1.3 %collective-permute-start.3 = (bf16[64,1024]{1,0:T(8,128)(2,1)}, bf16[64,1024]{1,0:T(8,128)(2,1)S(1)}, u32[]{:S(2)}, u32[]{:S(2)}) collective-permute-start(bf16[64,1024]{1,0:T(8,128)(2,1)} %refs_4_.1), channel_id=1, source_target_pairs={{0,12},{4,8},{8,4},{12,0},{1,13},{5,9},{9,5},{13,1},{2,14},{6,10},... | collective-permute-start | bytes 393224 | tf_op jit(solution)/shard_map/ppermute | solution.py:267
  7.1 2.2 %copy-done.1 = bf16[4096,2,256]{2,1,0:T(2,128)(2,1)S(1)} copy-done((bf16[4096,2,256]{2,1,0:T(2,128)(2,1)S(1)}, bf16[4096,2,256]{2,1,0:T(2,128)(2,1)}, u32[]{:S(2)}) %copy-start.1) | copy-done | bytes 4194328
  9.3 0.9 %copy-done.2 = bf16[256,2,256]{2,1,0:T(2,128)(2,1)S(1)} copy-done((bf16[256,2,256]{2,1,0:T(2,128)(2,1)S(1)}, bf16[256,2,256]{2,1,0:T(2,128)(2,1)}, u32[]{:S(2)}) %copy-start.2) | copy-done | bytes 262168
  10.2 0.8 %copy-done.4 = bf16[64,2,256]{2,1,0:T(2,128)(2,1)S(1)} copy-done((bf16[64,2,256]{2,1,0:T(2,128)(2,1)S(1)}, bf16[64,2,256]{2,1,0:T(2,128)(2,1)}, u32[]{:S(2)}) %copy-start.4) | copy-done | bytes 65560
  11.1 0.7 %copy-done.5 = s32[2,32]{1,0:T(2,128)S(1)} copy-done((s32[2,32]{1,0:T(2,128)S(1)}, s32[2,32]{1,0:T(2,128)}, u32[]{:S(2)}) %copy-start.5) | copy-done | bytes 280
  11.7 3.6 %prepare.1 = (bf16[4480,256]{1,0:T(8,128)(2,1)S(1)}, bf16[4480,256]{1,0:T(8,128)(2,1)S(1)}) custom-call(s32[2,32]{1,0:T(2,128)S(1)} %copy-done.5, bf16[4096,2,256]{2,1,0:T(2,128)(2,1)S(1)} %copy-done.1, bf16[256,2,256]{2,1,0:T(2,128)(2,1)S(1)} %copy-done.2, bf16[64,2,256]{2,1,0:T(2,128)(2,1)S(1)} %copy-done.4), custom_call_target="tpu_custom_call" | custom-call | bytes 12582912 | tf_op jit(solution)/shard_map/prepare/pallas_call | solution.py:76
  15.3 4.7 %attend.3 = (bf16[64,1152]{1,0:T(8,128)(2,1)S(1)}, bf16[64,1152]{1,0:T(8,128)(2,1)S(1)}) custom-call(s32[3]{0:T(128)S(1)} %pad_add_fusion.2.refs_0_, s32[2,32]{1,0:T(2,128)S(1)} %copy-done.5, bf16[4480,256]{1,0:T(8,128)(2,1)S(1)} %get-tuple-element.11.refs_2_, bf16[4480,256]{1,0:T(8,128)(2,1)S(1)} %get-tuple-element.12.refs_3_, ...), custom_call_target="tpu_custom_call" | custom-call | flops 1207959552 | bytes 4587520 | tf_op jit(solution)/shard_map/attend/pallas_call | solution.py:192
  20.0 2.6 %collective-permute-start.4 = (bf16[64,1152]{1,0:T(8,128)(2,1)S(1)}, bf16[64,1152]{1,0:T(8,128)(2,1)S(1)}, u32[]{:S(2)}, u32[]{:S(2)}) collective-permute-start(bf16[64,1152]{1,0:T(8,128)(2,1)S(1)} %get-tuple-element.15), channel_id=1, source_target_pairs={{0,8},{4,12},{8,0},{12,4},{1,9},{5,13},{9,1},{13,5},{2,10},{6,14},... | collective-permute-start | bytes 442376 | tf_op jit(solution)/shard_map/ppermute | solution.py:281
  22.8 5.1 %attend.2 = (bf16[64,1152]{1,0:T(8,128)(2,1)S(1)}, bf16[64,1152]{1,0:T(8,128)(2,1)S(1)}) custom-call(s32[3]{0:T(128)S(1)} %pad_add_fusion.refs_0_, s32[2,32]{1,0:T(2,128)S(1)} %copy-done.5, bf16[4480,256]{1,0:T(8,128)(2,1)S(1)} %get-tuple-element.11.refs_2_, bf16[4480,256]{1,0:T(8,128)(2,1)S(1)} %get-tuple-element.12.refs_3_, ...), custom_call_target="tpu_custom_call" | custom-call | flops 1207959552 | bytes 4587520 | tf_op jit(solution)/shard_map/attend/pallas_call | solution.py:192
  28.3 4.6 %collective-permute-done.4.refs_2_ = bf16[64,1152]{1,0:T(8,128)(2,1)S(1)} collective-permute-done((bf16[64,1152]{1,0:T(8,128)(2,1)S(1)}, bf16[64,1152]{1,0:T(8,128)(2,1)S(1)}, u32[]{:S(2)}, u32[]{:S(2)}) %collective-permute-start.4) | collective-permute-done | bytes 147488 | tf_op jit(solution)/shard_map/ppermute | solution.py:281
  32.9 3.0 %collective-permute-done.1.refs_1_ = bf16[64,1152]{1,0:T(8,128)(2,1)S(1)} collective-permute-done((bf16[64,1152]{1,0:T(8,128)(2,1)S(1)}, bf16[64,1152]{1,0:T(8,128)(2,1)S(1)}, u32[]{:S(2)}, u32[]{:S(2)}) %collective-permute-start.1) | collective-permute-done | bytes 147488 | tf_op jit(solution)/shard_map/ppermute | solution.py:281
  36.5 0.7 %collective-permute-start.6 = (bf16[64,1024]{1,0:T(8,128)(2,1)S(1)}, bf16[64,1024]{1,0:T(8,128)(2,1)S(1)}, u32[]{:S(2)}, u32[]{:S(2)}) collective-permute-start(bf16[64,1024]{1,0:T(8,128)(2,1)S(1)} %merge.1), channel_id=1, source_target_pairs={{0,4},{4,0},{8,12},{12,8},{1,5},{5,1},{9,13},{13,9},{2,6},{6,2},{1... | collective-permute-start | bytes 393224 | tf_op jit(solution)/shard_map/ppermute | solution.py:283
  37.2 0.9 %collective-permute-start.7 = (bf16[64,1024]{1,0:T(8,128)(2,1)S(1)}, bf16[64,1024]{1,0:T(8,128)(2,1)S(1)}, u32[]{:S(2)}, u32[]{:S(2)}) collective-permute-start(bf16[64,1024]{1,0:T(8,128)(2,1)S(1)} %merge.1), channel_id=1, source_target_pairs={{0,8},{4,12},{8,0},{12,4},{1,9},{5,13},{9,1},{13,5},{2,10},{6,14},... | collective-permute-start | bytes 393224 | tf_op jit(solution)/shard_map/ppermute | solution.py:283
  38.1 2.8 %collective-permute-start.8 = (bf16[64,1024]{1,0:T(8,128)(2,1)S(1)}, bf16[64,1024]{1,0:T(8,128)(2,1)S(1)}, u32[]{:S(2)}, u32[]{:S(2)}) collective-permute-start(bf16[64,1024]{1,0:T(8,128)(2,1)S(1)} %merge.1), channel_id=1, source_target_pairs={{0,12},{4,8},{8,4},{12,0},{1,13},{5,9},{9,5},{13,1},{2,14},{6,10},... | collective-permute-start | bytes 393224 | tf_op jit(solution)/shard_map/ppermute | solution.py:283
  40.9 2.0 %collective-permute-done.6 = bf16[64,1024]{1,0:T(8,128)(2,1)S(1)} collective-permute-done((bf16[64,1024]{1,0:T(8,128)(2,1)S(1)}, bf16[64,1024]{1,0:T(8,128)(2,1)S(1)}, u32[]{:S(2)}, u32[]{:S(2)}) %collective-permute-start.6) | collective-permute-done | bytes 131104 | tf_op jit(solution)/shard_map/ppermute | solution.py:283
  42.9 6.9 %collective-permute-done.7 = bf16[64,1024]{1,0:T(8,128)(2,1)S(1)} collective-permute-done((bf16[64,1024]{1,0:T(8,128)(2,1)S(1)}, bf16[64,1024]{1,0:T(8,128)(2,1)S(1)}, u32[]{:S(2)}, u32[]{:S(2)}) %collective-permute-start.7) | collective-permute-done | bytes 131104 | tf_op jit(solution)/shard_map/ppermute | solution.py:283
  49.8 0.7 %copy-done.6 = bf16[64,1024]{1,0:T(8,128)(2,1)} copy-done((bf16[64,1024]{1,0:T(8,128)(2,1)}, bf16[64,1024]{1,0:T(8,128)(2,1)S(1)}, u32[]{:S(2)}) %copy-start.6) | copy-done | bytes 131096
  50.5 1.6 %fusion = f32[4,64,1024]{2,1,0:T(8,128)S(1)} fusion(bf16[1024,1024]{1,0:T(8,128)(2,1)S(1)} %copy-done, bf16[1,64,1024]{2,1,0:T(8,128)(2,1)} %bitcast.22, bf16[1,64,1024]{2,1,0:T(8,128)(2,1)S(1)} %bitcast.21, bf16[1,64,1024]{2,1,0:T(8,128)(2,1)S(1)} %bitcast.20, bf16[1,64,1024]{2,1,0:T(8,128)(2,1)S(1)} %bitcast.19), kind=kOutput, calls=%fused_computation | convolution fusion | flops 537657344 | bytes 3670016 | tf_op jit(solution)/shard_map/ktf,fd->ktd/dot_general | solution.py:285
  52.1 0.7 %pad_maximum_fusion = bf16[2,64,1024]{2,1,0:T(8,128)(2,1)} fusion(bf16[1,64,1024]{2,1,0:T(8,128)(2,1)S(1)} %get-tuple-element.18, bf16[1,64,1024]{2,1,0:T(8,128)(2,1)S(1)} %get-tuple-element.17), kind=kLoop, calls=%fused_computation.10 | loop fusion | flops 131072 | bytes 524288 | tf_op jit(solution)/shard_map/stack | solution.py:294
  52.9 1.7 %collective-permute-done.9 = bf16[2,64,1024]{2,1,0:T(8,128)(2,1)S(1)} collective-permute-done((bf16[2,64,1024]{2,1,0:T(8,128)(2,1)}, bf16[2,64,1024]{2,1,0:T(8,128)(2,1)S(1)}, u32[]{:S(2)}, u32[]{:S(2)}) %collective-permute-start.9) | collective-permute-done | bytes 262176 | tf_op jit(solution)/shard_map/ppermute | solution.py:295
  54.7 1.6 %collective-permute-start.10 = (bf16[64,1024]{1,0:T(8,128)(2,1)S(1)}, bf16[64,1024]{1,0:T(8,128)(2,1)S(1)}, u32[]{:S(2)}, u32[]{:S(2)}) collective-permute-start(bf16[64,1024]{1,0:T(8,128)(2,1)S(1)} %fusion.9), channel_id=1, source_target_pairs={{0,2},{1,3},{2,0},{3,1},{4,6},{5,7},{6,4},{7,5},{8,10},{9,11},{10,... | collective-permute-start | bytes 393224 | tf_op jit(solution)/shard_map/ppermute | solution.py:299
  56.3 4.0 %collective-permute-done.10 = bf16[64,1024]{1,0:T(8,128)(2,1)S(1)} collective-permute-done((bf16[64,1024]{1,0:T(8,128)(2,1)S(1)}, bf16[64,1024]{1,0:T(8,128)(2,1)S(1)}, u32[]{:S(2)}, u32[]{:S(2)}) %collective-permute-start.10) | collective-permute-done | bytes 131104 | tf_op jit(solution)/shard_map/ppermute | solution.py:299
  60.3 0.7 %bitcast_add_fusion = f32[64,1024]{1,0:T(8,128)} fusion(bf16[64,1024]{1,0:T(8,128)(2,1)S(1)} %collective-permute-done.10, f32[2,64,1024]{2,1,0:T(8,128)S(1)} %maximum_add_fusion, s32[]{:T(128)S(6)} %select_n.45), kind=kLoop, calls=%fused_computation.11 | loop fusion | flops 131072 | bytes 655364 | tf_op jit(solution)/shard_map/add | solution.py:299
  (25 shorter events, 1.6 us)
Async XLA Ops:
  0.0 50.5 %copy-start = (bf16[1024,1024]{1,0:T(8,128)(2,1)S(1)}, bf16[1024,1024]{1,0:T(8,128)(2,1)}, u32[]{:S(2)}) copy-start(bf16[1024,1024]{1,0:T(8,128)(2,1)} %param.15) | copy-start | bytes 6291460
  0.0 15.3 %collective-permute-start.2 = (bf16[64,1024]{1,0:T(8,128)(2,1)}, bf16[64,1024]{1,0:T(8,128)(2,1)S(1)}, u32[]{:S(2)}, u32[]{:S(2)}) collective-permute-start(bf16[64,1024]{1,0:T(8,128)(2,1)} %refs_4_.1), channel_id=1, source_target_pairs={{0,8},{4,12},{8,0},{12,4},{1,9},{5,13},{9,1},{13,5},{2,10},{6,14},... | collective-permute-start | bytes 393224 | tf_op jit(solution)/shard_map/ppermute | solution.py:267
  4.0 11.3 %collective-permute-start.3 = (bf16[64,1024]{1,0:T(8,128)(2,1)}, bf16[64,1024]{1,0:T(8,128)(2,1)S(1)}, u32[]{:S(2)}, u32[]{:S(2)}) collective-permute-start(bf16[64,1024]{1,0:T(8,128)(2,1)} %refs_4_.1), channel_id=1, source_target_pairs={{0,12},{4,8},{8,4},{12,0},{1,13},{5,9},{9,5},{13,1},{2,14},{6,10},... | collective-permute-start | bytes 393224 | tf_op jit(solution)/shard_map/ppermute | solution.py:267
  5.4 17.4 %collective-permute-start = (bf16[64,1024]{1,0:T(8,128)(2,1)}, bf16[64,1024]{1,0:T(8,128)(2,1)S(1)}, u32[]{:S(2)}, u32[]{:S(2)}) collective-permute-start(bf16[64,1024]{1,0:T(8,128)(2,1)} %refs_4_.1), channel_id=1, source_target_pairs={{0,4},{4,0},{8,12},{12,8},{1,5},{5,1},{9,13},{13,9},{2,6},{6,2},{1... | collective-permute-start | bytes 393224 | tf_op jit(solution)/shard_map/ppermute | solution.py:267
  7.1 2.2 %copy-start.1 = (bf16[4096,2,256]{2,1,0:T(2,128)(2,1)S(1)}, bf16[4096,2,256]{2,1,0:T(2,128)(2,1)}, u32[]{:S(2)}) copy-start(bf16[4096,2,256]{2,1,0:T(2,128)(2,1)} %cache_ref.1) | copy-start | bytes 12582916
  9.3 0.9 %copy-start.2 = (bf16[256,2,256]{2,1,0:T(2,128)(2,1)S(1)}, bf16[256,2,256]{2,1,0:T(2,128)(2,1)}, u32[]{:S(2)}) copy-start(bf16[256,2,256]{2,1,0:T(2,128)(2,1)} %fin_ref.1) | copy-start | bytes 786436
  10.2 0.8 %copy-start.4 = (bf16[64,2,256]{2,1,0:T(2,128)(2,1)S(1)}, bf16[64,2,256]{2,1,0:T(2,128)(2,1)}, u32[]{:S(2)}) copy-start(bf16[64,2,256]{2,1,0:T(2,128)(2,1)} %own_ref.1) | copy-start | bytes 196612
  11.1 0.7 %copy-start.5 = (s32[2,32]{1,0:T(2,128)S(1)}, s32[2,32]{1,0:T(2,128)}, u32[]{:S(2)}) copy-start(s32[2,32]{1,0:T(2,128)} %refs_1_.3) | copy-start | bytes 772
  15.3 7.4 %copy-start.3 = (bf16[64,1024]{1,0:T(8,128)(2,1)S(1)}, bf16[64,1024]{1,0:T(8,128)(2,1)}, u32[]{:S(2)}) copy-start(bf16[64,1024]{1,0:T(8,128)(2,1)} %refs_4_.1) | copy-start | bytes 393220
  20.0 12.9 %collective-permute-start.4 = (bf16[64,1152]{1,0:T(8,128)(2,1)S(1)}, bf16[64,1152]{1,0:T(8,128)(2,1)S(1)}, u32[]{:S(2)}, u32[]{:S(2)}) collective-permute-start(bf16[64,1152]{1,0:T(8,128)(2,1)S(1)} %get-tuple-element.15), channel_id=1, source_target_pairs={{0,8},{4,12},{8,0},{12,4},{1,9},{5,13},{9,1},{13,5},{2,10},{6,14},... | collective-permute-start | bytes 442376 | tf_op jit(solution)/shard_map/ppermute | solution.py:281
  22.7 10.3 %collective-permute-start.5 = (bf16[64,1152]{1,0:T(8,128)(2,1)S(1)}, bf16[64,1152]{1,0:T(8,128)(2,1)S(1)}, u32[]{:S(2)}, u32[]{:S(2)}) collective-permute-start(bf16[64,1152]{1,0:T(8,128)(2,1)S(1)} %get-tuple-element.16), channel_id=1, source_target_pairs={{0,12},{4,8},{8,4},{12,0},{1,13},{5,9},{9,5},{13,1},{2,14},{6,10},... | collective-permute-start | bytes 442376 | tf_op jit(solution)/shard_map/ppermute | solution.py:281
  27.9 8.1 %collective-permute-start.1 = (bf16[64,1152]{1,0:T(8,128)(2,1)S(1)}, bf16[64,1152]{1,0:T(8,128)(2,1)S(1)}, u32[]{:S(2)}, u32[]{:S(2)}) collective-permute-start(bf16[64,1152]{1,0:T(8,128)(2,1)S(1)} %get-tuple-element.14), channel_id=1, source_target_pairs={{0,4},{4,0},{8,12},{12,8},{1,5},{5,1},{9,13},{13,9},{2,6},{6,2},{1... | collective-permute-start | bytes 442376 | tf_op jit(solution)/shard_map/ppermute | solution.py:281
  36.5 6.4 %collective-permute-start.6 = (bf16[64,1024]{1,0:T(8,128)(2,1)S(1)}, bf16[64,1024]{1,0:T(8,128)(2,1)S(1)}, u32[]{:S(2)}, u32[]{:S(2)}) collective-permute-start(bf16[64,1024]{1,0:T(8,128)(2,1)S(1)} %merge.1), channel_id=1, source_target_pairs={{0,4},{4,0},{8,12},{12,8},{1,5},{5,1},{9,13},{13,9},{2,6},{6,2},{1... | collective-permute-start | bytes 393224 | tf_op jit(solution)/shard_map/ppermute | solution.py:283
  37.2 12.6 %collective-permute-start.7 = (bf16[64,1024]{1,0:T(8,128)(2,1)S(1)}, bf16[64,1024]{1,0:T(8,128)(2,1)S(1)}, u32[]{:S(2)}, u32[]{:S(2)}) collective-permute-start(bf16[64,1024]{1,0:T(8,128)(2,1)S(1)} %merge.1), channel_id=1, source_target_pairs={{0,8},{4,12},{8,0},{12,4},{1,9},{5,13},{9,1},{13,5},{2,10},{6,14},... | collective-permute-start | bytes 393224 | tf_op jit(solution)/shard_map/ppermute | solution.py:283
  38.1 11.7 %collective-permute-start.8 = (bf16[64,1024]{1,0:T(8,128)(2,1)S(1)}, bf16[64,1024]{1,0:T(8,128)(2,1)S(1)}, u32[]{:S(2)}, u32[]{:S(2)}) collective-permute-start(bf16[64,1024]{1,0:T(8,128)(2,1)S(1)} %merge.1), channel_id=1, source_target_pairs={{0,12},{4,8},{8,4},{12,0},{1,13},{5,9},{9,5},{13,1},{2,14},{6,10},... | collective-permute-start | bytes 393224 | tf_op jit(solution)/shard_map/ppermute | solution.py:283
  49.8 0.7 %copy-start.6 = (bf16[64,1024]{1,0:T(8,128)(2,1)}, bf16[64,1024]{1,0:T(8,128)(2,1)S(1)}, u32[]{:S(2)}) copy-start(bf16[64,1024]{1,0:T(8,128)(2,1)S(1)} %collective-permute-done.8) | copy-start | bytes 393220
  52.9 1.7 %collective-permute-start.9 = (bf16[2,64,1024]{2,1,0:T(8,128)(2,1)}, bf16[2,64,1024]{2,1,0:T(8,128)(2,1)S(1)}, u32[]{:S(2)}, u32[]{:S(2)}) collective-permute-start(bf16[2,64,1024]{2,1,0:T(8,128)(2,1)} %pad_maximum_fusion), channel_id=1, source_target_pairs={{0,1},{1,0},{2,3},{3,2},{4,5},{5,4},{6,7},{7,6},{8,9},{9,8},{10,11... | collective-permute-start | bytes 786440 | tf_op jit(solution)/shard_map/ppermute | solution.py:295
  54.7 5.6 %collective-permute-start.10 = (bf16[64,1024]{1,0:T(8,128)(2,1)S(1)}, bf16[64,1024]{1,0:T(8,128)(2,1)S(1)}, u32[]{:S(2)}, u32[]{:S(2)}) collective-permute-start(bf16[64,1024]{1,0:T(8,128)(2,1)S(1)} %fusion.9), channel_id=1, source_target_pairs={{0,2},{1,3},{2,0},{3,1},{4,6},{5,7},{6,4},{7,5},{8,10},{9,11},{10,... | collective-permute-start | bytes 393224 | tf_op jit(solution)/shard_map/ppermute | solution.py:299

commit v3 on v2

--- a/solution.py
+++ b/solution.py
@@ -18,7 +18,7 @@
 F32 = jnp.float32
 
 
-VMEM_LIMIT = 30 << 20
+VMEM_LIMIT = 26 << 20
 UNROLL = 4
 
 
@@ -34,8 +34,50 @@
     return pl.BlockSpec(memory_space=pltpu.SMEM)
 
 
-def prepare_body(ctx_blocks, fin_blocks, own_rows, mask_ref, cache_ref, fin_ref, own_ref, keys_ref, values_ref, used_ref):
+def list_body(fin_blocks, heading, meta_ref, lists_ref):
+    query_blocks, ctx_blocks = meta_ref.shape[0] - 1, meta_ref.shape[1]
+    end = lists_ref.shape[1] - 1
+    own_block = ctx_blocks + fin_blocks
+
+    def note(i, counts):
+        bits = [meta_ref[q, i] for q in range(query_blocks)]
+        bits.append(functools.reduce(lambda x, y: x | y, bits))
+        for q, count in enumerate(counts):
+            lists_ref[q, count] = i
+        return tuple(count + jnp.where(bit > 0, 1, 0) for count, bit in zip(counts, bits, strict=True))
+
+    counts = lax.fori_loop(0, ctx_blocks, note, (jnp.int32(0),) * (query_blocks + 1))
+    for q, count in enumerate(counts[:-1]):
+        for i in range(fin_blocks):
+            lists_ref[q, count] = ctx_blocks + i
+            count = count + meta_ref[query_blocks, 0]
+        lists_ref[q, count] = own_block
+        lists_ref[q, count + 1] = own_block
+        lists_ref[q, end] = count
+    for i in range(UNROLL - 1):
+        lists_ref[query_blocks, counts[-1] + i] = ctx_blocks - 1
+    lists_ref[query_blocks, end] = counts[-1]
+    for i in range(heading):
+        lists_ref[query_blocks + 1, i] = meta_ref[query_blocks, i]
+
+
+def make_lists(meta, fin_blocks, heading):
+    query_blocks, ctx_blocks = meta.shape[0] - 1, meta.shape[1]
+    shape = (query_blocks + 2, ctx_blocks + fin_blocks + UNROLL + 2)
+    return pl.pallas_call(
+        functools.partial(list_body, fin_blocks, heading),
+        in_specs=[smem_spec()],
+        out_specs=smem_spec(),
+        out_shape=jax.ShapeDtypeStruct(shape, jnp.int32),
+        cost_estimate=pl.CostEstimate(flops=4 * 1024**3, bytes_accessed=0, transcendentals=0),
+        compiler_params=params(),
+        name="lists",
+    )(meta)
+
+
+def prepare_body(ctx_blocks, lists_ref, cache_ref, fin_ref, own_ref, keys_ref, values_ref):
     width = keys_ref.shape[1]
+    any_row, end = lists_ref.shape[0] - 2, lists_ref.shape[1] - 1
     row = lax.broadcasted_iota(jnp.int32, (2 * BLOCK, 2 * BLOCK), 0)
     col = lax.broadcasted_iota(jnp.int32, (2 * BLOCK, 2 * BLOCK), 1)
     source = jnp.where(row < BLOCK, 2 * row, 2 * row - 2 * BLOCK + 1)
@@ -46,67 +88,45 @@
         keys_ref[pl.ds(start, BLOCK)] = parts[:BLOCK]
         values_ref[pl.ds(start, BLOCK)] = parts[BLOCK:]
 
-    def note(i, count):
-        used_ref[count] = i
-        used = mask_ref[0, i]
-        for q in range(1, mask_ref.shape[0]):
-            used = used | mask_ref[q, i]
-        return count + jnp.where(used > 0, 1, 0)
-
-    count = lax.fori_loop(0, ctx_blocks, note, jnp.int32(0))
-    for i in range(UNROLL):
-        used_ref[count + i] = ctx_blocks - 1
-
-    @pl.loop(0, (count + UNROLL - 1) // UNROLL)
+    @pl.loop(0, (lists_ref[any_row, end] + UNROLL - 1) // UNROLL)
     def _(j):
         for i in range(UNROLL):
-            start = pl.multiple_of(used_ref[j * UNROLL + i] * BLOCK, BLOCK)
+            start = pl.multiple_of(lists_ref[any_row, j * UNROLL + i] * BLOCK, BLOCK)
             take_apart(cache_ref[pl.ds(start, BLOCK)], start)
 
+    fin_blocks, own_rows = fin_ref.shape[0] // BLOCK, own_ref.shape[0]
     for i in range(fin_blocks):
-        take_apart(fin_ref[pl.ds(i * BLOCK, BLOCK)], (ctx_blocks + i) * BLOCK)
-    own = jnp.concatenate([own_ref[...], jnp.zeros((BLOCK - own_rows, 2, width), BF)], axis=0)
-    take_apart(own, (ctx_blocks + fin_blocks) * BLOCK)
-
-
-def prepare(mask, cache, finished, own):
+        take_apart(fin_ref[i * BLOCK : (i + 1) * BLOCK], (ctx_blocks + i) * BLOCK)
+    filler = jnp.zeros((BLOCK - own_rows, 2, width), BF)
+    take_apart(jnp.concatenate([own_ref[...], filler], axis=0), (ctx_blocks + fin_blocks) * BLOCK)
+
+
+def prepare(lists, cache, finished, own):
     rows, _, width = cache.shape
-    ctx_blocks, fin_blocks = rows // BLOCK, finished.shape[0] // BLOCK
-    total = (ctx_blocks + fin_blocks + 1) * BLOCK
+    total = rows + finished.shape[0] + BLOCK
     return pl.pallas_call(
-        functools.partial(prepare_body, ctx_blocks, fin_blocks, own.shape[0]),
+        functools.partial(prepare_body, rows // BLOCK),
         in_specs=[smem_spec(), vmem_spec(), vmem_spec(), vmem_spec()],
         out_specs=[vmem_spec(), vmem_spec()],
         out_shape=[jax.ShapeDtypeStruct((total, width), BF)] * 2,
-        scratch_shapes=[pltpu.SMEM((ctx_blocks + UNROLL,), jnp.int32)],
-        cost_estimate=pl.CostEstimate(flops=0, bytes_accessed=12 * 1024 * 1024, transcendentals=0),
+        cost_estimate=pl.CostEstimate(flops=4 * 1024**3, bytes_accessed=12 * 1024**2, transcendentals=0),
         compiler_params=params(),
         name="prepare",
-    )(mask, cache, finished, own)
+    )(lists, cache, finished, own)
 
 
 def attend_body(geometry, *refs):
-    kv, group, tokens, ctx_blocks, fin_blocks, n = geometry
-    meta_ref, mask_ref, keys_ref, values_ref = refs[:4]
-    query_refs, message_refs = refs[4 : 4 + n], refs[4 + n : 4 + 2 * n]
-    blocks_ref, scores, peaks, totals, sums = refs[4 + 2 * n :]
+    kv, group, tokens, n, at = geometry
+    lists_ref, keys_ref, values_ref = refs[:3]
+    query_refs, message_refs = refs[3 : 3 + n], refs[4 + n : 4 + 2 * n]
+    scores, peaks, totals, sums = refs[4 + 2 * n :]
     rows = n * group * tokens
-    own_block = ctx_blocks + fin_blocks
-    is_owner, limit, query_block = meta_ref[0], meta_ref[1], meta_ref[2]
+    heading = lists_ref.shape[0] - 1
+    limit, query_block = lists_ref[heading, 1], lists_ref[heading, 2 + at]
+    full = lists_ref[query_block, lists_ref.shape[1] - 1]
+    pairs = (full + 2) // 2
     lane = lax.broadcasted_iota(jnp.int32, (1, 2 * BLOCK), 1)
     stat_lane = lax.broadcasted_iota(jnp.int32, (1, LANES), 1)
-
-    def gather_block(i, count):
-        blocks_ref[count] = i
-        return count + jnp.where(mask_ref[query_block, i] > 0, 1, 0)
-
-    full = lax.fori_loop(0, ctx_blocks, gather_block, jnp.int32(0))
-    for i in range(fin_blocks):
-        blocks_ref[full] = ctx_blocks + i
-        full = full + is_owner
-    blocks_ref[full] = own_block
-    blocks_ref[full + 1] = own_block
-    pairs = (full + 2) // 2
 
     def cols(h):
         return slice(h * HD, (h + 1) * HD)
@@ -118,7 +138,7 @@
 
     def block_rows(ref, j, g, count):
         parts = [
-            ref[pl.ds(pl.multiple_of(blocks_ref[2 * j + i] * BLOCK, BLOCK), BLOCK), cols(g)] for i in range(2 * count)
+            ref[pl.ds(pl.multiple_of(lists_ref[query_block, 2 * j + i] * BLOCK, BLOCK), BLOCK), cols(g)] for i in range(2 * count)
         ]
         return jnp.concatenate(parts, axis=0)
 
@@ -152,12 +172,14 @@
                 jnp.concatenate(weights, axis=1), block_rows(values_ref, j, g, count), preferred_element_type=F32
             )
 
-    def by_twos(total, step):
-        pl.loop(0, total // 2)(lambda j: step(2 * j, 2))
+    def in_steps(total, step):
+        pl.loop(0, total // 4)(lambda j: step(4 * j, 4))
+        done = total // 4 * 4
+        pl.when(total - done >= 2)(lambda: step(done, 2))
         pl.when(total % 2 == 1)(lambda: step(total - 1, 1))
 
     peaks[...] = jnp.full(peaks.shape, LOW_PEAK, F32)
-    by_twos(pairs - 1, lambda j, count: score(j, count, False))
+    in_steps(pairs - 1, lambda j, count: score(j, count, False))
     score(pairs - 1, 1, True)
 
     for g in range(kv):
@@ -165,7 +187,7 @@
         peaks[g] = jnp.broadcast_to(peak.astype(BF).astype(F32), (rows, LANES))
     totals[...] = jnp.zeros(totals.shape, F32)
     sums[...] = jnp.zeros(sums.shape, F32)
-    by_twos(pairs, accumulate)
+    in_steps(pairs, accumulate)
 
     stats = [jnp.zeros((tokens, LANES), F32) for _ in range(n)]
     for g in range(kv):
@@ -182,20 +204,18 @@
         message_refs[r][:, kv * group * HD :] = stats[r].astype(BF)
 
 
-def attend(meta, mask, keys, values, queries, kv, fin_blocks):
+def attend(lists, keys, values, queries, after, kv, at):
     tokens, width = queries[0].shape
     n = len(queries)
     group = width // (kv * HD)
-    ctx_blocks = mask.shape[1]
-    slots = ctx_blocks + fin_blocks + 2
+    slots = keys.shape[0] // BLOCK + 1
     rows = n * group * tokens
     return pl.pallas_call(
-        functools.partial(attend_body, (kv, group, tokens, ctx_blocks, fin_blocks, n)),
-        in_specs=[smem_spec(), smem_spec()] + [vmem_spec()] * (2 + n),
+        functools.partial(attend_body, (kv, group, tokens, n, at)),
+        in_specs=[smem_spec()] + [vmem_spec()] * (2 + n) + [pl.BlockSpec(memory_space=pl.ANY)],
         out_specs=[vmem_spec()] * n,
         out_shape=[jax.ShapeDtypeStruct((tokens, width + LANES), BF)] * n,
         scratch_shapes=[
-            pltpu.SMEM((slots + 1,), jnp.int32),
             pltpu.VMEM(((slots + 1) // 2, kv, rows, 2 * BLOCK), F32),
             pltpu.VMEM((kv, rows, LANES), F32),
             pltpu.VMEM((kv, rows, LANES), F32),
@@ -208,7 +228,7 @@
         ),
         compiler_params=params(),
         name="attend",
-    )(meta, mask, keys, values, *queries)
+    )(lists, keys, values, *queries, after)
 
 
 def merge_body(heads, *refs):
@@ -260,43 +280,57 @@
     is_owner = (here == owner_index[0]).astype(jnp.int32)
     limit = jnp.clip(valid_count[0] - here * own_tokens, 0, own_tokens)
 
+    def swap(value, axis, size, k):
+        return lax.ppermute(value, axis, [(i, i ^ k) for i in range(size)])
+
+    def gather_over_seq(value):
+        near, far = swap(value, "seq", n_seq, 1), swap(value, "seq", n_seq, 2)
+        return [value, near, far, swap(far, "seq", n_seq, 1)]
+
     if direct:
-        def toward(k):
-            return [(i, i ^ k) for i in range(n_seq)]
-
-        queries = [segment_query] + [lax.ppermute(segment_query, "seq", toward(k)) for k in range(1, n_seq)]
-        per_block = BLOCK // own_tokens
-        batches = [(((here ^ k) * own_tokens) // BLOCK, queries[k : k + per_block]) for k in range(0, n_seq, per_block)]
+        batches = ((2,), (3,), (1,), (0,))
+        query_blocks = [((here ^ batch[0]) * own_tokens) // BLOCK for batch in batches]
+    else:
+        query_blocks = list(range(own_tokens * n_seq // BLOCK))
+    heading = jnp.stack([jnp.asarray(x, jnp.int32) for x in [is_owner, limit] + query_blocks])
+    heading_row = jnp.pad(heading, (0, block_mask.shape[1] - heading.shape[0]))
+    lists = make_lists(jnp.concatenate([block_mask, heading_row[None]]), fin_blocks, heading.shape[0])
+
+    if direct:
+        order = [k for batch in batches for k in batch]
+        arrived = gather_over_seq(segment_query)
+        queries = [[arrived[k] for k in batch] for batch in batches]
     else:
         gathered = lax.all_gather(segment_query, "seq", axis=0, tiled=True)
-        batches = [(i, [gathered[i * BLOCK : (i + 1) * BLOCK]]) for i in range(gathered.shape[0] // BLOCK)]
-
-    keys, values = prepare(block_mask, cache_memory, finished_memory, segment_memory)
+        queries = [[gathered[i * BLOCK : (i + 1) * BLOCK]] for i in query_blocks]
+
+    keys, values = prepare(lists, cache_memory, finished_memory, segment_memory)
     messages = []
-    for query_block, queries in batches:
-        meta = jnp.stack([is_owner, limit, jnp.asarray(query_block, jnp.int32)])
-        messages += attend(meta, block_mask, keys, values, queries, kv, fin_blocks)
+    for at, batch in enumerate(queries):
+        messages += attend(lists, keys, values, batch, messages[-1] if messages else lists, kv, at)
 
     if direct:
-        parts = [messages[0]] + [lax.ppermute(messages[k], "seq", toward(k)) for k in range(1, n_seq)]
+        parts = [m if k == 0 else swap(m, "seq", n_seq, k) for k, m in zip(order, messages, strict=True)]
         attended = merge(parts, heads)
-        shards = [attended] + [lax.ppermute(attended, "seq", toward(k)) for k in range(1, n_seq)]
-        stacked = jnp.stack(shards)
-        projected = jnp.einsum("ktf,fd->ktd", stacked, output_weight, preferred_element_type=F32)
+
+        shards = gather_over_seq(attended)
         head_at = lax.axis_index("head")
-        tile = projected.shape[1:]
         core, side = head_at % 2, head_at // 2
 
-        def shard_of(token_shard):
-            return lax.dynamic_index_in_dim(projected, token_shard ^ here, 0, keepdims=False)
-
-        mine_core = [shard_of(core), shard_of(2 + core)]
-        other_core = jnp.stack([shard_of(1 - core), shard_of(3 - core)]).astype(BF)
-        received = lax.ppermute(other_core, "head", [(i, i ^ 1) for i in range(n_head)])
-        joined = jnp.stack(mine_core) + received.astype(F32)
-        mine = lax.dynamic_index_in_dim(joined, side, 0, keepdims=False)
-        other = lax.dynamic_index_in_dim(joined, 1 - side, 0, keepdims=False).astype(BF)
-        return mine + lax.ppermute(other, "head", [(i, i ^ 2) for i in range(n_head)]).astype(F32)
+        def project(rows):
+            return jnp.dot(rows, output_weight, preferred_element_type=F32)
+
+        def over_cores(pair):
+            first_mine = (here ^ pair[0]) % 2 == core
+            first, second = shards[pair[0]], shards[pair[1]]
+            other = project(jnp.where(first_mine, second, first)).astype(BF)
+            mine = project(jnp.where(first_mine, first, second))
+            return mine + swap(other, "head", n_head, 1).astype(F32)
+
+        near, far = over_cores((0, 1)), over_cores((2, 3))
+        near_mine = here // 2 == side
+        mine, other = jnp.where(near_mine, near, far), jnp.where(near_mine, far, near)
+        return mine + swap(other.astype(BF), "head", n_head, 2).astype(F32)
 
     sent = jnp.concatenate(messages, axis=0)
     got = lax.all_to_all(sent, "seq", 0, 0, tiled=True).reshape(n_seq, own_tokens, -1)

time: 61.6 us -> 56.4 us (0.916); the launches traced: 61 us -> 56.8 us
  local copies, waits for them, and re-layouts: 5.43 us -> 0.12 us
  Pallas kernels: 13.9 us -> 17.4 us
  waiting for transfers between devices: 22.2 us -> 19.2 us
    unnamed x14 -> x10, local copies, waits for them, and re-layouts: 5.32 us -> 0.02 us
    pallas_call x3 -> x6, Pallas kernels: 13.4 us -> 16.9 us  [the longest x4 12 us: attend(): pl.pallas_call(functools.partial(attend_body, (kv, group, tokens, n, at))...]
    ppermute x11 -> x12, waiting for transfers between devices: 22.2 us -> 19.2 us  [swap(): return lax.ppermute(value, axis, [(i, i ^ k) for i in range(size)])]
    another operation x3 -> x0, other arithmetic: 0.88 us -> none  [the longest x1 0.73 us: per_device(): other_core = jnp.stack([shard_of(1 - core), shard_of(3 - core)]).astype(BF)]
    concatenate x0 -> x1, other arithmetic: none -> 0.69 us  [per_device(): jnp.concatenate([block_mask, heading_row[None]])]
    ppermute x11 -> x12, starting transfers between devices: 14.8 us -> 15.2 us  [swap(): return lax.ppermute(value, axis, [(i, i ^ k) for i in range(size)])]
    dot_general x1 -> x4, matrix products: 1.61 us -> 1.93 us  [project(): return jnp.dot(rows, output_weight, preferred_element_type=F32)]
  transfers between devices with their start and end apart: 11 -> 12, of which waited for: 6 -> 6; matrix products, arithmetic and copies ran while one was open for 0% -> 4% of each run, Pallas kernels for 22% -> 30%
where the time goes in v3:
time: 56.4 us; the launch traced here: 56.8 us
  waiting for transfers between devices  19.2 us (34%)
  Pallas kernels  17.4 us (31%)
  starting transfers between devices  15.2 us (27%)
  matrix products  1.93 us (3%)
  between operations  1.48 us (3%)
  other arithmetic  1.44 us (3%)
    ppermute x12, waiting for transfers between devices, swap(): return lax.ppermute(value, axis, [(i, i ^ k) for i in range(size)])  19.2 us
    ppermute x12, starting transfers between devices, swap(): return lax.ppermute(value, axis, [(i, i ^ k) for i in range(size)])  15.2 us
    pallas_call x4, Pallas kernels, attend(): pl.pallas_call(functools.partial(attend_body, (kv, group, tokens, n, at))...  12 us
    pallas_call x1, Pallas kernels, prepare(): pl.pallas_call(functools.partial(prepare_body, rows // BLOCK), in_specs=[...  3.2 us
    dot_general x4, matrix products, project(): return jnp.dot(rows, output_weight, preferred_element_type=F32)  1.93 us
    pallas_call x1, Pallas kernels, make_lists(): pl.pallas_call(functools.partial(list_body, fin_blocks, heading), in_spec...  1.66 us
  transfers between devices with their start and end apart: 12, of which 6 were waited for; matrix products, arithmetic and copies ran while one was open for 4% of the time, Pallas kernels for 30%

profile of v3, /device:TPU:0, one launch (start us, length us, event | category | flops | bytes accessed | tf_op | source)
XLA Modules:
  0.0 56.8 jit_solution(1188764190283969967)
XLA Ops:
  0.0 4.0 %collective-permute-start = (bf16[64,1024]{1,0:T(8,128)(2,1)}, bf16[64,1024]{1,0:T(8,128)(2,1)S(1)}, u32[]{:S(2)}, u32[]{:S(2)}) collective-permute-start(bf16[64,1024]{1,0:T(8,128)(2,1)} %refs_3_.1), channel_id=1, source_target_pairs={{0,8},{4,12},{8,0},{12,4},{1,9},{5,13},{9,1},{13,5},{2,10},{6,14},... | collective-permute-start | bytes 393224 | tf_op jit(solution)/shard_map/ppermute | solution.py:284
  4.0 1.6 %collective-permute-start.4 = (bf16[64,1024]{1,0:T(8,128)(2,1)}, bf16[64,1024]{1,0:T(8,128)(2,1)S(1)}, u32[]{:S(2)}, u32[]{:S(2)}) collective-permute-start(bf16[64,1024]{1,0:T(8,128)(2,1)} %refs_3_.1), channel_id=1, source_target_pairs={{0,4},{4,0},{8,12},{12,8},{1,5},{5,1},{9,13},{13,9},{2,6},{6,2},{1... | collective-permute-start | bytes 393224 | tf_op jit(solution)/shard_map/ppermute | solution.py:284
  7.0 0.7 %pad_add_fusion.meta_ref = s32[3,32]{1,0:T(4,128)S(1)} fusion(s32[1,32]{1,0:T(1,128)S(1)} %pad_bitcast_fusion, s32[2,32]{1,0:T(2,128)} %param.12), kind=kLoop, calls=%fused_computation.14 | loop fusion | flops 96 | bytes 768 | tf_op jit(solution)/shard_map/concatenate | solution.py:297
  7.7 1.7 %lists.1.lists_ref.refs_0_.refs_4_ = s32[4,40]{1,0:T(4,128)S(1)} custom-call(s32[3,32]{1,0:T(4,128)S(1)} %pad_add_fusion.meta_ref), custom_call_target="tpu_custom_call" | custom-call | flops 4294967296 | tf_op jit(solution)/shard_map/lists/pallas_call | solution.py:67
  9.4 1.3 %collective-permute-done.refs_3_ = bf16[64,1024]{1,0:T(8,128)(2,1)S(1)} collective-permute-done((bf16[64,1024]{1,0:T(8,128)(2,1)}, bf16[64,1024]{1,0:T(8,128)(2,1)S(1)}, u32[]{:S(2)}, u32[]{:S(2)}) %collective-permute-start) | collective-permute-done | bytes 131104 | tf_op jit(solution)/shard_map/ppermute | solution.py:284
  10.7 0.7 %collective-permute-start.2 = (bf16[64,1024]{1,0:T(8,128)(2,1)S(1)}, bf16[64,1024]{1,0:T(8,128)(2,1)S(1)}, u32[]{:S(2)}, u32[]{:S(2)}) collective-permute-start(bf16[64,1024]{1,0:T(8,128)(2,1)S(1)} %collective-permute-done.refs_3_), channel_id=1, source_target_pairs={{0,4},{4,0},{8,12},{12,8},{1,5},{5,1},{9,13},{13,9},{2,6},{6,2},{1... | collective-permute-start | bytes 393224 | tf_op jit(solution)/shard_map/ppermute | solution.py:284
  11.4 3.2 %prepare.1 = (bf16[4480,256]{1,0:T(8,128)(2,1)S(1)}, bf16[4480,256]{1,0:T(8,128)(2,1)S(1)}) custom-call(s32[4,40]{1,0:T(4,128)S(1)} %lists.1.lists_ref.refs_0_.refs_4_, bf16[4096,2,256]{2,1,0:T(2,128)(2,1)S(1)} %copy-done.2, bf16[256,2,256]{2,1,0:T(2,128)(2,1)S(1)} %copy-done.3, bf16[64,2,256]{2,1,0:T(2,128)(2,1)S(1)} %copy-done.4), custom_call_target="tpu_custom_call" | custom-call | flops 4294967296 | bytes 12582912 | tf_op jit(solution)/shard_map/prepare/pallas_call | solution.py:107
  14.6 2.9 %attend.4.refs_4_ = bf16[64,1152]{1,0:T(8,128)(2,1)S(1)} custom-call(s32[4,40]{1,0:T(4,128)S(1)} %lists.1.lists_ref.refs_0_.refs_4_, bf16[4480,256]{1,0:T(8,128)(2,1)S(1)} %get-tuple-element.7.refs_1_, bf16[4480,256]{1,0:T(8,128)(2,1)S(1)} %get-tuple-element.8.refs_2_, bf16[64,1024]{1,0:T(8,128)(2,1)S(1)} %collective-permute-done.refs_3_, ...), custom_call_target="tpu_custom_call" | custom-call | flops 603979776 | bytes 4587520 | tf_op jit(solution)/shard_map/attend/pallas_call | solution.py:213
  17.5 2.7 %collective-permute-start.1 = (bf16[64,1152]{1,0:T(8,128)(2,1)S(1)}, bf16[64,1152]{1,0:T(8,128)(2,1)S(1)}, u32[]{:S(2)}, u32[]{:S(2)}) collective-permute-start(bf16[64,1152]{1,0:T(8,128)(2,1)S(1)} %attend.4.refs_4_), channel_id=1, source_target_pairs={{0,8},{4,12},{8,0},{12,4},{1,9},{5,13},{9,1},{13,5},{2,10},{6,14},... | collective-permute-start | bytes 442376 | tf_op jit(solution)/shard_map/ppermute | solution.py:284
  20.2 2.9 %attend.5.refs_4_ = bf16[64,1152]{1,0:T(8,128)(2,1)S(1)} custom-call(s32[4,40]{1,0:T(4,128)S(1)} %lists.1.lists_ref.refs_0_.refs_4_, bf16[4480,256]{1,0:T(8,128)(2,1)S(1)} %get-tuple-element.7.refs_1_, bf16[4480,256]{1,0:T(8,128)(2,1)S(1)} %get-tuple-element.8.refs_2_, bf16[64,1024]{1,0:T(8,128)(2,1)S(1)} %collective-permute-done.2.refs_3_, ...), custom_call_target="tpu_custom_call" | custom-call | flops 603979776 | bytes 4587520 | tf_op jit(solution)/shard_map/attend/pallas_call | solution.py:213
  23.1 3.1 %attend.6.refs_4_ = bf16[64,1152]{1,0:T(8,128)(2,1)S(1)} custom-call(s32[4,40]{1,0:T(4,128)S(1)} %lists.1.lists_ref.refs_0_.refs_4_, bf16[4480,256]{1,0:T(8,128)(2,1)S(1)} %get-tuple-element.7.refs_1_, bf16[4480,256]{1,0:T(8,128)(2,1)S(1)} %get-tuple-element.8.refs_2_, bf16[64,1024]{1,0:T(8,128)(2,1)S(1)} %collective-permute-done.4.refs_3_, ...), custom_call_target="tpu_custom_call" | custom-call | flops 603979776 | bytes 4587520 | tf_op jit(solution)/shard_map/attend/pallas_call | solution.py:213
  26.3 0.7 %collective-permute-start.3 = (bf16[64,1152]{1,0:T(8,128)(2,1)S(1)}, bf16[64,1152]{1,0:T(8,128)(2,1)S(1)}, u32[]{:S(2)}, u32[]{:S(2)}) collective-permute-start(bf16[64,1152]{1,0:T(8,128)(2,1)S(1)} %attend.5.refs_4_), channel_id=1, source_target_pairs={{0,12},{4,8},{8,4},{12,0},{1,13},{5,9},{9,5},{13,1},{2,14},{6,10},... | collective-permute-start | bytes 442376 | tf_op jit(solution)/shard_map/ppermute | solution.py:284
  27.0 3.1 %attend.7.refs_3_ = bf16[64,1152]{1,0:T(8,128)(2,1)S(1)} custom-call(s32[4,40]{1,0:T(4,128)S(1)} %lists.1.lists_ref.refs_0_.refs_4_, bf16[4480,256]{1,0:T(8,128)(2,1)S(1)} %get-tuple-element.7.refs_1_, bf16[4480,256]{1,0:T(8,128)(2,1)S(1)} %get-tuple-element.8.refs_2_, bf16[64,1024]{1,0:T(8,128)(2,1)S(1)} %copy-done.1, bf16[64,1152]{1,0:T(8,128)(2,1)S(1)} %attend.6.refs_4_), custom_call_target="tpu_custom_call" | custom-call | flops 603979776 | bytes 4587520 | tf_op jit(solution)/shard_map/attend/pallas_call | solution.py:213
  30.1 4.6 %collective-permute-done.5.refs_2_ = bf16[64,1152]{1,0:T(8,128)(2,1)S(1)} collective-permute-done((bf16[64,1152]{1,0:T(8,128)(2,1)S(1)}, bf16[64,1152]{1,0:T(8,128)(2,1)S(1)}, u32[]{:S(2)}, u32[]{:S(2)}) %collective-permute-start.5) | collective-permute-done | bytes 147488 | tf_op jit(solution)/shard_map/ppermute | solution.py:284
  34.7 0.5 merge.1
  35.2 1.5 %collective-permute-start.8 = (bf16[64,1024]{1,0:T(8,128)(2,1)S(1)}, bf16[64,1024]{1,0:T(8,128)(2,1)S(1)}, u32[]{:S(2)}, u32[]{:S(2)}) collective-permute-start(bf16[64,1024]{1,0:T(8,128)(2,1)S(1)} %merge.1), channel_id=1, source_target_pairs={{0,8},{4,12},{8,0},{12,4},{1,9},{5,13},{9,1},{13,5},{2,10},{6,14},... | collective-permute-start | bytes 393224 | tf_op jit(solution)/shard_map/ppermute | solution.py:284
  36.7 1.3 %collective-permute-start.6 = (bf16[64,1024]{1,0:T(8,128)(2,1)S(1)}, bf16[64,1024]{1,0:T(8,128)(2,1)S(1)}, u32[]{:S(2)}, u32[]{:S(2)}) collective-permute-start(bf16[64,1024]{1,0:T(8,128)(2,1)S(1)} %merge.1), channel_id=1, source_target_pairs={{0,4},{4,0},{8,12},{12,8},{1,5},{5,1},{9,13},{13,9},{2,6},{6,2},{1... | collective-permute-start | bytes 393224 | tf_op jit(solution)/shard_map/ppermute | solution.py:284
  38.0 5.0 %collective-permute-done.8 = bf16[64,1024]{1,0:T(8,128)(2,1)S(1)} collective-permute-done((bf16[64,1024]{1,0:T(8,128)(2,1)S(1)}, bf16[64,1024]{1,0:T(8,128)(2,1)S(1)}, u32[]{:S(2)}, u32[]{:S(2)}) %collective-permute-start.8) | collective-permute-done | bytes 131104 | tf_op jit(solution)/shard_map/ppermute | solution.py:284
  43.0 0.9 %collective-permute-start.9 = (bf16[64,1024]{1,0:T(8,128)(2,1)S(1)}, bf16[64,1024]{1,0:T(8,128)(2,1)S(1)}, u32[]{:S(2)}, u32[]{:S(2)}) collective-permute-start(bf16[64,1024]{1,0:T(8,128)(2,1)S(1)} %collective-permute-done.8), channel_id=1, source_target_pairs={{0,4},{4,0},{8,12},{12,8},{1,5},{5,1},{9,13},{13,9},{2,6},{6,2},{1... | collective-permute-start | bytes 393224 | tf_op jit(solution)/shard_map/ppermute | solution.py:284
  44.6 3.5 %collective-permute-done.9 = bf16[64,1024]{1,0:T(8,128)(2,1)S(1)} collective-permute-done((bf16[64,1024]{1,0:T(8,128)(2,1)S(1)}, bf16[64,1024]{1,0:T(8,128)(2,1)S(1)}, u32[]{:S(2)}, u32[]{:S(2)}) %collective-permute-start.9) | collective-permute-done | bytes 131104 | tf_op jit(solution)/shard_map/ppermute | solution.py:284
  49.1 0.8 %collective-permute-done.10 = bf16[64,1024]{1,0:T(8,128)(2,1)S(1)} collective-permute-done((bf16[64,1024]{1,0:T(8,128)(2,1)S(1)}, bf16[64,1024]{1,0:T(8,128)(2,1)S(1)}, u32[]{:S(2)}, u32[]{:S(2)}) %collective-permute-start.10) | collective-permute-done | bytes 131104 | tf_op jit(solution)/shard_map/ppermute | solution.py:284
  50.4 1.6 %collective-permute-start.11 = (bf16[64,1024]{1,0:T(8,128)(2,1)S(1)}, bf16[64,1024]{1,0:T(8,128)(2,1)S(1)}, u32[]{:S(2)}, u32[]{:S(2)}) collective-permute-start(bf16[64,1024]{1,0:T(8,128)(2,1)S(1)} %get-tuple-element.9), channel_id=1, source_target_pairs={{0,2},{1,3},{2,0},{3,1},{4,6},{5,7},{6,4},{7,5},{8,10},{9,11},{10,... | collective-permute-start | bytes 393224 | tf_op jit(solution)/shard_map/ppermute | solution.py:284
  52.0 4.1 %collective-permute-done.11 = bf16[64,1024]{1,0:T(8,128)(2,1)S(1)} collective-permute-done((bf16[64,1024]{1,0:T(8,128)(2,1)S(1)}, bf16[64,1024]{1,0:T(8,128)(2,1)S(1)}, u32[]{:S(2)}, u32[]{:S(2)}) %collective-permute-start.11) | collective-permute-done | bytes 131104 | tf_op jit(solution)/shard_map/ppermute | solution.py:284
  56.0 0.8 %convert_add_fusion = f32[64,1024]{1,0:T(8,128)} fusion(bf16[64,1024]{1,0:T(8,128)(2,1)S(1)} %collective-permute-done.11, f32[64,1024]{1,0:T(8,128)S(1)} %convolution_add_fusion.1, f32[64,1024]{1,0:T(8,128)S(1)} %get-tuple-element.10, pred[]{:T(512)S(6)} %eq.16), kind=kLoop, calls=%fused_computation.4 | loop fusion | flops 196608 | bytes 917505 | tf_op jit(solution)/shard_map/add | solution.py:333
  (25 shorter events, 2.3 us)
Async XLA Ops:
  0.0 44.0 %copy-start = (bf16[1024,1024]{1,0:T(8,128)(2,1)S(1)}, bf16[1024,1024]{1,0:T(8,128)(2,1)}, u32[]{:S(2)}) copy-start(bf16[1024,1024]{1,0:T(8,128)(2,1)} %param.15) | copy-start | bytes 6291460
  0.0 10.7 %collective-permute-start = (bf16[64,1024]{1,0:T(8,128)(2,1)}, bf16[64,1024]{1,0:T(8,128)(2,1)S(1)}, u32[]{:S(2)}, u32[]{:S(2)}) collective-permute-start(bf16[64,1024]{1,0:T(8,128)(2,1)} %refs_3_.1), channel_id=1, source_target_pairs={{0,8},{4,12},{8,0},{12,4},{1,9},{5,13},{9,1},{13,5},{2,10},{6,14},... | collective-permute-start | bytes 393224 | tf_op jit(solution)/shard_map/ppermute | solution.py:284
  4.0 19.1 %collective-permute-start.4 = (bf16[64,1024]{1,0:T(8,128)(2,1)}, bf16[64,1024]{1,0:T(8,128)(2,1)S(1)}, u32[]{:S(2)}, u32[]{:S(2)}) collective-permute-start(bf16[64,1024]{1,0:T(8,128)(2,1)} %refs_3_.1), channel_id=1, source_target_pairs={{0,4},{4,0},{8,12},{12,8},{1,5},{5,1},{9,13},{13,9},{2,6},{6,2},{1... | collective-permute-start | bytes 393224 | tf_op jit(solution)/shard_map/ppermute | solution.py:284
  7.7 3.7 %copy-start.2 = (bf16[4096,2,256]{2,1,0:T(2,128)(2,1)S(1)}, bf16[4096,2,256]{2,1,0:T(2,128)(2,1)}, u32[]{:S(2)}) copy-start(bf16[4096,2,256]{2,1,0:T(2,128)(2,1)} %cache_ref.1) | copy-start | bytes 12582916
  7.7 3.7 %copy-start.3 = (bf16[256,2,256]{2,1,0:T(2,128)(2,1)S(1)}, bf16[256,2,256]{2,1,0:T(2,128)(2,1)}, u32[]{:S(2)}) copy-start(bf16[256,2,256]{2,1,0:T(2,128)(2,1)} %fin_ref.1) | copy-start | bytes 786436
  7.7 3.7 %copy-start.4 = (bf16[64,2,256]{2,1,0:T(2,128)(2,1)S(1)}, bf16[64,2,256]{2,1,0:T(2,128)(2,1)}, u32[]{:S(2)}) copy-start(bf16[64,2,256]{2,1,0:T(2,128)(2,1)} %own_ref.1) | copy-start | bytes 196612
  10.7 9.5 %collective-permute-start.2 = (bf16[64,1024]{1,0:T(8,128)(2,1)S(1)}, bf16[64,1024]{1,0:T(8,128)(2,1)S(1)}, u32[]{:S(2)}, u32[]{:S(2)}) collective-permute-start(bf16[64,1024]{1,0:T(8,128)(2,1)S(1)} %collective-permute-done.refs_3_), channel_id=1, source_target_pairs={{0,4},{4,0},{8,12},{12,8},{1,5},{5,1},{9,13},{13,9},{2,6},{6,2},{1... | collective-permute-start | bytes 393224 | tf_op jit(solution)/shard_map/ppermute | solution.py:284
  17.5 12.6 %collective-permute-start.1 = (bf16[64,1152]{1,0:T(8,128)(2,1)S(1)}, bf16[64,1152]{1,0:T(8,128)(2,1)S(1)}, u32[]{:S(2)}, u32[]{:S(2)}) collective-permute-start(bf16[64,1152]{1,0:T(8,128)(2,1)S(1)} %attend.4.refs_4_), channel_id=1, source_target_pairs={{0,8},{4,12},{8,0},{12,4},{1,9},{5,13},{9,1},{13,5},{2,10},{6,14},... | collective-permute-start | bytes 442376 | tf_op jit(solution)/shard_map/ppermute | solution.py:284
  23.1 3.9 %copy-start.1 = (bf16[64,1024]{1,0:T(8,128)(2,1)S(1)}, bf16[64,1024]{1,0:T(8,128)(2,1)}, u32[]{:S(2)}) copy-start(bf16[64,1024]{1,0:T(8,128)(2,1)} %refs_3_.1) | copy-start | bytes 393220
  26.2 8.4 %collective-permute-start.5 = (bf16[64,1152]{1,0:T(8,128)(2,1)S(1)}, bf16[64,1152]{1,0:T(8,128)(2,1)S(1)}, u32[]{:S(2)}, u32[]{:S(2)}) collective-permute-start(bf16[64,1152]{1,0:T(8,128)(2,1)S(1)} %attend.6.refs_4_), channel_id=1, source_target_pairs={{0,4},{4,0},{8,12},{12,8},{1,5},{5,1},{9,13},{13,9},{2,6},{6,2},{1... | collective-permute-start | bytes 442376 | tf_op jit(solution)/shard_map/ppermute | solution.py:284
  26.3 8.4 %collective-permute-start.3 = (bf16[64,1152]{1,0:T(8,128)(2,1)S(1)}, bf16[64,1152]{1,0:T(8,128)(2,1)S(1)}, u32[]{:S(2)}, u32[]{:S(2)}) collective-permute-start(bf16[64,1152]{1,0:T(8,128)(2,1)S(1)} %attend.5.refs_4_), channel_id=1, source_target_pairs={{0,12},{4,8},{8,4},{12,0},{1,13},{5,9},{9,5},{13,1},{2,14},{6,10},... | collective-permute-start | bytes 442376 | tf_op jit(solution)/shard_map/ppermute | solution.py:284
  35.2 7.8 %collective-permute-start.8 = (bf16[64,1024]{1,0:T(8,128)(2,1)S(1)}, bf16[64,1024]{1,0:T(8,128)(2,1)S(1)}, u32[]{:S(2)}, u32[]{:S(2)}) collective-permute-start(bf16[64,1024]{1,0:T(8,128)(2,1)S(1)} %merge.1), channel_id=1, source_target_pairs={{0,8},{4,12},{8,0},{12,4},{1,9},{5,13},{9,1},{13,5},{2,10},{6,14},... | collective-permute-start | bytes 393224 | tf_op jit(solution)/shard_map/ppermute | solution.py:284
  36.7 7.2 %collective-permute-start.6 = (bf16[64,1024]{1,0:T(8,128)(2,1)S(1)}, bf16[64,1024]{1,0:T(8,128)(2,1)S(1)}, u32[]{:S(2)}, u32[]{:S(2)}) collective-permute-start(bf16[64,1024]{1,0:T(8,128)(2,1)S(1)} %merge.1), channel_id=1, source_target_pairs={{0,4},{4,0},{8,12},{12,8},{1,5},{5,1},{9,13},{13,9},{2,6},{6,2},{1... | collective-permute-start | bytes 393224 | tf_op jit(solution)/shard_map/ppermute | solution.py:284
  43.0 5.0 %collective-permute-start.9 = (bf16[64,1024]{1,0:T(8,128)(2,1)S(1)}, bf16[64,1024]{1,0:T(8,128)(2,1)S(1)}, u32[]{:S(2)}, u32[]{:S(2)}) collective-permute-start(bf16[64,1024]{1,0:T(8,128)(2,1)S(1)} %collective-permute-done.8), channel_id=1, source_target_pairs={{0,4},{4,0},{8,12},{12,8},{1,5},{5,1},{9,13},{13,9},{2,6},{6,2},{1... | collective-permute-start | bytes 393224 | tf_op jit(solution)/shard_map/ppermute | solution.py:284
  44.5 4.1 %collective-permute-start.7 = (bf16[64,1024]{1,0:T(8,128)(2,1)S(1)}, bf16[64,1024]{1,0:T(8,128)(2,1)S(1)}, u32[]{:S(2)}, u32[]{:S(2)}) collective-permute-start(bf16[64,1024]{1,0:T(8,128)(2,1)S(1)} %convolution_convert_fusion.1), channel_id=1, source_target_pairs={{0,1},{1,0},{2,3},{3,2},{4,5},{5,4},{6,7},{7,6},{8,9},{9,8},{10,11... | collective-permute-start | bytes 393224 | tf_op jit(solution)/shard_map/ppermute | solution.py:284
  48.5 1.4 %collective-permute-start.10 = (bf16[64,1024]{1,0:T(8,128)(2,1)S(1)}, bf16[64,1024]{1,0:T(8,128)(2,1)S(1)}, u32[]{:S(2)}, u32[]{:S(2)}) collective-permute-start(bf16[64,1024]{1,0:T(8,128)(2,1)S(1)} %convolution_convert_fusion), channel_id=1, source_target_pairs={{0,1},{1,0},{2,3},{3,2},{4,5},{5,4},{6,7},{7,6},{8,9},{9,8},{10,11... | collective-permute-start | bytes 393224 | tf_op jit(solution)/shard_map/ppermute | solution.py:284
  50.4 5.6 %collective-permute-start.11 = (bf16[64,1024]{1,0:T(8,128)(2,1)S(1)}, bf16[64,1024]{1,0:T(8,128)(2,1)S(1)}, u32[]{:S(2)}, u32[]{:S(2)}) collective-permute-start(bf16[64,1024]{1,0:T(8,128)(2,1)S(1)} %get-tuple-element.9), channel_id=1, source_target_pairs={{0,2},{1,3},{2,0},{3,1},{4,6},{5,7},{6,4},{7,5},{8,10},{9,11},{10,... | collective-permute-start | bytes 393224 | tf_op jit(solution)/shard_map/ppermute | solution.py:284

commit v4 on v3

--- a/solution.py
+++ b/solution.py
@@ -34,38 +34,35 @@
     return pl.BlockSpec(memory_space=pltpu.SMEM)
 
 
-def list_body(fin_blocks, heading, meta_ref, lists_ref):
-    query_blocks, ctx_blocks = meta_ref.shape[0] - 1, meta_ref.shape[1]
-    end = lists_ref.shape[1] - 1
-    own_block = ctx_blocks + fin_blocks
+def list_body(axis, own_tokens, shards, fin_blocks, meta_ref, lists_ref):
+    here = lax.axis_index(axis)
+    ctx_blocks = meta_ref.shape[1]
+    owner, valid = meta_ref[meta_ref.shape[0] - 2, 0], meta_ref[meta_ref.shape[0] - 1, 0]
+    end = lists_ref.shape[1] - 3
+    blocks = [((here ^ k) * own_tokens) // BLOCK if here_is_first else k for here_is_first, k in shards]
 
     def note(i, counts):
-        bits = [meta_ref[q, i] for q in range(query_blocks)]
-        bits.append(functools.reduce(lambda x, y: x | y, bits))
-        for q, count in enumerate(counts):
-            lists_ref[q, count] = i
-        return tuple(count + jnp.where(bit > 0, 1, 0) for count, bit in zip(counts, bits, strict=True))
-
-    counts = lax.fori_loop(0, ctx_blocks, note, (jnp.int32(0),) * (query_blocks + 1))
-    for q, count in enumerate(counts[:-1]):
-        for i in range(fin_blocks):
-            lists_ref[q, count] = ctx_blocks + i
-            count = count + meta_ref[query_blocks, 0]
-        lists_ref[q, count] = own_block
-        lists_ref[q, count + 1] = own_block
-        lists_ref[q, end] = count
-    for i in range(UNROLL - 1):
-        lists_ref[query_blocks, counts[-1] + i] = ctx_blocks - 1
-    lists_ref[query_blocks, end] = counts[-1]
-    for i in range(heading):
-        lists_ref[query_blocks + 1, i] = meta_ref[query_blocks, i]
-
-
-def make_lists(meta, fin_blocks, heading):
-    query_blocks, ctx_blocks = meta.shape[0] - 1, meta.shape[1]
-    shape = (query_blocks + 2, ctx_blocks + fin_blocks + UNROLL + 2)
+        for at, count in enumerate(counts):
+            lists_ref[at, count] = i
+        return tuple(
+            count + jnp.where(meta_ref[block, i] > 0, 1, 0) for count, block in zip(counts, blocks, strict=True)
+        )
+
+    counts = lax.fori_loop(0, ctx_blocks, note, (jnp.int32(0),) * len(blocks))
+    for at, count in enumerate(counts):
+        for i in range(UNROLL - 1):
+            lists_ref[at, count + i] = ctx_blocks - 1
+        lists_ref[at, end] = count
+        lists_ref[at, end + 1] = jnp.where(here == owner, 1, 0)
+        lists_ref[at, end + 2] = jnp.clip(valid - here * own_tokens, 0, own_tokens)
+
+
+def make_lists(mask, owner, count, axis, own_tokens, shards, fin_blocks):
+    shape = (len(shards), mask.shape[1] + UNROLL + 3)
+    rows = [jnp.pad(x[None], ((0, 0), (0, mask.shape[1] - 1))) for x in (owner, count)]
+    meta = jnp.concatenate([mask] + rows)
     return pl.pallas_call(
-        functools.partial(list_body, fin_blocks, heading),
+        functools.partial(list_body, axis, own_tokens, shards, fin_blocks),
         in_specs=[smem_spec()],
         out_specs=smem_spec(),
         out_shape=jax.ShapeDtypeStruct(shape, jnp.int32),
@@ -75,57 +72,70 @@
     )(meta)
 
 
-def prepare_body(ctx_blocks, lists_ref, cache_ref, fin_ref, own_ref, keys_ref, values_ref):
+def prepare_body(at, lists_ref, cache_ref, fin_ref, own_ref, *refs):
+    keys_ref, values_ref, info_ref = refs[-3:]
     width = keys_ref.shape[1]
-    any_row, end = lists_ref.shape[0] - 2, lists_ref.shape[1] - 1
+    end = lists_ref.shape[1] - 3
+    count, is_owner, limit = lists_ref[at, end], lists_ref[at, end + 1], lists_ref[at, end + 2]
     row = lax.broadcasted_iota(jnp.int32, (2 * BLOCK, 2 * BLOCK), 0)
     col = lax.broadcasted_iota(jnp.int32, (2 * BLOCK, 2 * BLOCK), 1)
     source = jnp.where(row < BLOCK, 2 * row, 2 * row - 2 * BLOCK + 1)
     pick = jnp.where(col == source, 1.0, 0.0).astype(BF)
 
-    def take_apart(pairs, start):
+    def take_apart(pairs, to):
         parts = jnp.dot(pick, pairs.reshape(2 * BLOCK, width), preferred_element_type=F32).astype(BF)
-        keys_ref[pl.ds(start, BLOCK)] = parts[:BLOCK]
-        values_ref[pl.ds(start, BLOCK)] = parts[BLOCK:]
-
-    @pl.loop(0, (lists_ref[any_row, end] + UNROLL - 1) // UNROLL)
+        rows = pl.ds(pl.multiple_of(to * BLOCK, BLOCK), BLOCK)
+        keys_ref[rows] = parts[:BLOCK]
+        values_ref[rows] = parts[BLOCK:]
+
+    @pl.loop(0, (count + UNROLL - 1) // UNROLL)
     def _(j):
         for i in range(UNROLL):
-            start = pl.multiple_of(lists_ref[any_row, j * UNROLL + i] * BLOCK, BLOCK)
-            take_apart(cache_ref[pl.ds(start, BLOCK)], start)
+            start = pl.multiple_of(lists_ref[at, j * UNROLL + i] * BLOCK, BLOCK)
+            take_apart(cache_ref[pl.ds(start, BLOCK)], j * UNROLL + i)
 
     fin_blocks, own_rows = fin_ref.shape[0] // BLOCK, own_ref.shape[0]
-    for i in range(fin_blocks):
-        take_apart(fin_ref[i * BLOCK : (i + 1) * BLOCK], (ctx_blocks + i) * BLOCK)
+
+    @pl.when(is_owner > 0)
+    def _():
+        for i in range(fin_blocks):
+            take_apart(fin_ref[i * BLOCK : (i + 1) * BLOCK], count + i)
+
+    full = count + is_owner * fin_blocks
     filler = jnp.zeros((BLOCK - own_rows, 2, width), BF)
-    take_apart(jnp.concatenate([own_ref[...], filler], axis=0), (ctx_blocks + fin_blocks) * BLOCK)
-
-
-def prepare(lists, cache, finished, own):
+    take_apart(jnp.concatenate([own_ref[...], filler], axis=0), full)
+    unread = pl.ds(pl.multiple_of((full + 1) * BLOCK, BLOCK), BLOCK)
+    keys_ref[unread] = jnp.zeros((BLOCK, width), BF)
+    values_ref[unread] = jnp.zeros((BLOCK, width), BF)
+
+    pairs = (full + 2) // 2
+    lane = lax.broadcasted_iota(jnp.int32, (8, 2 * BLOCK), 1)
+    edge = jnp.where(full % 2 == 0, limit, BLOCK + limit)
+    info_ref[:8] = jnp.zeros((8, 2 * BLOCK), F32) + pairs.astype(F32)
+    info_ref[8:] = jnp.where(lane < edge, 0.0, FLOOR)
+
+
+def prepare(at, lists, cache, finished, own, after):
     rows, _, width = cache.shape
-    total = rows + finished.shape[0] + BLOCK
+    total = rows + finished.shape[0] + UNROLL * BLOCK
     return pl.pallas_call(
-        functools.partial(prepare_body, rows // BLOCK),
-        in_specs=[smem_spec(), vmem_spec(), vmem_spec(), vmem_spec()],
-        out_specs=[vmem_spec(), vmem_spec()],
-        out_shape=[jax.ShapeDtypeStruct((total, width), BF)] * 2,
+        functools.partial(prepare_body, at),
+        in_specs=[smem_spec(), vmem_spec(), vmem_spec(), vmem_spec()] + [pl.BlockSpec(memory_space=pl.ANY)] * len(after),
+        out_specs=[vmem_spec()] * 3,
+        out_shape=[jax.ShapeDtypeStruct((total, width), BF)] * 2 + [jax.ShapeDtypeStruct((16, 2 * BLOCK), F32)],
         cost_estimate=pl.CostEstimate(flops=4 * 1024**3, bytes_accessed=12 * 1024**2, transcendentals=0),
         compiler_params=params(),
         name="prepare",
-    )(lists, cache, finished, own)
+    )(lists, cache, finished, own, *after)
 
 
 def attend_body(geometry, *refs):
-    kv, group, tokens, n, at = geometry
-    lists_ref, keys_ref, values_ref = refs[:3]
+    kv, group, tokens, n = geometry
+    info_ref, keys_ref, values_ref = refs[:3]
     query_refs, message_refs = refs[3 : 3 + n], refs[4 + n : 4 + 2 * n]
     scores, peaks, totals, sums = refs[4 + 2 * n :]
     rows = n * group * tokens
-    heading = lists_ref.shape[0] - 1
-    limit, query_block = lists_ref[heading, 1], lists_ref[heading, 2 + at]
-    full = lists_ref[query_block, lists_ref.shape[1] - 1]
-    pairs = (full + 2) // 2
-    lane = lax.broadcasted_iota(jnp.int32, (1, 2 * BLOCK), 1)
+    pairs = jnp.max(info_ref[:8, :LANES]).astype(jnp.int32)
     stat_lane = lax.broadcasted_iota(jnp.int32, (1, LANES), 1)
 
     def cols(h):
@@ -137,10 +147,7 @@
     ]
 
     def block_rows(ref, j, g, count):
-        parts = [
-            ref[pl.ds(pl.multiple_of(lists_ref[query_block, 2 * j + i] * BLOCK, BLOCK), BLOCK), cols(g)] for i in range(2 * count)
-        ]
-        return jnp.concatenate(parts, axis=0)
+        return ref[pl.ds(pl.multiple_of(2 * BLOCK * j, 2 * BLOCK), 2 * BLOCK * count), cols(g)]
 
     def score(j, count, masked):
         for g in range(kv):
@@ -150,10 +157,7 @@
                     queries[g], block_rows(keys_ref, j + i, g, 1), (((1,), (1,)), ((), ())), preferred_element_type=F32
                 )
                 if masked:
-                    bound = jnp.where(2 * j < full, BLOCK, limit)
-                    bound_next = jnp.where(2 * j + 1 == full, limit, 0)
-                    edge = jnp.where(lane < BLOCK, bound, BLOCK + bound_next)
-                    s = s + jnp.where(lane < edge, 0.0, FLOOR)
+                    s = s + info_ref[8:9]
                 scores[j + i, g] = s
                 top = jnp.maximum(top, jnp.maximum(s[:, :BLOCK], s[:, BLOCK:]))
             peaks[g] = top
@@ -204,15 +208,16 @@
         message_refs[r][:, kv * group * HD :] = stats[r].astype(BF)
 
 
-def attend(lists, keys, values, queries, after, kv, at):
+def attend(prepared, queries, after, kv):
     tokens, width = queries[0].shape
     n = len(queries)
     group = width // (kv * HD)
-    slots = keys.shape[0] // BLOCK + 1
+    keys, values, info = prepared
+    slots = keys.shape[0] // BLOCK
     rows = n * group * tokens
     return pl.pallas_call(
-        functools.partial(attend_body, (kv, group, tokens, n, at)),
-        in_specs=[smem_spec()] + [vmem_spec()] * (2 + n) + [pl.BlockSpec(memory_space=pl.ANY)],
+        functools.partial(attend_body, (kv, group, tokens, n)),
+        in_specs=[vmem_spec()] * (3 + n) + [pl.BlockSpec(memory_space=pl.ANY)],
         out_specs=[vmem_spec()] * n,
         out_shape=[jax.ShapeDtypeStruct((tokens, width + LANES), BF)] * n,
         scratch_shapes=[
@@ -221,14 +226,10 @@
             pltpu.VMEM((kv, rows, LANES), F32),
             pltpu.VMEM((kv, rows, HD), F32),
         ],
-        cost_estimate=pl.CostEstimate(
-            flops=4 * rows * kv * HD * BLOCK * slots // 2,
-            bytes_accessed=2 * keys.size * 2,
-            transcendentals=rows * kv * BLOCK * slots // 2,
-        ),
+        cost_estimate=pl.CostEstimate(flops=64 * 1024**2, bytes_accessed=0, transcendentals=0),
         compiler_params=params(),
         name="attend",
-    )(lists, keys, values, *queries, after)
+    )(info, keys, values, *queries, after)
 
 
 def merge_body(heads, *refs):
@@ -277,43 +278,46 @@
     fin_blocks = finished_memory.shape[0] // BLOCK
     direct = n_seq == 4 and n_head == 4 and BLOCK == 2 * own_tokens
 
-    is_owner = (here == owner_index[0]).astype(jnp.int32)
-    limit = jnp.clip(valid_count[0] - here * own_tokens, 0, own_tokens)
-
     def swap(value, axis, size, k):
         return lax.ppermute(value, axis, [(i, i ^ k) for i in range(size)])
 
-    def gather_over_seq(value):
+    def gather_over_seq(value, between=lambda: None):
         near, far = swap(value, "seq", n_seq, 1), swap(value, "seq", n_seq, 2)
-        return [value, near, far, swap(far, "seq", n_seq, 1)]
+        made = between()
+        if made is not None:
+            far, made = lax.optimization_barrier((far, made))
+        return [value, near, far, swap(far, "seq", n_seq, 1)], made
 
     if direct:
-        batches = ((2,), (3,), (1,), (0,))
-        query_blocks = [((here ^ batch[0]) * own_tokens) // BLOCK for batch in batches]
+        shards = [(True, 2), (True, 0)]
+        order = [2, 3, 1, 0]
     else:
-        query_blocks = list(range(own_tokens * n_seq // BLOCK))
-    heading = jnp.stack([jnp.asarray(x, jnp.int32) for x in [is_owner, limit] + query_blocks])
-    heading_row = jnp.pad(heading, (0, block_mask.shape[1] - heading.shape[0]))
-    lists = make_lists(jnp.concatenate([block_mask, heading_row[None]]), fin_blocks, heading.shape[0])
+        shards = [(False, i) for i in range(own_tokens * n_seq // BLOCK)]
+    lists = make_lists(block_mask, owner_index, valid_count, "seq", own_tokens, shards, fin_blocks)
+
+    def prepare_for(at, after):
+        return prepare(at, lists, cache_memory, finished_memory, segment_memory, after)
 
     if direct:
-        order = [k for batch in batches for k in batch]
-        arrived = gather_over_seq(segment_query)
-        queries = [[arrived[k] for k in batch] for batch in batches]
+        arrived, prepared = gather_over_seq(segment_query, lambda: prepare_for(0, []))
+        batches = [[[arrived[k]] for k in order[:2]], [[arrived[k]] for k in order[2:]]]
     else:
         gathered = lax.all_gather(segment_query, "seq", axis=0, tiled=True)
-        queries = [[gathered[i * BLOCK : (i + 1) * BLOCK]] for i in query_blocks]
-
-    keys, values = prepare(lists, cache_memory, finished_memory, segment_memory)
-    messages = []
-    for at, batch in enumerate(queries):
-        messages += attend(lists, keys, values, batch, messages[-1] if messages else lists, kv, at)
+        batches = [[[gathered[i * BLOCK : (i + 1) * BLOCK]]] for _, i in shards]
+        prepared = prepare_for(0, [])
+
+    messages, last = [], lists
+    for at, of_block in enumerate(batches):
+        prepared = prepared if at == 0 else prepare_for(at, [last] + of_block[0])
+        for batch in of_block:
+            messages += attend(prepared, batch, last, kv)
+            last = messages[-1]
 
     if direct:
         parts = [m if k == 0 else swap(m, "seq", n_seq, k) for k, m in zip(order, messages, strict=True)]
-        attended = merge(parts, heads)
-
-        shards = gather_over_seq(attended)
+        attended = merge([parts[i] for i in [3, 1, 0, 2]], heads)
+
+        shards, _ = gather_over_seq(attended)
         head_at = lax.axis_index("head")
         core, side = head_at % 2, head_at // 2
 

time: 56.4 us -> 53.8 us (0.954); the launches traced: 56.8 us -> 53.4 us
  Pallas kernels: 17.4 us -> 13.7 us
  waiting for transfers between devices: 19.2 us -> 17.3 us
  starting transfers between devices: 15.2 us -> 16.9 us
    pallas_call x6 -> x7, Pallas kernels: 16.9 us -> 13.2 us  [the longest x4 7.73 us: attend(): pl.pallas_call(functools.partial(attend_body, (kv, group, tokens, n)), in...]
    ppermute x12, waiting for transfers between devices: 19.2 us -> 17.3 us  [swap(): return lax.ppermute(value, axis, [(i, i ^ k) for i in range(size)])]
    ppermute x12, starting transfers between devices: 15.2 us -> 16.9 us  [swap(): return lax.ppermute(value, axis, [(i, i ^ k) for i in range(size)])]
    unnamed x10, local copies, waits for them, and re-layouts: 0.02 us -> 0.6 us
  transfers between devices with their start and end apart: 12 -> 12, of which waited for: 6 -> 7; matrix products, arithmetic and copies ran while one was open for 4% -> 4% of each run, Pallas kernels for 30% -> 25%
where the time goes in v4:
time: 53.8 us; the launch traced here: 53.4 us
  waiting for transfers between devices  17.3 us (32%)
  starting transfers between devices  16.9 us (31%)
  Pallas kernels  13.7 us (25%)
  matrix products  1.93 us (4%)
  between operations  1.46 us (3%)
  other arithmetic  1.44 us (3%)
  local copies, waits for them, and re-layouts  0.6 us (1%)
    ppermute x12, waiting for transfers between devices, swap(): return lax.ppermute(value, axis, [(i, i ^ k) for i in range(size)])  17.3 us
    ppermute x12, starting transfers between devices, swap(): return lax.ppermute(value, axis, [(i, i ^ k) for i in range(size)])  16.9 us
    pallas_call x4, Pallas kernels, attend(): pl.pallas_call(functools.partial(attend_body, (kv, group, tokens, n)), in...  7.73 us
    pallas_call x2, Pallas kernels, prepare(): pl.pallas_call(functools.partial(prepare_body, at), in_specs=[smem_spec()...  3.86 us
    dot_general x4, matrix products, project(): return jnp.dot(rows, output_weight, preferred_element_type=F32)  1.93 us
    pallas_call x1, Pallas kernels, make_lists(): pl.pallas_call(functools.partial(list_body, axis, own_tokens, shards, fin...  1.6 us
  transfers between devices with their start and end apart: 12, of which 7 were waited for; matrix products, arithmetic and copies ran while one was open for 4% of the time, Pallas kernels for 25%

profile of v4, /device:TPU:0, one launch (start us, length us, event | category | flops | bytes accessed | tf_op | source)
XLA Modules:
  0.0 53.4 jit_solution(10961865277857855364)
XLA Ops:
  0.0 4.0 %collective-permute-start = (bf16[64,1024]{1,0:T(8,128)(2,1)}, bf16[64,1024]{1,0:T(8,128)(2,1)S(1)}, u32[]{:S(2)}, u32[]{:S(2)}) collective-permute-start(bf16[64,1024]{1,0:T(8,128)(2,1)} %refs_3_.1), channel_id=1, source_target_pairs={{0,8},{4,12},{8,0},{12,4},{1,9},{5,13},{9,1},{13,5},{2,10},{6,14},... | collective-permute-start | bytes 393224 | tf_op jit(solution)/shard_map/ppermute | solution.py:282
  5.3 0.7 %pad_add_fusion.meta_ref = s32[4,32]{1,0:T(4,128)S(1)} fusion(s32[1,1]{1,0:T(1,128)} %bitcast.7, s32[1,1]{1,0:T(1,128)} %bitcast.6, s32[2,32]{1,0:T(2,128)} %param.12), kind=kLoop, calls=%fused_computation.14 | loop fusion | flops 256 | bytes 776 | tf_op jit(solution)/shard_map/concatenate | solution.py:63
  6.0 1.6 %lists.1.lists_ref.refs_4_ = s32[2,39]{1,0:T(2,128)S(1)} custom-call(s32[4,32]{1,0:T(4,128)S(1)} %pad_add_fusion.meta_ref), custom_call_target="tpu_custom_call" | custom-call | flops 4294967296 | tf_op jit(solution)/shard_map/lists/pallas_call | solution.py:64
  7.7 0.6 %copy-done.2 = bf16[4096,2,256]{2,1,0:T(2,128)(2,1)S(1)} copy-done((bf16[4096,2,256]{2,1,0:T(2,128)(2,1)S(1)}, bf16[4096,2,256]{2,1,0:T(2,128)(2,1)}, u32[]{:S(2)}) %copy-start.2) | copy-done | bytes 4194328
  8.2 1.9 %prepare.2 = (bf16[4864,256]{1,0:T(8,128)(2,1)S(1)}, bf16[4864,256]{1,0:T(8,128)(2,1)S(1)}, f32[16,256]{1,0:T(8,128)S(1)}) custom-call(s32[2,39]{1,0:T(2,128)S(1)} %lists.1.lists_ref.refs_4_, bf16[4096,2,256]{2,1,0:T(2,128)(2,1)S(1)} %copy-done.2, bf16[256,2,256]{2,1,0:T(2,128)(2,1)S(1)} %copy-done.3, bf16[64,2,256]{2,1,0:T(2,128)(2,1)S(1)} %copy-done.4), custom_call_target="tpu_custom_call" | custom-call | flops 4294967296 | bytes 12582912 | tf_op jit(solution)/shard_map/prepare/pallas_call | solution.py:121
  10.6 1.3 %collective-permute-start.1 = (bf16[64,1024]{1,0:T(8,128)(2,1)S(1)}, bf16[64,1024]{1,0:T(8,128)(2,1)S(1)}, u32[]{:S(2)}, u32[]{:S(2)}) collective-permute-start(bf16[64,1024]{1,0:T(8,128)(2,1)S(1)} %collective-permute-done.refs_3_), channel_id=1, source_target_pairs={{0,4},{4,0},{8,12},{12,8},{1,5},{5,1},{9,13},{13,9},{2,6},{6,2},{1... | collective-permute-start | bytes 393224 | tf_op jit(solution)/shard_map/ppermute | solution.py:282
  11.8 0.7 %collective-permute-start.2 = (bf16[64,1024]{1,0:T(8,128)(2,1)S(1)}, bf16[64,1024]{1,0:T(8,128)(2,1)S(1)}, u32[]{:S(2)}, u32[]{:S(2)}) collective-permute-start(bf16[64,1024]{1,0:T(8,128)(2,1)S(1)} %copy-done.1), channel_id=1, source_target_pairs={{0,4},{4,0},{8,12},{12,8},{1,5},{5,1},{9,13},{13,9},{2,6},{6,2},{1... | collective-permute-start | bytes 393224 | tf_op jit(solution)/shard_map/ppermute | solution.py:282
  12.6 2.1 %attend.4.refs_4_ = bf16[64,1152]{1,0:T(8,128)(2,1)S(1)} custom-call(f32[16,256]{1,0:T(8,128)S(1)} %get-tuple-element.18.refs_0_, bf16[4864,256]{1,0:T(8,128)(2,1)S(1)} %get-tuple-element.19.refs_1_, bf16[4864,256]{1,0:T(8,128)(2,1)S(1)} %get-tuple-element.20.refs_2_, bf16[64,1024]{1,0:T(8,128)(2,1)S(1)} %collective-permute-done.refs_3_, ...), custom_call_target="tpu_custom_call" | custom-call | flops 67108864 | tf_op jit(solution)/shard_map/attend/pallas_call | solution.py:218
  14.7 1.9 %collective-permute-start.4 = (bf16[64,1152]{1,0:T(8,128)(2,1)S(1)}, bf16[64,1152]{1,0:T(8,128)(2,1)S(1)}, u32[]{:S(2)}, u32[]{:S(2)}) collective-permute-start(bf16[64,1152]{1,0:T(8,128)(2,1)S(1)} %attend.4.refs_4_), channel_id=1, source_target_pairs={{0,8},{4,12},{8,0},{12,4},{1,9},{5,13},{9,1},{13,5},{2,10},{6,14},... | collective-permute-start | bytes 442376 | tf_op jit(solution)/shard_map/ppermute | solution.py:282
  16.6 2.1 %attend.5.refs_0_.refs_4_ = bf16[64,1152]{1,0:T(8,128)(2,1)S(1)} custom-call(f32[16,256]{1,0:T(8,128)S(1)} %get-tuple-element.18.refs_0_, bf16[4864,256]{1,0:T(8,128)(2,1)S(1)} %get-tuple-element.19.refs_1_, bf16[4864,256]{1,0:T(8,128)(2,1)S(1)} %get-tuple-element.20.refs_2_, bf16[64,1024]{1,0:T(8,128)(2,1)S(1)} %collective-permute-done.1.refs_3_, ...), custom_call_target="tpu_custom_call" | custom-call | flops 67108864 | tf_op jit(solution)/shard_map/attend/pallas_call | solution.py:218
  18.7 4.2 %collective-permute-start.3 = (bf16[64,1152]{1,0:T(8,128)(2,1)S(1)}, bf16[64,1152]{1,0:T(8,128)(2,1)S(1)}, u32[]{:S(2)}, u32[]{:S(2)}) collective-permute-start(bf16[64,1152]{1,0:T(8,128)(2,1)S(1)} %attend.5.refs_0_.refs_4_), channel_id=1, source_target_pairs={{0,12},{4,8},{8,4},{12,0},{1,13},{5,9},{9,5},{13,1},{2,14},{6,10},... | collective-permute-start | bytes 442376 | tf_op jit(solution)/shard_map/ppermute | solution.py:282
  22.9 1.9 %prepare.3 = (bf16[4864,256]{1,0:T(8,128)(2,1)S(1)}, bf16[4864,256]{1,0:T(8,128)(2,1)S(1)}, f32[16,256]{1,0:T(8,128)S(1)}) custom-call(s32[2,39]{1,0:T(2,128)S(1)} %lists.1.lists_ref.refs_4_, bf16[4096,2,256]{2,1,0:T(2,128)(2,1)S(1)} %copy-done.2, bf16[256,2,256]{2,1,0:T(2,128)(2,1)S(1)} %copy-done.3, bf16[64,2,256]{2,1,0:T(2,128)(2,1)S(1)} %copy-done.4, ...), custom_call_target="tpu_custom_call" | custom-call | flops 4294967296 | bytes 12582912 | tf_op jit(solution)/shard_map/prepare/pallas_call | solution.py:121
  24.8 1.8 %attend.6.refs_4_ = bf16[64,1152]{1,0:T(8,128)(2,1)S(1)} custom-call(f32[16,256]{1,0:T(8,128)S(1)} %get-tuple-element.22.refs_0_, bf16[4864,256]{1,0:T(8,128)(2,1)S(1)} %get-tuple-element.23.refs_1_, bf16[4864,256]{1,0:T(8,128)(2,1)S(1)} %get-tuple-element.24.refs_2_, bf16[64,1024]{1,0:T(8,128)(2,1)S(1)} %collective-permute-done.2.refs_1_.refs_3_, ...), custom_call_target="tpu_custom_call" | custom-call | flops 67108864 | tf_op jit(solution)/shard_map/attend/pallas_call | solution.py:218
  26.7 1.8 %attend.7.refs_0_ = bf16[64,1152]{1,0:T(8,128)(2,1)S(1)} custom-call(f32[16,256]{1,0:T(8,128)S(1)} %get-tuple-element.22.refs_0_, bf16[4864,256]{1,0:T(8,128)(2,1)S(1)} %get-tuple-element.23.refs_1_, bf16[4864,256]{1,0:T(8,128)(2,1)S(1)} %get-tuple-element.24.refs_2_, bf16[64,1024]{1,0:T(8,128)(2,1)S(1)} %copy-done.1, bf16[64,1152]{1,0:T(8,128)(2,1)S(1)} %attend.6.refs_4_), custom_call_target="tpu_custom_call" | custom-call | flops 67108864 | tf_op jit(solution)/shard_map/attend/pallas_call | solution.py:218
  28.5 3.3 %collective-permute-done.5.refs_3_ = bf16[64,1152]{1,0:T(8,128)(2,1)S(1)} collective-permute-done((bf16[64,1152]{1,0:T(8,128)(2,1)S(1)}, bf16[64,1152]{1,0:T(8,128)(2,1)S(1)}, u32[]{:S(2)}, u32[]{:S(2)}) %collective-permute-start.5) | collective-permute-done | bytes 147488 | tf_op jit(solution)/shard_map/ppermute | solution.py:282
  31.8 0.5 merge.1
  32.3 1.1 %collective-permute-start.8 = (bf16[64,1024]{1,0:T(8,128)(2,1)S(1)}, bf16[64,1024]{1,0:T(8,128)(2,1)S(1)}, u32[]{:S(2)}, u32[]{:S(2)}) collective-permute-start(bf16[64,1024]{1,0:T(8,128)(2,1)S(1)} %merge.1), channel_id=1, source_target_pairs={{0,8},{4,12},{8,0},{12,4},{1,9},{5,13},{9,1},{13,5},{2,10},{6,14},... | collective-permute-start | bytes 393224 | tf_op jit(solution)/shard_map/ppermute | solution.py:282
  33.5 1.5 %collective-permute-start.6 = (bf16[64,1024]{1,0:T(8,128)(2,1)S(1)}, bf16[64,1024]{1,0:T(8,128)(2,1)S(1)}, u32[]{:S(2)}, u32[]{:S(2)}) collective-permute-start(bf16[64,1024]{1,0:T(8,128)(2,1)S(1)} %merge.1), channel_id=1, source_target_pairs={{0,4},{4,0},{8,12},{12,8},{1,5},{5,1},{9,13},{13,9},{2,6},{6,2},{1... | collective-permute-start | bytes 393224 | tf_op jit(solution)/shard_map/ppermute | solution.py:282
  34.9 4.7 %collective-permute-done.8 = bf16[64,1024]{1,0:T(8,128)(2,1)S(1)} collective-permute-done((bf16[64,1024]{1,0:T(8,128)(2,1)S(1)}, bf16[64,1024]{1,0:T(8,128)(2,1)S(1)}, u32[]{:S(2)}, u32[]{:S(2)}) %collective-permute-start.8) | collective-permute-done | bytes 131104 | tf_op jit(solution)/shard_map/ppermute | solution.py:282
  40.8 3.8 %collective-permute-done.9 = bf16[64,1024]{1,0:T(8,128)(2,1)S(1)} collective-permute-done((bf16[64,1024]{1,0:T(8,128)(2,1)S(1)}, bf16[64,1024]{1,0:T(8,128)(2,1)S(1)}, u32[]{:S(2)}, u32[]{:S(2)}) %collective-permute-start.9) | collective-permute-done | bytes 131104 | tf_op jit(solution)/shard_map/ppermute | solution.py:282
  45.7 0.8 %collective-permute-done.10 = bf16[64,1024]{1,0:T(8,128)(2,1)S(1)} collective-permute-done((bf16[64,1024]{1,0:T(8,128)(2,1)S(1)}, bf16[64,1024]{1,0:T(8,128)(2,1)S(1)}, u32[]{:S(2)}, u32[]{:S(2)}) %collective-permute-start.10) | collective-permute-done | bytes 131104 | tf_op jit(solution)/shard_map/ppermute | solution.py:282
  47.0 1.6 %collective-permute-start.11 = (bf16[64,1024]{1,0:T(8,128)(2,1)S(1)}, bf16[64,1024]{1,0:T(8,128)(2,1)S(1)}, u32[]{:S(2)}, u32[]{:S(2)}) collective-permute-start(bf16[64,1024]{1,0:T(8,128)(2,1)S(1)} %get-tuple-element.25), channel_id=1, source_target_pairs={{0,2},{1,3},{2,0},{3,1},{4,6},{5,7},{6,4},{7,5},{8,10},{9,11},{10,... | collective-permute-start | bytes 393224 | tf_op jit(solution)/shard_map/ppermute | solution.py:282
  48.6 4.0 %collective-permute-done.11 = bf16[64,1024]{1,0:T(8,128)(2,1)S(1)} collective-permute-done((bf16[64,1024]{1,0:T(8,128)(2,1)S(1)}, bf16[64,1024]{1,0:T(8,128)(2,1)S(1)}, u32[]{:S(2)}, u32[]{:S(2)}) %collective-permute-start.11) | collective-permute-done | bytes 131104 | tf_op jit(solution)/shard_map/ppermute | solution.py:282
  52.6 0.8 %convert_add_fusion = f32[64,1024]{1,0:T(8,128)} fusion(bf16[64,1024]{1,0:T(8,128)(2,1)S(1)} %collective-permute-done.11, f32[64,1024]{1,0:T(8,128)S(1)} %convolution_add_fusion.1, f32[64,1024]{1,0:T(8,128)S(1)} %get-tuple-element.26, pred[]{:T(512)S(6)} %eq.13), kind=kLoop, calls=%fused_computation.4 | loop fusion | flops 196608 | bytes 917505 | tf_op jit(solution)/shard_map/add | solution.py:337
  (24 shorter events, 3.2 us)
Async XLA Ops:
  0.0 40.2 %copy-start = (bf16[1024,1024]{1,0:T(8,128)(2,1)S(1)}, bf16[1024,1024]{1,0:T(8,128)(2,1)}, u32[]{:S(2)}) copy-start(bf16[1024,1024]{1,0:T(8,128)(2,1)} %param.15) | copy-start | bytes 6291460
  0.0 10.5 %collective-permute-start = (bf16[64,1024]{1,0:T(8,128)(2,1)}, bf16[64,1024]{1,0:T(8,128)(2,1)S(1)}, u32[]{:S(2)}, u32[]{:S(2)}) collective-permute-start(bf16[64,1024]{1,0:T(8,128)(2,1)} %refs_3_.1), channel_id=1, source_target_pairs={{0,8},{4,12},{8,0},{12,4},{1,9},{5,13},{9,1},{13,5},{2,10},{6,14},... | collective-permute-start | bytes 393224 | tf_op jit(solution)/shard_map/ppermute | solution.py:282
  6.0 2.2 %copy-start.2 = (bf16[4096,2,256]{2,1,0:T(2,128)(2,1)S(1)}, bf16[4096,2,256]{2,1,0:T(2,128)(2,1)}, u32[]{:S(2)}) copy-start(bf16[4096,2,256]{2,1,0:T(2,128)(2,1)} %cache_ref.3) | copy-start | bytes 12582916
  6.0 2.2 %copy-start.3 = (bf16[256,2,256]{2,1,0:T(2,128)(2,1)S(1)}, bf16[256,2,256]{2,1,0:T(2,128)(2,1)}, u32[]{:S(2)}) copy-start(bf16[256,2,256]{2,1,0:T(2,128)(2,1)} %fin_ref.3) | copy-start | bytes 786436
  6.0 2.2 %copy-start.4 = (bf16[64,2,256]{2,1,0:T(2,128)(2,1)S(1)}, bf16[64,2,256]{2,1,0:T(2,128)(2,1)}, u32[]{:S(2)}) copy-start(bf16[64,2,256]{2,1,0:T(2,128)(2,1)} %own_ref.3) | copy-start | bytes 196612
  8.2 3.6 %copy-start.1 = (bf16[64,1024]{1,0:T(8,128)(2,1)S(1)}, bf16[64,1024]{1,0:T(8,128)(2,1)}, u32[]{:S(2)}) copy-start(bf16[64,1024]{1,0:T(8,128)(2,1)} %refs_3_.1) | copy-start | bytes 393220
  10.6 6.1 %collective-permute-start.1 = (bf16[64,1024]{1,0:T(8,128)(2,1)S(1)}, bf16[64,1024]{1,0:T(8,128)(2,1)S(1)}, u32[]{:S(2)}, u32[]{:S(2)}) collective-permute-start(bf16[64,1024]{1,0:T(8,128)(2,1)S(1)} %collective-permute-done.refs_3_), channel_id=1, source_target_pairs={{0,4},{4,0},{8,12},{12,8},{1,5},{5,1},{9,13},{13,9},{2,6},{6,2},{1... | collective-permute-start | bytes 393224 | tf_op jit(solution)/shard_map/ppermute | solution.py:282
  11.8 11.1 %collective-permute-start.2 = (bf16[64,1024]{1,0:T(8,128)(2,1)S(1)}, bf16[64,1024]{1,0:T(8,128)(2,1)S(1)}, u32[]{:S(2)}, u32[]{:S(2)}) collective-permute-start(bf16[64,1024]{1,0:T(8,128)(2,1)S(1)} %copy-done.1), channel_id=1, source_target_pairs={{0,4},{4,0},{8,12},{12,8},{1,5},{5,1},{9,13},{13,9},{2,6},{6,2},{1... | collective-permute-start | bytes 393224 | tf_op jit(solution)/shard_map/ppermute | solution.py:282
  14.7 13.8 %collective-permute-start.4 = (bf16[64,1152]{1,0:T(8,128)(2,1)S(1)}, bf16[64,1152]{1,0:T(8,128)(2,1)S(1)}, u32[]{:S(2)}, u32[]{:S(2)}) collective-permute-start(bf16[64,1152]{1,0:T(8,128)(2,1)S(1)} %attend.4.refs_4_), channel_id=1, source_target_pairs={{0,8},{4,12},{8,0},{12,4},{1,9},{5,13},{9,1},{13,5},{2,10},{6,14},... | collective-permute-start | bytes 442376 | tf_op jit(solution)/shard_map/ppermute | solution.py:282
  18.7 9.7 %collective-permute-start.3 = (bf16[64,1152]{1,0:T(8,128)(2,1)S(1)}, bf16[64,1152]{1,0:T(8,128)(2,1)S(1)}, u32[]{:S(2)}, u32[]{:S(2)}) collective-permute-start(bf16[64,1152]{1,0:T(8,128)(2,1)S(1)} %attend.5.refs_0_.refs_4_), channel_id=1, source_target_pairs={{0,12},{4,8},{8,4},{12,0},{1,13},{5,9},{9,5},{13,1},{2,14},{6,10},... | collective-permute-start | bytes 442376 | tf_op jit(solution)/shard_map/ppermute | solution.py:282
  26.6 5.2 %collective-permute-start.5 = (bf16[64,1152]{1,0:T(8,128)(2,1)S(1)}, bf16[64,1152]{1,0:T(8,128)(2,1)S(1)}, u32[]{:S(2)}, u32[]{:S(2)}) collective-permute-start(bf16[64,1152]{1,0:T(8,128)(2,1)S(1)} %attend.6.refs_4_), channel_id=1, source_target_pairs={{0,4},{4,0},{8,12},{12,8},{1,5},{5,1},{9,13},{13,9},{2,6},{6,2},{1... | collective-permute-start | bytes 442376 | tf_op jit(solution)/shard_map/ppermute | solution.py:282
  32.3 7.3 %collective-permute-start.8 = (bf16[64,1024]{1,0:T(8,128)(2,1)S(1)}, bf16[64,1024]{1,0:T(8,128)(2,1)S(1)}, u32[]{:S(2)}, u32[]{:S(2)}) collective-permute-start(bf16[64,1024]{1,0:T(8,128)(2,1)S(1)} %merge.1), channel_id=1, source_target_pairs={{0,8},{4,12},{8,0},{12,4},{1,9},{5,13},{9,1},{13,5},{2,10},{6,14},... | collective-permute-start | bytes 393224 | tf_op jit(solution)/shard_map/ppermute | solution.py:282
  33.5 6.7 %collective-permute-start.6 = (bf16[64,1024]{1,0:T(8,128)(2,1)S(1)}, bf16[64,1024]{1,0:T(8,128)(2,1)S(1)}, u32[]{:S(2)}, u32[]{:S(2)}) collective-permute-start(bf16[64,1024]{1,0:T(8,128)(2,1)S(1)} %merge.1), channel_id=1, source_target_pairs={{0,4},{4,0},{8,12},{12,8},{1,5},{5,1},{9,13},{13,9},{2,6},{6,2},{1... | collective-permute-start | bytes 393224 | tf_op jit(solution)/shard_map/ppermute | solution.py:282
  39.6 5.0 %collective-permute-start.9 = (bf16[64,1024]{1,0:T(8,128)(2,1)S(1)}, bf16[64,1024]{1,0:T(8,128)(2,1)S(1)}, u32[]{:S(2)}, u32[]{:S(2)}) collective-permute-start(bf16[64,1024]{1,0:T(8,128)(2,1)S(1)} %collective-permute-done.8), channel_id=1, source_target_pairs={{0,4},{4,0},{8,12},{12,8},{1,5},{5,1},{9,13},{13,9},{2,6},{6,2},{1... | collective-permute-start | bytes 393224 | tf_op jit(solution)/shard_map/ppermute | solution.py:282
  40.7 4.5 %collective-permute-start.7 = (bf16[64,1024]{1,0:T(8,128)(2,1)S(1)}, bf16[64,1024]{1,0:T(8,128)(2,1)S(1)}, u32[]{:S(2)}, u32[]{:S(2)}) collective-permute-start(bf16[64,1024]{1,0:T(8,128)(2,1)S(1)} %convolution_convert_fusion.1), channel_id=1, source_target_pairs={{0,1},{1,0},{2,3},{3,2},{4,5},{5,4},{6,7},{7,6},{8,9},{9,8},{10,11... | collective-permute-start | bytes 393224 | tf_op jit(solution)/shard_map/ppermute | solution.py:282
  45.1 1.4 %collective-permute-start.10 = (bf16[64,1024]{1,0:T(8,128)(2,1)S(1)}, bf16[64,1024]{1,0:T(8,128)(2,1)S(1)}, u32[]{:S(2)}, u32[]{:S(2)}) collective-permute-start(bf16[64,1024]{1,0:T(8,128)(2,1)S(1)} %convolution_convert_fusion), channel_id=1, source_target_pairs={{0,1},{1,0},{2,3},{3,2},{4,5},{5,4},{6,7},{7,6},{8,9},{9,8},{10,11... | collective-permute-start | bytes 393224 | tf_op jit(solution)/shard_map/ppermute | solution.py:282
  47.0 5.6 %collective-permute-start.11 = (bf16[64,1024]{1,0:T(8,128)(2,1)S(1)}, bf16[64,1024]{1,0:T(8,128)(2,1)S(1)}, u32[]{:S(2)}, u32[]{:S(2)}) collective-permute-start(bf16[64,1024]{1,0:T(8,128)(2,1)S(1)} %get-tuple-element.25), channel_id=1, source_target_pairs={{0,2},{1,3},{2,0},{3,1},{4,6},{5,7},{6,4},{7,5},{8,10},{9,11},{10,... | collective-permute-start | bytes 393224 | tf_op jit(solution)/shard_map/ppermute | solution.py:282

commit v5 on v4

--- a/solution.py
+++ b/solution.py
@@ -73,40 +73,43 @@
 
 
 def prepare_body(at, lists_ref, cache_ref, fin_ref, own_ref, *refs):
-    keys_ref, values_ref, info_ref = refs[-3:]
+    keys_ref, values_ref, info_ref, list_ref, sem = refs[-5:]
+    fetch = pltpu.make_async_copy(lists_ref, list_ref, sem)
+    fetch.start()
     width = keys_ref.shape[1]
-    end = lists_ref.shape[1] - 3
-    count, is_owner, limit = lists_ref[at, end], lists_ref[at, end + 1], lists_ref[at, end + 2]
     row = lax.broadcasted_iota(jnp.int32, (2 * BLOCK, 2 * BLOCK), 0)
     col = lax.broadcasted_iota(jnp.int32, (2 * BLOCK, 2 * BLOCK), 1)
     source = jnp.where(row < BLOCK, 2 * row, 2 * row - 2 * BLOCK + 1)
     pick = jnp.where(col == source, 1.0, 0.0).astype(BF)
 
-    def take_apart(pairs, to):
+    def take_apart(pairs):
         parts = jnp.dot(pick, pairs.reshape(2 * BLOCK, width), preferred_element_type=F32).astype(BF)
+        return parts[:BLOCK], parts[BLOCK:]
+
+    def put(parts, to):
         rows = pl.ds(pl.multiple_of(to * BLOCK, BLOCK), BLOCK)
-        keys_ref[rows] = parts[:BLOCK]
-        values_ref[rows] = parts[BLOCK:]
+        keys_ref[rows], values_ref[rows] = parts
+
+    fin_blocks, own_rows = fin_ref.shape[0] // BLOCK, own_ref.shape[0]
+    filler = jnp.zeros((BLOCK - own_rows, 2, width), BF)
+    own = take_apart(jnp.concatenate([own_ref[...], filler], axis=0))
+    finished = [take_apart(fin_ref[i * BLOCK : (i + 1) * BLOCK]) for i in range(fin_blocks)]
+    fetch.wait()
+    end = list_ref.shape[1] - 3
+    count, is_owner, limit = list_ref[at, end], list_ref[at, end + 1], list_ref[at, end + 2]
+    full = count + is_owner * fin_blocks
 
     @pl.loop(0, (count + UNROLL - 1) // UNROLL)
     def _(j):
         for i in range(UNROLL):
-            start = pl.multiple_of(lists_ref[at, j * UNROLL + i] * BLOCK, BLOCK)
-            take_apart(cache_ref[pl.ds(start, BLOCK)], j * UNROLL + i)
-
-    fin_blocks, own_rows = fin_ref.shape[0] // BLOCK, own_ref.shape[0]
-
-    @pl.when(is_owner > 0)
-    def _():
-        for i in range(fin_blocks):
-            take_apart(fin_ref[i * BLOCK : (i + 1) * BLOCK], count + i)
-
-    full = count + is_owner * fin_blocks
-    filler = jnp.zeros((BLOCK - own_rows, 2, width), BF)
-    take_apart(jnp.concatenate([own_ref[...], filler], axis=0), full)
-    unread = pl.ds(pl.multiple_of((full + 1) * BLOCK, BLOCK), BLOCK)
-    keys_ref[unread] = jnp.zeros((BLOCK, width), BF)
-    values_ref[unread] = jnp.zeros((BLOCK, width), BF)
+            start = pl.multiple_of(list_ref[at, j * UNROLL + i] * BLOCK, BLOCK)
+            put(take_apart(cache_ref[pl.ds(start, BLOCK)]), j * UNROLL + i)
+
+    for i in range(fin_blocks):
+        put(finished[i], count + i)
+    put(own, full)
+    zeros = jnp.zeros((BLOCK, width), BF)
+    put((zeros, zeros), full + 1)
 
     pairs = (full + 2) // 2
     lane = lax.broadcasted_iota(jnp.int32, (8, 2 * BLOCK), 1)
@@ -120,9 +123,10 @@
     total = rows + finished.shape[0] + UNROLL * BLOCK
     return pl.pallas_call(
         functools.partial(prepare_body, at),
-        in_specs=[smem_spec(), vmem_spec(), vmem_spec(), vmem_spec()] + [pl.BlockSpec(memory_space=pl.ANY)] * len(after),
+        in_specs=[vmem_spec()] * 4 + [pl.BlockSpec(memory_space=pl.ANY)] * len(after),
         out_specs=[vmem_spec()] * 3,
         out_shape=[jax.ShapeDtypeStruct((total, width), BF)] * 2 + [jax.ShapeDtypeStruct((16, 2 * BLOCK), F32)],
+        scratch_shapes=[pltpu.SMEM(lists.shape, jnp.int32), pltpu.SemaphoreType.DMA],
         cost_estimate=pl.CostEstimate(flops=4 * 1024**3, bytes_accessed=12 * 1024**2, transcendentals=0),
         compiler_params=params(),
         name="prepare",
@@ -177,7 +181,8 @@
             )
 
     def in_steps(total, step):
-        pl.loop(0, total // 4)(lambda j: step(4 * j, 4))
+        pl.loop(0, total // 8)(lambda j: step(8 * j, 8))
+        pl.when(total % 8 >= 4)(lambda: step(total // 8 * 8, 4))
         done = total // 4 * 4
         pl.when(total - done >= 2)(lambda: step(done, 2))
         pl.when(total % 2 == 1)(lambda: step(total - 1, 1))

time: 53.8 us -> 54.3 us (level); the launches traced: 53.4 us -> 54.4 us
  Pallas kernels: 13.7 us -> 16.1 us
  starting transfers between devices: 16.9 us -> 15 us
  waiting for transfers between devices: 17.3 us -> 18 us
    pallas_call x4, Pallas kernels: 7.73 us -> 10.1 us  [attend(): pl.pallas_call(functools.partial(attend_body, (kv, group, tokens, n)), in...]
    ppermute x12, starting transfers between devices: 16.9 us -> 15 us  [swap(): return lax.ppermute(value, axis, [(i, i ^ k) for i in range(size)])]
    ppermute x12, waiting for transfers between devices: 17.3 us -> 18 us  [swap(): return lax.ppermute(value, axis, [(i, i ^ k) for i in range(size)])]
  transfers between devices with their start and end apart: 12 -> 12, of which waited for: 7 -> 7; matrix products, arithmetic and copies ran while one was open for 4% -> 4% of each run, Pallas kernels for 25% -> 29%
where the time goes in v5:
time: 54.3 us; the launch traced here: 54.4 us
  waiting for transfers between devices  18 us (33%)
  Pallas kernels  16.1 us (30%)
  starting transfers between devices  15 us (28%)
  matrix products  1.93 us (4%)
  between operations  1.46 us (3%)
  other arithmetic  1.44 us (3%)
  local copies, waits for them, and re-layouts  0.6 us (1%)
    ppermute x12, waiting for transfers between devices, swap(): return lax.ppermute(value, axis, [(i, i ^ k) for i in range(size)])  18 us
    ppermute x12, starting transfers between devices, swap(): return lax.ppermute(value, axis, [(i, i ^ k) for i in range(size)])  15 us
    pallas_call x4, Pallas kernels, attend(): pl.pallas_call(functools.partial(attend_body, (kv, group, tokens, n)), in...  10.1 us
    pallas_call x2, Pallas kernels, prepare(): pl.pallas_call(functools.partial(prepare_body, at), in_specs=[vmem_spec()...  3.83 us
    dot_general x4, matrix products, project(): return jnp.dot(rows, output_weight, preferred_element_type=F32)  1.93 us
    pallas_call x1, Pallas kernels, make_lists(): pl.pallas_call(functools.partial(list_body, axis, own_tokens, shards, fin...  1.6 us
  transfers between devices with their start and end apart: 12, of which 7 were waited for; matrix products, arithmetic and copies ran while one was open for 4% of the time, Pallas kernels for 29%

profile of v5, /device:TPU:0, one launch (start us, length us, event | category | flops | bytes accessed | tf_op | source)
XLA Modules:
  0.0 54.4 jit_solution(5725397942646402707)
XLA Ops:
  0.0 4.0 %collective-permute-start = (bf16[64,1024]{1,0:T(8,128)(2,1)}, bf16[64,1024]{1,0:T(8,128)(2,1)S(1)}, u32[]{:S(2)}, u32[]{:S(2)}) collective-permute-start(bf16[64,1024]{1,0:T(8,128)(2,1)} %refs_3_.1), channel_id=1, source_target_pairs={{0,8},{4,12},{8,0},{12,4},{1,9},{5,13},{9,1},{13,5},{2,10},{6,14},... | collective-permute-start | bytes 393224 | tf_op jit(solution)/shard_map/ppermute | solution.py:287
  5.3 0.7 %pad_add_fusion.meta_ref = s32[4,32]{1,0:T(4,128)S(1)} fusion(s32[1,1]{1,0:T(1,128)} %bitcast.7, s32[1,1]{1,0:T(1,128)} %bitcast.6, s32[2,32]{1,0:T(2,128)} %param.12), kind=kLoop, calls=%fused_computation.14 | loop fusion | flops 256 | bytes 776 | tf_op jit(solution)/shard_map/concatenate | solution.py:63
  6.0 1.6 %lists.1.lists_ref.refs_4_ = s32[2,39]{1,0:T(2,128)S(1)} custom-call(s32[4,32]{1,0:T(4,128)S(1)} %pad_add_fusion.meta_ref), custom_call_target="tpu_custom_call" | custom-call | flops 4294967296 | tf_op jit(solution)/shard_map/lists/pallas_call | solution.py:64
  7.7 0.6 %copy-done.2 = bf16[4096,2,256]{2,1,0:T(2,128)(2,1)S(1)} copy-done((bf16[4096,2,256]{2,1,0:T(2,128)(2,1)S(1)}, bf16[4096,2,256]{2,1,0:T(2,128)(2,1)}, u32[]{:S(2)}) %copy-start.2) | copy-done | bytes 4194328
  8.2 1.7 %prepare.2 = (bf16[4864,256]{1,0:T(8,128)(2,1)S(1)}, bf16[4864,256]{1,0:T(8,128)(2,1)S(1)}, f32[16,256]{1,0:T(8,128)S(1)}) custom-call(s32[2,39]{1,0:T(2,128)S(1)} %lists.1.lists_ref.refs_4_, bf16[4096,2,256]{2,1,0:T(2,128)(2,1)S(1)} %copy-done.2, bf16[256,2,256]{2,1,0:T(2,128)(2,1)S(1)} %copy-done.3, bf16[64,2,256]{2,1,0:T(2,128)(2,1)S(1)} %copy-done.4), custom_call_target="tpu_custom_call" | custom-call | flops 4294967296 | bytes 12582912 | tf_op jit(solution)/shard_map/prepare/pallas_call | solution.py:124
  10.0 0.6 %collective-permute-done.refs_3_ = bf16[64,1024]{1,0:T(8,128)(2,1)S(1)} collective-permute-done((bf16[64,1024]{1,0:T(8,128)(2,1)}, bf16[64,1024]{1,0:T(8,128)(2,1)S(1)}, u32[]{:S(2)}, u32[]{:S(2)}) %collective-permute-start) | collective-permute-done | bytes 131104 | tf_op jit(solution)/shard_map/ppermute | solution.py:287
  10.6 1.1 %collective-permute-start.1 = (bf16[64,1024]{1,0:T(8,128)(2,1)S(1)}, bf16[64,1024]{1,0:T(8,128)(2,1)S(1)}, u32[]{:S(2)}, u32[]{:S(2)}) collective-permute-start(bf16[64,1024]{1,0:T(8,128)(2,1)S(1)} %collective-permute-done.refs_3_), channel_id=1, source_target_pairs={{0,4},{4,0},{8,12},{12,8},{1,5},{5,1},{9,13},{13,9},{2,6},{6,2},{1... | collective-permute-start | bytes 393224 | tf_op jit(solution)/shard_map/ppermute | solution.py:287
  11.6 1.0 %collective-permute-start.2 = (bf16[64,1024]{1,0:T(8,128)(2,1)S(1)}, bf16[64,1024]{1,0:T(8,128)(2,1)S(1)}, u32[]{:S(2)}, u32[]{:S(2)}) collective-permute-start(bf16[64,1024]{1,0:T(8,128)(2,1)S(1)} %copy-done.1), channel_id=1, source_target_pairs={{0,4},{4,0},{8,12},{12,8},{1,5},{5,1},{9,13},{13,9},{2,6},{6,2},{1... | collective-permute-start | bytes 393224 | tf_op jit(solution)/shard_map/ppermute | solution.py:287
  12.6 2.5 %attend.4.refs_4_ = bf16[64,1152]{1,0:T(8,128)(2,1)S(1)} custom-call(f32[16,256]{1,0:T(8,128)S(1)} %get-tuple-element.18.refs_0_, bf16[4864,256]{1,0:T(8,128)(2,1)S(1)} %get-tuple-element.19.refs_1_, bf16[4864,256]{1,0:T(8,128)(2,1)S(1)} %get-tuple-element.20.refs_2_, bf16[64,1024]{1,0:T(8,128)(2,1)S(1)} %collective-permute-done.refs_3_, ...), custom_call_target="tpu_custom_call" | custom-call | flops 67108864 | tf_op jit(solution)/shard_map/attend/pallas_call | solution.py:223
  15.1 2.2 %collective-permute-start.4 = (bf16[64,1152]{1,0:T(8,128)(2,1)S(1)}, bf16[64,1152]{1,0:T(8,128)(2,1)S(1)}, u32[]{:S(2)}, u32[]{:S(2)}) collective-permute-start(bf16[64,1152]{1,0:T(8,128)(2,1)S(1)} %attend.4.refs_4_), channel_id=1, source_target_pairs={{0,8},{4,12},{8,0},{12,4},{1,9},{5,13},{9,1},{13,5},{2,10},{6,14},... | collective-permute-start | bytes 442376 | tf_op jit(solution)/shard_map/ppermute | solution.py:287
  17.3 2.5 %attend.5.refs_0_.refs_4_ = bf16[64,1152]{1,0:T(8,128)(2,1)S(1)} custom-call(f32[16,256]{1,0:T(8,128)S(1)} %get-tuple-element.18.refs_0_, bf16[4864,256]{1,0:T(8,128)(2,1)S(1)} %get-tuple-element.19.refs_1_, bf16[4864,256]{1,0:T(8,128)(2,1)S(1)} %get-tuple-element.20.refs_2_, bf16[64,1024]{1,0:T(8,128)(2,1)S(1)} %collective-permute-done.1.refs_3_, ...), custom_call_target="tpu_custom_call" | custom-call | flops 67108864 | tf_op jit(solution)/shard_map/attend/pallas_call | solution.py:223
  19.7 3.2 %collective-permute-start.3 = (bf16[64,1152]{1,0:T(8,128)(2,1)S(1)}, bf16[64,1152]{1,0:T(8,128)(2,1)S(1)}, u32[]{:S(2)}, u32[]{:S(2)}) collective-permute-start(bf16[64,1152]{1,0:T(8,128)(2,1)S(1)} %attend.5.refs_0_.refs_4_), channel_id=1, source_target_pairs={{0,12},{4,8},{8,4},{12,0},{1,13},{5,9},{9,5},{13,1},{2,14},{6,10},... | collective-permute-start | bytes 442376 | tf_op jit(solution)/shard_map/ppermute | solution.py:287
  23.0 2.1 %prepare.3 = (bf16[4864,256]{1,0:T(8,128)(2,1)S(1)}, bf16[4864,256]{1,0:T(8,128)(2,1)S(1)}, f32[16,256]{1,0:T(8,128)S(1)}) custom-call(s32[2,39]{1,0:T(2,128)S(1)} %lists.1.lists_ref.refs_4_, bf16[4096,2,256]{2,1,0:T(2,128)(2,1)S(1)} %copy-done.2, bf16[256,2,256]{2,1,0:T(2,128)(2,1)S(1)} %copy-done.3, bf16[64,2,256]{2,1,0:T(2,128)(2,1)S(1)} %copy-done.4, ...), custom_call_target="tpu_custom_call" | custom-call | flops 4294967296 | bytes 12582912 | tf_op jit(solution)/shard_map/prepare/pallas_call | solution.py:124
  25.1 2.7 %attend.6.refs_4_ = bf16[64,1152]{1,0:T(8,128)(2,1)S(1)} custom-call(f32[16,256]{1,0:T(8,128)S(1)} %get-tuple-element.22.refs_0_, bf16[4864,256]{1,0:T(8,128)(2,1)S(1)} %get-tuple-element.23.refs_1_, bf16[4864,256]{1,0:T(8,128)(2,1)S(1)} %get-tuple-element.24.refs_2_, bf16[64,1024]{1,0:T(8,128)(2,1)S(1)} %collective-permute-done.2.refs_1_.refs_3_, ...), custom_call_target="tpu_custom_call" | custom-call | flops 67108864 | tf_op jit(solution)/shard_map/attend/pallas_call | solution.py:223
  27.9 2.5 %attend.7.refs_0_ = bf16[64,1152]{1,0:T(8,128)(2,1)S(1)} custom-call(f32[16,256]{1,0:T(8,128)S(1)} %get-tuple-element.22.refs_0_, bf16[4864,256]{1,0:T(8,128)(2,1)S(1)} %get-tuple-element.23.refs_1_, bf16[4864,256]{1,0:T(8,128)(2,1)S(1)} %get-tuple-element.24.refs_2_, bf16[64,1024]{1,0:T(8,128)(2,1)S(1)} %copy-done.1, bf16[64,1152]{1,0:T(8,128)(2,1)S(1)} %attend.6.refs_4_), custom_call_target="tpu_custom_call" | custom-call | flops 67108864 | tf_op jit(solution)/shard_map/attend/pallas_call | solution.py:223
  30.4 2.6 %collective-permute-done.5.refs_3_ = bf16[64,1152]{1,0:T(8,128)(2,1)S(1)} collective-permute-done((bf16[64,1152]{1,0:T(8,128)(2,1)S(1)}, bf16[64,1152]{1,0:T(8,128)(2,1)S(1)}, u32[]{:S(2)}, u32[]{:S(2)}) %collective-permute-start.5) | collective-permute-done | bytes 147488 | tf_op jit(solution)/shard_map/ppermute | solution.py:287
  33.0 0.5 merge.1
  33.7 1.5 %collective-permute-start.6 = (bf16[64,1024]{1,0:T(8,128)(2,1)S(1)}, bf16[64,1024]{1,0:T(8,128)(2,1)S(1)}, u32[]{:S(2)}, u32[]{:S(2)}) collective-permute-start(bf16[64,1024]{1,0:T(8,128)(2,1)S(1)} %merge.1), channel_id=1, source_target_pairs={{0,4},{4,0},{8,12},{12,8},{1,5},{5,1},{9,13},{13,9},{2,6},{6,2},{1... | collective-permute-start | bytes 393224 | tf_op jit(solution)/shard_map/ppermute | solution.py:287
  35.2 5.5 %collective-permute-done.8 = bf16[64,1024]{1,0:T(8,128)(2,1)S(1)} collective-permute-done((bf16[64,1024]{1,0:T(8,128)(2,1)S(1)}, bf16[64,1024]{1,0:T(8,128)(2,1)S(1)}, u32[]{:S(2)}, u32[]{:S(2)}) %collective-permute-start.8) | collective-permute-done | bytes 131104 | tf_op jit(solution)/shard_map/ppermute | solution.py:287
  41.6 4.1 %collective-permute-done.9 = bf16[64,1024]{1,0:T(8,128)(2,1)S(1)} collective-permute-done((bf16[64,1024]{1,0:T(8,128)(2,1)S(1)}, bf16[64,1024]{1,0:T(8,128)(2,1)S(1)}, u32[]{:S(2)}, u32[]{:S(2)}) %collective-permute-start.9) | collective-permute-done | bytes 131104 | tf_op jit(solution)/shard_map/ppermute | solution.py:287
  46.7 0.8 %collective-permute-done.10 = bf16[64,1024]{1,0:T(8,128)(2,1)S(1)} collective-permute-done((bf16[64,1024]{1,0:T(8,128)(2,1)S(1)}, bf16[64,1024]{1,0:T(8,128)(2,1)S(1)}, u32[]{:S(2)}, u32[]{:S(2)}) %collective-permute-start.10) | collective-permute-done | bytes 131104 | tf_op jit(solution)/shard_map/ppermute | solution.py:287
  48.1 1.5 %collective-permute-start.11 = (bf16[64,1024]{1,0:T(8,128)(2,1)S(1)}, bf16[64,1024]{1,0:T(8,128)(2,1)S(1)}, u32[]{:S(2)}, u32[]{:S(2)}) collective-permute-start(bf16[64,1024]{1,0:T(8,128)(2,1)S(1)} %get-tuple-element.25), channel_id=1, source_target_pairs={{0,2},{1,3},{2,0},{3,1},{4,6},{5,7},{6,4},{7,5},{8,10},{9,11},{10,... | collective-permute-start | bytes 393224 | tf_op jit(solution)/shard_map/ppermute | solution.py:287
  49.6 4.1 %collective-permute-done.11 = bf16[64,1024]{1,0:T(8,128)(2,1)S(1)} collective-permute-done((bf16[64,1024]{1,0:T(8,128)(2,1)S(1)}, bf16[64,1024]{1,0:T(8,128)(2,1)S(1)}, u32[]{:S(2)}, u32[]{:S(2)}) %collective-permute-start.11) | collective-permute-done | bytes 131104 | tf_op jit(solution)/shard_map/ppermute | solution.py:287
  53.7 0.8 %convert_add_fusion = f32[64,1024]{1,0:T(8,128)} fusion(bf16[64,1024]{1,0:T(8,128)(2,1)S(1)} %collective-permute-done.11, f32[64,1024]{1,0:T(8,128)S(1)} %convolution_add_fusion.1, f32[64,1024]{1,0:T(8,128)S(1)} %get-tuple-element.26, pred[]{:T(512)S(6)} %eq.13), kind=kLoop, calls=%fused_computation.4 | loop fusion | flops 196608 | bytes 917505 | tf_op jit(solution)/shard_map/add | solution.py:342
  (24 shorter events, 2.8 us)
Async XLA Ops:
  0.0 41.1 %copy-start = (bf16[1024,1024]{1,0:T(8,128)(2,1)S(1)}, bf16[1024,1024]{1,0:T(8,128)(2,1)}, u32[]{:S(2)}) copy-start(bf16[1024,1024]{1,0:T(8,128)(2,1)} %param.15) | copy-start | bytes 6291460
  0.0 10.5 %collective-permute-start = (bf16[64,1024]{1,0:T(8,128)(2,1)}, bf16[64,1024]{1,0:T(8,128)(2,1)S(1)}, u32[]{:S(2)}, u32[]{:S(2)}) collective-permute-start(bf16[64,1024]{1,0:T(8,128)(2,1)} %refs_3_.1), channel_id=1, source_target_pairs={{0,8},{4,12},{8,0},{12,4},{1,9},{5,13},{9,1},{13,5},{2,10},{6,14},... | collective-permute-start | bytes 393224 | tf_op jit(solution)/shard_map/ppermute | solution.py:287
  6.0 2.2 %copy-start.2 = (bf16[4096,2,256]{2,1,0:T(2,128)(2,1)S(1)}, bf16[4096,2,256]{2,1,0:T(2,128)(2,1)}, u32[]{:S(2)}) copy-start(bf16[4096,2,256]{2,1,0:T(2,128)(2,1)} %cache_ref.3) | copy-start | bytes 12582916
  6.0 2.2 %copy-start.3 = (bf16[256,2,256]{2,1,0:T(2,128)(2,1)S(1)}, bf16[256,2,256]{2,1,0:T(2,128)(2,1)}, u32[]{:S(2)}) copy-start(bf16[256,2,256]{2,1,0:T(2,128)(2,1)} %fin_ref.3) | copy-start | bytes 786436
  6.0 2.2 %copy-start.4 = (bf16[64,2,256]{2,1,0:T(2,128)(2,1)S(1)}, bf16[64,2,256]{2,1,0:T(2,128)(2,1)}, u32[]{:S(2)}) copy-start(bf16[64,2,256]{2,1,0:T(2,128)(2,1)} %own_ref.3) | copy-start | bytes 196612
  8.2 3.4 %copy-start.1 = (bf16[64,1024]{1,0:T(8,128)(2,1)S(1)}, bf16[64,1024]{1,0:T(8,128)(2,1)}, u32[]{:S(2)}) copy-start(bf16[64,1024]{1,0:T(8,128)(2,1)} %refs_3_.1) | copy-start | bytes 393220
  10.6 6.7 %collective-permute-start.1 = (bf16[64,1024]{1,0:T(8,128)(2,1)S(1)}, bf16[64,1024]{1,0:T(8,128)(2,1)S(1)}, u32[]{:S(2)}, u32[]{:S(2)}) collective-permute-start(bf16[64,1024]{1,0:T(8,128)(2,1)S(1)} %collective-permute-done.refs_3_), channel_id=1, source_target_pairs={{0,4},{4,0},{8,12},{12,8},{1,5},{5,1},{9,13},{13,9},{2,6},{6,2},{1... | collective-permute-start | bytes 393224 | tf_op jit(solution)/shard_map/ppermute | solution.py:287
  11.6 11.4 %collective-permute-start.2 = (bf16[64,1024]{1,0:T(8,128)(2,1)S(1)}, bf16[64,1024]{1,0:T(8,128)(2,1)S(1)}, u32[]{:S(2)}, u32[]{:S(2)}) collective-permute-start(bf16[64,1024]{1,0:T(8,128)(2,1)S(1)} %copy-done.1), channel_id=1, source_target_pairs={{0,4},{4,0},{8,12},{12,8},{1,5},{5,1},{9,13},{13,9},{2,6},{6,2},{1... | collective-permute-start | bytes 393224 | tf_op jit(solution)/shard_map/ppermute | solution.py:287
  15.1 15.3 %collective-permute-start.4 = (bf16[64,1152]{1,0:T(8,128)(2,1)S(1)}, bf16[64,1152]{1,0:T(8,128)(2,1)S(1)}, u32[]{:S(2)}, u32[]{:S(2)}) collective-permute-start(bf16[64,1152]{1,0:T(8,128)(2,1)S(1)} %attend.4.refs_4_), channel_id=1, source_target_pairs={{0,8},{4,12},{8,0},{12,4},{1,9},{5,13},{9,1},{13,5},{2,10},{6,14},... | collective-permute-start | bytes 442376 | tf_op jit(solution)/shard_map/ppermute | solution.py:287
  19.7 10.6 %collective-permute-start.3 = (bf16[64,1152]{1,0:T(8,128)(2,1)S(1)}, bf16[64,1152]{1,0:T(8,128)(2,1)S(1)}, u32[]{:S(2)}, u32[]{:S(2)}) collective-permute-start(bf16[64,1152]{1,0:T(8,128)(2,1)S(1)} %attend.5.refs_0_.refs_4_), channel_id=1, source_target_pairs={{0,12},{4,8},{8,4},{12,0},{1,13},{5,9},{9,5},{13,1},{2,14},{6,10},... | collective-permute-start | bytes 442376 | tf_op jit(solution)/shard_map/ppermute | solution.py:287
  27.8 5.2 %collective-permute-start.5 = (bf16[64,1152]{1,0:T(8,128)(2,1)S(1)}, bf16[64,1152]{1,0:T(8,128)(2,1)S(1)}, u32[]{:S(2)}, u32[]{:S(2)}) collective-permute-start(bf16[64,1152]{1,0:T(8,128)(2,1)S(1)} %attend.6.refs_4_), channel_id=1, source_target_pairs={{0,4},{4,0},{8,12},{12,8},{1,5},{5,1},{9,13},{13,9},{2,6},{6,2},{1... | collective-permute-start | bytes 442376 | tf_op jit(solution)/shard_map/ppermute | solution.py:287
  33.5 7.2 %collective-permute-start.8 = (bf16[64,1024]{1,0:T(8,128)(2,1)S(1)}, bf16[64,1024]{1,0:T(8,128)(2,1)S(1)}, u32[]{:S(2)}, u32[]{:S(2)}) collective-permute-start(bf16[64,1024]{1,0:T(8,128)(2,1)S(1)} %merge.1), channel_id=1, source_target_pairs={{0,8},{4,12},{8,0},{12,4},{1,9},{5,13},{9,1},{13,5},{2,10},{6,14},... | collective-permute-start | bytes 393224 | tf_op jit(solution)/shard_map/ppermute | solution.py:287
  33.7 7.3 %collective-permute-start.6 = (bf16[64,1024]{1,0:T(8,128)(2,1)S(1)}, bf16[64,1024]{1,0:T(8,128)(2,1)S(1)}, u32[]{:S(2)}, u32[]{:S(2)}) collective-permute-start(bf16[64,1024]{1,0:T(8,128)(2,1)S(1)} %merge.1), channel_id=1, source_target_pairs={{0,4},{4,0},{8,12},{12,8},{1,5},{5,1},{9,13},{13,9},{2,6},{6,2},{1... | collective-permute-start | bytes 393224 | tf_op jit(solution)/shard_map/ppermute | solution.py:287
  40.7 5.0 %collective-permute-start.9 = (bf16[64,1024]{1,0:T(8,128)(2,1)S(1)}, bf16[64,1024]{1,0:T(8,128)(2,1)S(1)}, u32[]{:S(2)}, u32[]{:S(2)}) collective-permute-start(bf16[64,1024]{1,0:T(8,128)(2,1)S(1)} %collective-permute-done.8), channel_id=1, source_target_pairs={{0,4},{4,0},{8,12},{12,8},{1,5},{5,1},{9,13},{13,9},{2,6},{6,2},{1... | collective-permute-start | bytes 393224 | tf_op jit(solution)/shard_map/ppermute | solution.py:287
  41.5 4.7 %collective-permute-start.7 = (bf16[64,1024]{1,0:T(8,128)(2,1)S(1)}, bf16[64,1024]{1,0:T(8,128)(2,1)S(1)}, u32[]{:S(2)}, u32[]{:S(2)}) collective-permute-start(bf16[64,1024]{1,0:T(8,128)(2,1)S(1)} %convolution_convert_fusion.1), channel_id=1, source_target_pairs={{0,1},{1,0},{2,3},{3,2},{4,5},{5,4},{6,7},{7,6},{8,9},{9,8},{10,11... | collective-permute-start | bytes 393224 | tf_op jit(solution)/shard_map/ppermute | solution.py:287
  46.2 1.4 %collective-permute-start.10 = (bf16[64,1024]{1,0:T(8,128)(2,1)S(1)}, bf16[64,1024]{1,0:T(8,128)(2,1)S(1)}, u32[]{:S(2)}, u32[]{:S(2)}) collective-permute-start(bf16[64,1024]{1,0:T(8,128)(2,1)S(1)} %convolution_convert_fusion), channel_id=1, source_target_pairs={{0,1},{1,0},{2,3},{3,2},{4,5},{5,4},{6,7},{7,6},{8,9},{9,8},{10,11... | collective-permute-start | bytes 393224 | tf_op jit(solution)/shard_map/ppermute | solution.py:287
  48.1 5.6 %collective-permute-start.11 = (bf16[64,1024]{1,0:T(8,128)(2,1)S(1)}, bf16[64,1024]{1,0:T(8,128)(2,1)S(1)}, u32[]{:S(2)}, u32[]{:S(2)}) collective-permute-start(bf16[64,1024]{1,0:T(8,128)(2,1)S(1)} %get-tuple-element.25), channel_id=1, source_target_pairs={{0,2},{1,3},{2,0},{3,1},{4,6},{5,7},{6,4},{7,5},{8,10},{9,11},{10,... | collective-permute-start | bytes 393224 | tf_op jit(solution)/shard_map/ppermute | solution.py:287

commit v6 on v5

--- a/solution.py
+++ b/solution.py
@@ -334,7 +334,12 @@
             first, second = shards[pair[0]], shards[pair[1]]
             other = project(jnp.where(first_mine, second, first)).astype(BF)
             mine = project(jnp.where(first_mine, first, second))
-            return mine + swap(other, "head", n_head, 1).astype(F32)
+            if pair[0] == 0:
+                other, mine = lax.optimization_barrier((other, mine))
+            received = swap(other, "head", n_head, 1)
+            if pair[0] == 2:
+                received, mine = lax.optimization_barrier((received, mine))
+            return mine + received.astype(F32)
 
         near, far = over_cores((0, 1)), over_cores((2, 3))
         near_mine = here // 2 == side

time: 54.3 us -> 53.4 us (0.983)
  Pallas kernels: 16.1 us -> 12.9 us
  starting transfers between devices: 15 us -> 17.3 us
    pallas_call x4, Pallas kernels: 10.1 us -> 7.65 us  [attend(): pl.pallas_call(functools.partial(attend_body, (kv, group, tokens, n)), in...]
    ppermute x12, starting transfers between devices: 15 us -> 17.3 us  [swap(): return lax.ppermute(value, axis, [(i, i ^ k) for i in range(size)])]
    pallas_call x2, Pallas kernels: 3.83 us -> 3.09 us  [prepare(): pl.pallas_call(functools.partial(prepare_body, at), in_specs=[vmem_spec()...]
  transfers between devices with their start and end apart: 12 -> 12, of which waited for: 7 -> 7; matrix products, arithmetic and copies ran while one was open for 4% -> 5% of each run, Pallas kernels for 29% -> 23%
where the time goes in v6:
time: 53.4 us; the launch traced here: 53.1 us
  waiting for transfers between devices  17.5 us (33%)
  starting transfers between devices  17.3 us (32%)
  Pallas kernels  12.9 us (24%)
  matrix products  1.91 us (4%)
  other arithmetic  1.52 us (3%)
  between operations  1.45 us (3%)
  local copies, waits for them, and re-layouts  0.6 us (1%)
    ppermute x12, waiting for transfers between devices, swap(): return lax.ppermute(value, axis, [(i, i ^ k) for i in range(size)])  17.5 us
    ppermute x12, starting transfers between devices, swap(): return lax.ppermute(value, axis, [(i, i ^ k) for i in range(size)])  17.3 us
    pallas_call x4, Pallas kernels, attend(): pl.pallas_call(functools.partial(attend_body, (kv, group, tokens, n)), in...  7.65 us
    pallas_call x2, Pallas kernels, prepare(): pl.pallas_call(functools.partial(prepare_body, at), in_specs=[vmem_spec()...  3.09 us
    dot_general x4, matrix products, project(): return jnp.dot(rows, output_weight, preferred_element_type=F32)  1.91 us
    pallas_call x1, Pallas kernels, make_lists(): pl.pallas_call(functools.partial(list_body, axis, own_tokens, shards, fin...  1.6 us
  transfers between devices with their start and end apart: 12, of which 7 were waited for; matrix products, arithmetic and copies ran while one was open for 5% of the time, Pallas kernels for 23%

profile of v6, /device:TPU:0, one launch (start us, length us, event | category | flops | bytes accessed | tf_op | source)
XLA Modules:
  0.0 53.1 jit_solution(2965759600205822187)
XLA Ops:
  0.0 4.0 %collective-permute-start = (bf16[64,1024]{1,0:T(8,128)(2,1)}, bf16[64,1024]{1,0:T(8,128)(2,1)S(1)}, u32[]{:S(2)}, u32[]{:S(2)}) collective-permute-start(bf16[64,1024]{1,0:T(8,128)(2,1)} %refs_3_.1), channel_id=1, source_target_pairs={{0,8},{4,12},{8,0},{12,4},{1,9},{5,13},{9,1},{13,5},{2,10},{6,14},... | collective-permute-start | bytes 393224 | tf_op jit(solution)/shard_map/ppermute | solution.py:287
  5.3 0.7 %pad_add_fusion.meta_ref = s32[4,32]{1,0:T(4,128)S(1)} fusion(s32[1,1]{1,0:T(1,128)} %bitcast.7, s32[1,1]{1,0:T(1,128)} %bitcast.6, s32[2,32]{1,0:T(2,128)} %param.12), kind=kLoop, calls=%fused_computation.16 | loop fusion | flops 256 | bytes 776 | tf_op jit(solution)/shard_map/concatenate | solution.py:63
  6.0 1.6 %lists.1.lists_ref.refs_4_ = s32[2,39]{1,0:T(2,128)S(1)} custom-call(s32[4,32]{1,0:T(4,128)S(1)} %pad_add_fusion.meta_ref), custom_call_target="tpu_custom_call" | custom-call | flops 4294967296 | tf_op jit(solution)/shard_map/lists/pallas_call | solution.py:64
  7.7 0.6 %copy-done.2 = bf16[4096,2,256]{2,1,0:T(2,128)(2,1)S(1)} copy-done((bf16[4096,2,256]{2,1,0:T(2,128)(2,1)S(1)}, bf16[4096,2,256]{2,1,0:T(2,128)(2,1)}, u32[]{:S(2)}) %copy-start.2) | copy-done | bytes 4194328
  8.2 1.4 %prepare.2 = (bf16[4864,256]{1,0:T(8,128)(2,1)S(1)}, bf16[4864,256]{1,0:T(8,128)(2,1)S(1)}, f32[16,256]{1,0:T(8,128)S(1)}) custom-call(s32[2,39]{1,0:T(2,128)S(1)} %lists.1.lists_ref.refs_4_, bf16[4096,2,256]{2,1,0:T(2,128)(2,1)S(1)} %copy-done.2, bf16[256,2,256]{2,1,0:T(2,128)(2,1)S(1)} %copy-done.3, bf16[64,2,256]{2,1,0:T(2,128)(2,1)S(1)} %copy-done.4), custom_call_target="tpu_custom_call" | custom-call | flops 4294967296 | bytes 12582912 | tf_op jit(solution)/shard_map/prepare/pallas_call | solution.py:124
  9.6 0.9 %collective-permute-done.refs_3_ = bf16[64,1024]{1,0:T(8,128)(2,1)S(1)} collective-permute-done((bf16[64,1024]{1,0:T(8,128)(2,1)}, bf16[64,1024]{1,0:T(8,128)(2,1)S(1)}, u32[]{:S(2)}, u32[]{:S(2)}) %collective-permute-start) | collective-permute-done | bytes 131104 | tf_op jit(solution)/shard_map/ppermute | solution.py:287
  10.6 0.8 %collective-permute-start.1 = (bf16[64,1024]{1,0:T(8,128)(2,1)S(1)}, bf16[64,1024]{1,0:T(8,128)(2,1)S(1)}, u32[]{:S(2)}, u32[]{:S(2)}) collective-permute-start(bf16[64,1024]{1,0:T(8,128)(2,1)S(1)} %collective-permute-done.refs_3_), channel_id=1, source_target_pairs={{0,4},{4,0},{8,12},{12,8},{1,5},{5,1},{9,13},{13,9},{2,6},{6,2},{1... | collective-permute-start | bytes 393224 | tf_op jit(solution)/shard_map/ppermute | solution.py:287
  11.4 1.2 %collective-permute-start.2 = (bf16[64,1024]{1,0:T(8,128)(2,1)S(1)}, bf16[64,1024]{1,0:T(8,128)(2,1)S(1)}, u32[]{:S(2)}, u32[]{:S(2)}) collective-permute-start(bf16[64,1024]{1,0:T(8,128)(2,1)S(1)} %copy-done.1), channel_id=1, source_target_pairs={{0,4},{4,0},{8,12},{12,8},{1,5},{5,1},{9,13},{13,9},{2,6},{6,2},{1... | collective-permute-start | bytes 393224 | tf_op jit(solution)/shard_map/ppermute | solution.py:287
  12.6 1.6 %attend.4.refs_4_ = bf16[64,1152]{1,0:T(8,128)(2,1)S(1)} custom-call(f32[16,256]{1,0:T(8,128)S(1)} %get-tuple-element.22.refs_0_, bf16[4864,256]{1,0:T(8,128)(2,1)S(1)} %get-tuple-element.23.refs_1_, bf16[4864,256]{1,0:T(8,128)(2,1)S(1)} %get-tuple-element.24.refs_2_, bf16[64,1024]{1,0:T(8,128)(2,1)S(1)} %collective-permute-done.refs_3_, ...), custom_call_target="tpu_custom_call" | custom-call | flops 67108864 | tf_op jit(solution)/shard_map/attend/pallas_call | solution.py:223
  14.2 2.2 %collective-permute-start.4 = (bf16[64,1152]{1,0:T(8,128)(2,1)S(1)}, bf16[64,1152]{1,0:T(8,128)(2,1)S(1)}, u32[]{:S(2)}, u32[]{:S(2)}) collective-permute-start(bf16[64,1152]{1,0:T(8,128)(2,1)S(1)} %attend.4.refs_4_), channel_id=1, source_target_pairs={{0,8},{4,12},{8,0},{12,4},{1,9},{5,13},{9,1},{13,5},{2,10},{6,14},... | collective-permute-start | bytes 442376 | tf_op jit(solution)/shard_map/ppermute | solution.py:287
  16.6 1.7 %attend.5.refs_0_.refs_4_ = bf16[64,1152]{1,0:T(8,128)(2,1)S(1)} custom-call(f32[16,256]{1,0:T(8,128)S(1)} %get-tuple-element.22.refs_0_, bf16[4864,256]{1,0:T(8,128)(2,1)S(1)} %get-tuple-element.23.refs_1_, bf16[4864,256]{1,0:T(8,128)(2,1)S(1)} %get-tuple-element.24.refs_2_, bf16[64,1024]{1,0:T(8,128)(2,1)S(1)} %collective-permute-done.1.refs_3_, ...), custom_call_target="tpu_custom_call" | custom-call | flops 67108864 | tf_op jit(solution)/shard_map/attend/pallas_call | solution.py:223
  18.3 4.6 %collective-permute-start.3 = (bf16[64,1152]{1,0:T(8,128)(2,1)S(1)}, bf16[64,1152]{1,0:T(8,128)(2,1)S(1)}, u32[]{:S(2)}, u32[]{:S(2)}) collective-permute-start(bf16[64,1152]{1,0:T(8,128)(2,1)S(1)} %attend.5.refs_0_.refs_4_), channel_id=1, source_target_pairs={{0,12},{4,8},{8,4},{12,0},{1,13},{5,9},{9,5},{13,1},{2,14},{6,10},... | collective-permute-start | bytes 442376 | tf_op jit(solution)/shard_map/ppermute | solution.py:287
  22.9 1.7 %prepare.3 = (bf16[4864,256]{1,0:T(8,128)(2,1)S(1)}, bf16[4864,256]{1,0:T(8,128)(2,1)S(1)}, f32[16,256]{1,0:T(8,128)S(1)}) custom-call(s32[2,39]{1,0:T(2,128)S(1)} %lists.1.lists_ref.refs_4_, bf16[4096,2,256]{2,1,0:T(2,128)(2,1)S(1)} %copy-done.2, bf16[256,2,256]{2,1,0:T(2,128)(2,1)S(1)} %copy-done.3, bf16[64,2,256]{2,1,0:T(2,128)(2,1)S(1)} %copy-done.4, ...), custom_call_target="tpu_custom_call" | custom-call | flops 4294967296 | bytes 12582912 | tf_op jit(solution)/shard_map/prepare/pallas_call | solution.py:124
  24.6 2.3 %attend.6.refs_4_ = bf16[64,1152]{1,0:T(8,128)(2,1)S(1)} custom-call(f32[16,256]{1,0:T(8,128)S(1)} %get-tuple-element.26.refs_0_, bf16[4864,256]{1,0:T(8,128)(2,1)S(1)} %get-tuple-element.27.refs_1_, bf16[4864,256]{1,0:T(8,128)(2,1)S(1)} %get-tuple-element.28.refs_2_, bf16[64,1024]{1,0:T(8,128)(2,1)S(1)} %collective-permute-done.2.refs_1_.refs_3_, ...), custom_call_target="tpu_custom_call" | custom-call | flops 67108864 | tf_op jit(solution)/shard_map/attend/pallas_call | solution.py:223
  27.0 2.1 %attend.7.refs_0_ = bf16[64,1152]{1,0:T(8,128)(2,1)S(1)} custom-call(f32[16,256]{1,0:T(8,128)S(1)} %get-tuple-element.26.refs_0_, bf16[4864,256]{1,0:T(8,128)(2,1)S(1)} %get-tuple-element.27.refs_1_, bf16[4864,256]{1,0:T(8,128)(2,1)S(1)} %get-tuple-element.28.refs_2_, bf16[64,1024]{1,0:T(8,128)(2,1)S(1)} %copy-done.1, bf16[64,1152]{1,0:T(8,128)(2,1)S(1)} %attend.6.refs_4_), custom_call_target="tpu_custom_call" | custom-call | flops 67108864 | tf_op jit(solution)/shard_map/attend/pallas_call | solution.py:223
  29.1 3.0 %collective-permute-done.5.refs_3_ = bf16[64,1152]{1,0:T(8,128)(2,1)S(1)} collective-permute-done((bf16[64,1152]{1,0:T(8,128)(2,1)S(1)}, bf16[64,1152]{1,0:T(8,128)(2,1)S(1)}, u32[]{:S(2)}, u32[]{:S(2)}) %collective-permute-start.5) | collective-permute-done | bytes 147488 | tf_op jit(solution)/shard_map/ppermute | solution.py:287
  32.7 0.8 %collective-permute-start.8 = (bf16[64,1024]{1,0:T(8,128)(2,1)S(1)}, bf16[64,1024]{1,0:T(8,128)(2,1)S(1)}, u32[]{:S(2)}, u32[]{:S(2)}) collective-permute-start(bf16[64,1024]{1,0:T(8,128)(2,1)S(1)} %merge.1), channel_id=1, source_target_pairs={{0,8},{4,12},{8,0},{12,4},{1,9},{5,13},{9,1},{13,5},{2,10},{6,14},... | collective-permute-start | bytes 393224 | tf_op jit(solution)/shard_map/ppermute | solution.py:287
  33.5 1.4 %collective-permute-start.6 = (bf16[64,1024]{1,0:T(8,128)(2,1)S(1)}, bf16[64,1024]{1,0:T(8,128)(2,1)S(1)}, u32[]{:S(2)}, u32[]{:S(2)}) collective-permute-start(bf16[64,1024]{1,0:T(8,128)(2,1)S(1)} %merge.1), channel_id=1, source_target_pairs={{0,4},{4,0},{8,12},{12,8},{1,5},{5,1},{9,13},{13,9},{2,6},{6,2},{1... | collective-permute-start | bytes 393224 | tf_op jit(solution)/shard_map/ppermute | solution.py:287
  34.9 4.9 %collective-permute-done.8 = bf16[64,1024]{1,0:T(8,128)(2,1)S(1)} collective-permute-done((bf16[64,1024]{1,0:T(8,128)(2,1)S(1)}, bf16[64,1024]{1,0:T(8,128)(2,1)S(1)}, u32[]{:S(2)}, u32[]{:S(2)}) %collective-permute-start.8) | collective-permute-done | bytes 131104 | tf_op jit(solution)/shard_map/ppermute | solution.py:287
  41.3 3.5 %collective-permute-done.9 = bf16[64,1024]{1,0:T(8,128)(2,1)S(1)} collective-permute-done((bf16[64,1024]{1,0:T(8,128)(2,1)S(1)}, bf16[64,1024]{1,0:T(8,128)(2,1)S(1)}, u32[]{:S(2)}, u32[]{:S(2)}) %collective-permute-start.9) | collective-permute-done | bytes 131104 | tf_op jit(solution)/shard_map/ppermute | solution.py:287
  45.8 0.8 %collective-permute-done.10 = bf16[64,1024]{1,0:T(8,128)(2,1)S(1)} collective-permute-done((bf16[64,1024]{1,0:T(8,128)(2,1)S(1)}, bf16[64,1024]{1,0:T(8,128)(2,1)S(1)}, u32[]{:S(2)}, u32[]{:S(2)}) %collective-permute-start.10) | collective-permute-done | bytes 131104 | tf_op jit(solution)/shard_map/ppermute | solution.py:287
  46.7 1.6 %collective-permute-start.11 = (bf16[64,1024]{1,0:T(8,128)(2,1)S(1)}, bf16[64,1024]{1,0:T(8,128)(2,1)S(1)}, u32[]{:S(2)}, u32[]{:S(2)}) collective-permute-start(bf16[64,1024]{1,0:T(8,128)(2,1)S(1)} %select_convert_fusion), channel_id=1, source_target_pairs={{0,2},{1,3},{2,0},{3,1},{4,6},{5,7},{6,4},{7,5},{8,10},{9,11},{10,... | collective-permute-start | bytes 393224 | tf_op jit(solution)/shard_map/ppermute | solution.py:287
  48.3 4.0 %collective-permute-done.11 = bf16[64,1024]{1,0:T(8,128)(2,1)S(1)} collective-permute-done((bf16[64,1024]{1,0:T(8,128)(2,1)S(1)}, bf16[64,1024]{1,0:T(8,128)(2,1)S(1)}, u32[]{:S(2)}, u32[]{:S(2)}) %collective-permute-start.11) | collective-permute-done | bytes 131104 | tf_op jit(solution)/shard_map/ppermute | solution.py:287
  52.4 0.8 %convert_add_fusion = f32[64,1024]{1,0:T(8,128)} fusion(bf16[64,1024]{1,0:T(8,128)(2,1)S(1)} %collective-permute-done.11, f32[64,1024]{1,0:T(8,128)S(1)} %fusion.3, bf16[64,1024]{1,0:T(8,128)(2,1)S(1)} %collective-permute-done.7, f32[64,1024]{1,0:T(8,128)S(1)} %fusion, bf16[64,1024]{1,0:T(8,128)(2,1)S(1)} %collective-permute-done.10, pred[]{:T(512)S(6)} %eq.13), kind=kLoop, calls=%fused_computation.2 | loop fusion | flops 458752 | bytes 1179649 | tf_op jit(solution)/shard_map/add | solution.py:347
  (25 shorter events, 3.4 us)
Async XLA Ops:
  0.0 40.3 %copy-start = (bf16[1024,1024]{1,0:T(8,128)(2,1)S(1)}, bf16[1024,1024]{1,0:T(8,128)(2,1)}, u32[]{:S(2)}) copy-start(bf16[1024,1024]{1,0:T(8,128)(2,1)} %param.15) | copy-start | bytes 6291460
  0.0 10.5 %collective-permute-start = (bf16[64,1024]{1,0:T(8,128)(2,1)}, bf16[64,1024]{1,0:T(8,128)(2,1)S(1)}, u32[]{:S(2)}, u32[]{:S(2)}) collective-permute-start(bf16[64,1024]{1,0:T(8,128)(2,1)} %refs_3_.1), channel_id=1, source_target_pairs={{0,8},{4,12},{8,0},{12,4},{1,9},{5,13},{9,1},{13,5},{2,10},{6,14},... | collective-permute-start | bytes 393224 | tf_op jit(solution)/shard_map/ppermute | solution.py:287
  6.0 2.2 %copy-start.2 = (bf16[4096,2,256]{2,1,0:T(2,128)(2,1)S(1)}, bf16[4096,2,256]{2,1,0:T(2,128)(2,1)}, u32[]{:S(2)}) copy-start(bf16[4096,2,256]{2,1,0:T(2,128)(2,1)} %cache_ref.3) | copy-start | bytes 12582916
  6.0 2.2 %copy-start.3 = (bf16[256,2,256]{2,1,0:T(2,128)(2,1)S(1)}, bf16[256,2,256]{2,1,0:T(2,128)(2,1)}, u32[]{:S(2)}) copy-start(bf16[256,2,256]{2,1,0:T(2,128)(2,1)} %fin_ref.3) | copy-start | bytes 786436
  6.0 2.2 %copy-start.4 = (bf16[64,2,256]{2,1,0:T(2,128)(2,1)S(1)}, bf16[64,2,256]{2,1,0:T(2,128)(2,1)}, u32[]{:S(2)}) copy-start(bf16[64,2,256]{2,1,0:T(2,128)(2,1)} %own_ref.3) | copy-start | bytes 196612
  8.2 3.1 %copy-start.1 = (bf16[64,1024]{1,0:T(8,128)(2,1)S(1)}, bf16[64,1024]{1,0:T(8,128)(2,1)}, u32[]{:S(2)}) copy-start(bf16[64,1024]{1,0:T(8,128)(2,1)} %refs_3_.1) | copy-start | bytes 393220
  10.6 6.1 %collective-permute-start.1 = (bf16[64,1024]{1,0:T(8,128)(2,1)S(1)}, bf16[64,1024]{1,0:T(8,128)(2,1)S(1)}, u32[]{:S(2)}, u32[]{:S(2)}) collective-permute-start(bf16[64,1024]{1,0:T(8,128)(2,1)S(1)} %collective-permute-done.refs_3_), channel_id=1, source_target_pairs={{0,4},{4,0},{8,12},{12,8},{1,5},{5,1},{9,13},{13,9},{2,6},{6,2},{1... | collective-permute-start | bytes 393224 | tf_op jit(solution)/shard_map/ppermute | solution.py:287
  11.4 11.5 %collective-permute-start.2 = (bf16[64,1024]{1,0:T(8,128)(2,1)S(1)}, bf16[64,1024]{1,0:T(8,128)(2,1)S(1)}, u32[]{:S(2)}, u32[]{:S(2)}) collective-permute-start(bf16[64,1024]{1,0:T(8,128)(2,1)S(1)} %copy-done.1), channel_id=1, source_target_pairs={{0,4},{4,0},{8,12},{12,8},{1,5},{5,1},{9,13},{13,9},{2,6},{6,2},{1... | collective-permute-start | bytes 393224 | tf_op jit(solution)/shard_map/ppermute | solution.py:287
  14.2 14.9 %collective-permute-start.4 = (bf16[64,1152]{1,0:T(8,128)(2,1)S(1)}, bf16[64,1152]{1,0:T(8,128)(2,1)S(1)}, u32[]{:S(2)}, u32[]{:S(2)}) collective-permute-start(bf16[64,1152]{1,0:T(8,128)(2,1)S(1)} %attend.4.refs_4_), channel_id=1, source_target_pairs={{0,8},{4,12},{8,0},{12,4},{1,9},{5,13},{9,1},{13,5},{2,10},{6,14},... | collective-permute-start | bytes 442376 | tf_op jit(solution)/shard_map/ppermute | solution.py:287
  18.3 10.8 %collective-permute-start.3 = (bf16[64,1152]{1,0:T(8,128)(2,1)S(1)}, bf16[64,1152]{1,0:T(8,128)(2,1)S(1)}, u32[]{:S(2)}, u32[]{:S(2)}) collective-permute-start(bf16[64,1152]{1,0:T(8,128)(2,1)S(1)} %attend.5.refs_0_.refs_4_), channel_id=1, source_target_pairs={{0,12},{4,8},{8,4},{12,0},{1,13},{5,9},{9,5},{13,1},{2,14},{6,10},... | collective-permute-start | bytes 442376 | tf_op jit(solution)/shard_map/ppermute | solution.py:287
  26.9 5.2 %collective-permute-start.5 = (bf16[64,1152]{1,0:T(8,128)(2,1)S(1)}, bf16[64,1152]{1,0:T(8,128)(2,1)S(1)}, u32[]{:S(2)}, u32[]{:S(2)}) collective-permute-start(bf16[64,1152]{1,0:T(8,128)(2,1)S(1)} %attend.6.refs_4_), channel_id=1, source_target_pairs={{0,4},{4,0},{8,12},{12,8},{1,5},{5,1},{9,13},{13,9},{2,6},{6,2},{1... | collective-permute-start | bytes 442376 | tf_op jit(solution)/shard_map/ppermute | solution.py:287
  32.7 7.1 %collective-permute-start.8 = (bf16[64,1024]{1,0:T(8,128)(2,1)S(1)}, bf16[64,1024]{1,0:T(8,128)(2,1)S(1)}, u32[]{:S(2)}, u32[]{:S(2)}) collective-permute-start(bf16[64,1024]{1,0:T(8,128)(2,1)S(1)} %merge.1), channel_id=1, source_target_pairs={{0,8},{4,12},{8,0},{12,4},{1,9},{5,13},{9,1},{13,5},{2,10},{6,14},... | collective-permute-start | bytes 393224 | tf_op jit(solution)/shard_map/ppermute | solution.py:287
  33.5 6.8 %collective-permute-start.6 = (bf16[64,1024]{1,0:T(8,128)(2,1)S(1)}, bf16[64,1024]{1,0:T(8,128)(2,1)S(1)}, u32[]{:S(2)}, u32[]{:S(2)}) collective-permute-start(bf16[64,1024]{1,0:T(8,128)(2,1)S(1)} %merge.1), channel_id=1, source_target_pairs={{0,4},{4,0},{8,12},{12,8},{1,5},{5,1},{9,13},{13,9},{2,6},{6,2},{1... | collective-permute-start | bytes 393224 | tf_op jit(solution)/shard_map/ppermute | solution.py:287
  39.8 5.0 %collective-permute-start.9 = (bf16[64,1024]{1,0:T(8,128)(2,1)S(1)}, bf16[64,1024]{1,0:T(8,128)(2,1)S(1)}, u32[]{:S(2)}, u32[]{:S(2)}) collective-permute-start(bf16[64,1024]{1,0:T(8,128)(2,1)S(1)} %collective-permute-done.8), channel_id=1, source_target_pairs={{0,4},{4,0},{8,12},{12,8},{1,5},{5,1},{9,13},{13,9},{2,6},{6,2},{1... | collective-permute-start | bytes 393224 | tf_op jit(solution)/shard_map/ppermute | solution.py:287
  41.2 5.4 %collective-permute-start.7 = (bf16[64,1024]{1,0:T(8,128)(2,1)S(1)}, bf16[64,1024]{1,0:T(8,128)(2,1)S(1)}, u32[]{:S(2)}, u32[]{:S(2)}) collective-permute-start(bf16[64,1024]{1,0:T(8,128)(2,1)S(1)} %convolution_convert_fusion.1), channel_id=1, source_target_pairs={{0,1},{1,0},{2,3},{3,2},{4,5},{5,4},{6,7},{7,6},{8,9},{9,8},{10,11... | collective-permute-start | bytes 393224 | tf_op jit(solution)/shard_map/ppermute | solution.py:287
  45.3 1.4 %collective-permute-start.10 = (bf16[64,1024]{1,0:T(8,128)(2,1)S(1)}, bf16[64,1024]{1,0:T(8,128)(2,1)S(1)}, u32[]{:S(2)}, u32[]{:S(2)}) collective-permute-start(bf16[64,1024]{1,0:T(8,128)(2,1)S(1)} %convolution_convert_fusion), channel_id=1, source_target_pairs={{0,1},{1,0},{2,3},{3,2},{4,5},{5,4},{6,7},{7,6},{8,9},{9,8},{10,11... | collective-permute-start | bytes 393224 | tf_op jit(solution)/shard_map/ppermute | solution.py:287
  46.7 5.6 %collective-permute-start.11 = (bf16[64,1024]{1,0:T(8,128)(2,1)S(1)}, bf16[64,1024]{1,0:T(8,128)(2,1)S(1)}, u32[]{:S(2)}, u32[]{:S(2)}) collective-permute-start(bf16[64,1024]{1,0:T(8,128)(2,1)S(1)} %select_convert_fusion), channel_id=1, source_target_pairs={{0,2},{1,3},{2,0},{3,1},{4,6},{5,7},{6,4},{7,5},{8,10},{9,11},{10,... | collective-permute-start | bytes 393224 | tf_op jit(solution)/shard_map/ppermute | solution.py:287

commit v7 on v6

--- a/solution.py
+++ b/solution.py
@@ -19,7 +19,7 @@
 
 
 VMEM_LIMIT = 26 << 20
-UNROLL = 4
+UNROLL = 6
 
 
 def params():

time: 53.4 us -> 53.4 us (level); the launches traced: 53.1 us -> 53.7 us
  Pallas kernels: 12.9 us -> 15 us
  starting transfers between devices: 17.3 us -> 16.1 us
    pallas_call x4, Pallas kernels: 7.65 us -> 9.32 us  [attend(): pl.pallas_call(functools.partial(attend_body, (kv, group, tokens, n)), in...]
    ppermute x12, starting transfers between devices: 17.3 us -> 16.1 us  [swap(): return lax.ppermute(value, axis, [(i, i ^ k) for i in range(size)])]
  transfers between devices with their start and end apart: 12 -> 12, of which waited for: 7 -> 6; matrix products, arithmetic and copies ran while one was open for 5% -> 5% of each run, Pallas kernels for 23% -> 27%
where the time goes in v7:
time: 53.4 us; the launch traced here: 53.7 us
  waiting for transfers between devices  17.2 us (32%)
  starting transfers between devices  16.1 us (30%)
  Pallas kernels  15 us (28%)
  matrix products  1.91 us (4%)
  other arithmetic  1.52 us (3%)
  between operations  1.45 us (3%)
  local copies, waits for them, and re-layouts  0.59 us (1%)
    ppermute x12, waiting for transfers between devices, swap(): return lax.ppermute(value, axis, [(i, i ^ k) for i in range(size)])  17.2 us
    ppermute x12, starting transfers between devices, swap(): return lax.ppermute(value, axis, [(i, i ^ k) for i in range(size)])  16.1 us
    pallas_call x4, Pallas kernels, attend(): pl.pallas_call(functools.partial(attend_body, (kv, group, tokens, n)), in...  9.32 us
    pallas_call x2, Pallas kernels, prepare(): pl.pallas_call(functools.partial(prepare_body, at), in_specs=[vmem_spec()...  3.54 us
    dot_general x4, matrix products, project(): return jnp.dot(rows, output_weight, preferred_element_type=F32)  1.91 us
    pallas_call x1, Pallas kernels, make_lists(): pl.pallas_call(functools.partial(list_body, axis, own_tokens, shards, fin...  1.61 us
  transfers between devices with their start and end apart: 12, of which 6 were waited for; matrix products, arithmetic and copies ran while one was open for 5% of the time, Pallas kernels for 27%

profile of v7, /device:TPU:0, one launch (start us, length us, event | category | flops | bytes accessed | tf_op | source)
XLA Modules:
  0.0 53.7 jit_solution(4743195128009876247)
XLA Ops:
  0.0 4.0 %collective-permute-start = (bf16[64,1024]{1,0:T(8,128)(2,1)}, bf16[64,1024]{1,0:T(8,128)(2,1)S(1)}, u32[]{:S(2)}, u32[]{:S(2)}) collective-permute-start(bf16[64,1024]{1,0:T(8,128)(2,1)} %refs_3_.1), channel_id=1, source_target_pairs={{0,8},{4,12},{8,0},{12,4},{1,9},{5,13},{9,1},{13,5},{2,10},{6,14},... | collective-permute-start | bytes 393224 | tf_op jit(solution)/shard_map/ppermute | solution.py:287
  5.3 0.7 %pad_add_fusion.meta_ref = s32[4,32]{1,0:T(4,128)S(1)} fusion(s32[1,1]{1,0:T(1,128)} %bitcast.7, s32[1,1]{1,0:T(1,128)} %bitcast.6, s32[2,32]{1,0:T(2,128)} %param.12), kind=kLoop, calls=%fused_computation.16 | loop fusion | flops 256 | bytes 776 | tf_op jit(solution)/shard_map/concatenate | solution.py:63
  6.0 1.6 %lists.1.lists_ref.refs_4_ = s32[2,41]{1,0:T(2,128)S(1)} custom-call(s32[4,32]{1,0:T(4,128)S(1)} %pad_add_fusion.meta_ref), custom_call_target="tpu_custom_call" | custom-call | flops 4294967296 | tf_op jit(solution)/shard_map/lists/pallas_call | solution.py:64
  7.7 0.6 %copy-done.2 = bf16[4096,2,256]{2,1,0:T(2,128)(2,1)S(1)} copy-done((bf16[4096,2,256]{2,1,0:T(2,128)(2,1)S(1)}, bf16[4096,2,256]{2,1,0:T(2,128)(2,1)}, u32[]{:S(2)}) %copy-start.2) | copy-done | bytes 4194328
  8.2 1.5 %prepare.2 = (bf16[5120,256]{1,0:T(8,128)(2,1)S(1)}, bf16[5120,256]{1,0:T(8,128)(2,1)S(1)}, f32[16,256]{1,0:T(8,128)S(1)}) custom-call(s32[2,41]{1,0:T(2,128)S(1)} %lists.1.lists_ref.refs_4_, bf16[4096,2,256]{2,1,0:T(2,128)(2,1)S(1)} %copy-done.2, bf16[256,2,256]{2,1,0:T(2,128)(2,1)S(1)} %copy-done.3, bf16[64,2,256]{2,1,0:T(2,128)(2,1)S(1)} %copy-done.4), custom_call_target="tpu_custom_call" | custom-call | flops 4294967296 | bytes 12582912 | tf_op jit(solution)/shard_map/prepare/pallas_call | solution.py:124
  9.8 0.8 %collective-permute-done.refs_3_ = bf16[64,1024]{1,0:T(8,128)(2,1)S(1)} collective-permute-done((bf16[64,1024]{1,0:T(8,128)(2,1)}, bf16[64,1024]{1,0:T(8,128)(2,1)S(1)}, u32[]{:S(2)}, u32[]{:S(2)}) %collective-permute-start) | collective-permute-done | bytes 131104 | tf_op jit(solution)/shard_map/ppermute | solution.py:287
  10.6 0.9 %collective-permute-start.1 = (bf16[64,1024]{1,0:T(8,128)(2,1)S(1)}, bf16[64,1024]{1,0:T(8,128)(2,1)S(1)}, u32[]{:S(2)}, u32[]{:S(2)}) collective-permute-start(bf16[64,1024]{1,0:T(8,128)(2,1)S(1)} %collective-permute-done.refs_3_), channel_id=1, source_target_pairs={{0,4},{4,0},{8,12},{12,8},{1,5},{5,1},{9,13},{13,9},{2,6},{6,2},{1... | collective-permute-start | bytes 393224 | tf_op jit(solution)/shard_map/ppermute | solution.py:287
  11.4 1.1 %collective-permute-start.2 = (bf16[64,1024]{1,0:T(8,128)(2,1)S(1)}, bf16[64,1024]{1,0:T(8,128)(2,1)S(1)}, u32[]{:S(2)}, u32[]{:S(2)}) collective-permute-start(bf16[64,1024]{1,0:T(8,128)(2,1)S(1)} %copy-done.1), channel_id=1, source_target_pairs={{0,4},{4,0},{8,12},{12,8},{1,5},{5,1},{9,13},{13,9},{2,6},{6,2},{1... | collective-permute-start | bytes 393224 | tf_op jit(solution)/shard_map/ppermute | solution.py:287
  12.6 2.1 %attend.4.refs_4_ = bf16[64,1152]{1,0:T(8,128)(2,1)S(1)} custom-call(f32[16,256]{1,0:T(8,128)S(1)} %get-tuple-element.22.refs_0_, bf16[5120,256]{1,0:T(8,128)(2,1)S(1)} %get-tuple-element.23.refs_1_, bf16[5120,256]{1,0:T(8,128)(2,1)S(1)} %get-tuple-element.24.refs_2_, bf16[64,1024]{1,0:T(8,128)(2,1)S(1)} %collective-permute-done.refs_3_, ...), custom_call_target="tpu_custom_call" | custom-call | flops 67108864 | tf_op jit(solution)/shard_map/attend/pallas_call | solution.py:223
  14.7 2.2 %collective-permute-start.4 = (bf16[64,1152]{1,0:T(8,128)(2,1)S(1)}, bf16[64,1152]{1,0:T(8,128)(2,1)S(1)}, u32[]{:S(2)}, u32[]{:S(2)}) collective-permute-start(bf16[64,1152]{1,0:T(8,128)(2,1)S(1)} %attend.4.refs_4_), channel_id=1, source_target_pairs={{0,8},{4,12},{8,0},{12,4},{1,9},{5,13},{9,1},{13,5},{2,10},{6,14},... | collective-permute-start | bytes 442376 | tf_op jit(solution)/shard_map/ppermute | solution.py:287
  16.9 2.1 %attend.5.refs_0_.refs_4_ = bf16[64,1152]{1,0:T(8,128)(2,1)S(1)} custom-call(f32[16,256]{1,0:T(8,128)S(1)} %get-tuple-element.22.refs_0_, bf16[5120,256]{1,0:T(8,128)(2,1)S(1)} %get-tuple-element.23.refs_1_, bf16[5120,256]{1,0:T(8,128)(2,1)S(1)} %get-tuple-element.24.refs_2_, bf16[64,1024]{1,0:T(8,128)(2,1)S(1)} %collective-permute-done.1.refs_3_, ...), custom_call_target="tpu_custom_call" | custom-call | flops 67108864 | tf_op jit(solution)/shard_map/attend/pallas_call | solution.py:223
  19.0 3.9 %collective-permute-start.3 = (bf16[64,1152]{1,0:T(8,128)(2,1)S(1)}, bf16[64,1152]{1,0:T(8,128)(2,1)S(1)}, u32[]{:S(2)}, u32[]{:S(2)}) collective-permute-start(bf16[64,1152]{1,0:T(8,128)(2,1)S(1)} %attend.5.refs_0_.refs_4_), channel_id=1, source_target_pairs={{0,12},{4,8},{8,4},{12,0},{1,13},{5,9},{9,5},{13,1},{2,14},{6,10},... | collective-permute-start | bytes 442376 | tf_op jit(solution)/shard_map/ppermute | solution.py:287
  22.9 2.0 %prepare.3 = (bf16[5120,256]{1,0:T(8,128)(2,1)S(1)}, bf16[5120,256]{1,0:T(8,128)(2,1)S(1)}, f32[16,256]{1,0:T(8,128)S(1)}) custom-call(s32[2,41]{1,0:T(2,128)S(1)} %lists.1.lists_ref.refs_4_, bf16[4096,2,256]{2,1,0:T(2,128)(2,1)S(1)} %copy-done.2, bf16[256,2,256]{2,1,0:T(2,128)(2,1)S(1)} %copy-done.3, bf16[64,2,256]{2,1,0:T(2,128)(2,1)S(1)} %copy-done.4, ...), custom_call_target="tpu_custom_call" | custom-call | flops 4294967296 | bytes 12582912 | tf_op jit(solution)/shard_map/prepare/pallas_call | solution.py:124
  24.9 2.7 %attend.6.refs_4_ = bf16[64,1152]{1,0:T(8,128)(2,1)S(1)} custom-call(f32[16,256]{1,0:T(8,128)S(1)} %get-tuple-element.26.refs_0_, bf16[5120,256]{1,0:T(8,128)(2,1)S(1)} %get-tuple-element.27.refs_1_, bf16[5120,256]{1,0:T(8,128)(2,1)S(1)} %get-tuple-element.28.refs_2_, bf16[64,1024]{1,0:T(8,128)(2,1)S(1)} %collective-permute-done.2.refs_1_.refs_3_, ...), custom_call_target="tpu_custom_call" | custom-call | flops 67108864 | tf_op jit(solution)/shard_map/attend/pallas_call | solution.py:223
  27.7 2.5 %attend.7.refs_0_ = bf16[64,1152]{1,0:T(8,128)(2,1)S(1)} custom-call(f32[16,256]{1,0:T(8,128)S(1)} %get-tuple-element.26.refs_0_, bf16[5120,256]{1,0:T(8,128)(2,1)S(1)} %get-tuple-element.27.refs_1_, bf16[5120,256]{1,0:T(8,128)(2,1)S(1)} %get-tuple-element.28.refs_2_, bf16[64,1024]{1,0:T(8,128)(2,1)S(1)} %copy-done.1, bf16[64,1152]{1,0:T(8,128)(2,1)S(1)} %attend.6.refs_4_), custom_call_target="tpu_custom_call" | custom-call | flops 67108864 | tf_op jit(solution)/shard_map/attend/pallas_call | solution.py:223
  30.2 2.6 %collective-permute-done.5.refs_3_ = bf16[64,1152]{1,0:T(8,128)(2,1)S(1)} collective-permute-done((bf16[64,1152]{1,0:T(8,128)(2,1)S(1)}, bf16[64,1152]{1,0:T(8,128)(2,1)S(1)}, u32[]{:S(2)}, u32[]{:S(2)}) %collective-permute-start.5) | collective-permute-done | bytes 147488 | tf_op jit(solution)/shard_map/ppermute | solution.py:287
  32.8 0.5 merge.1
  33.7 1.4 %collective-permute-start.6 = (bf16[64,1024]{1,0:T(8,128)(2,1)S(1)}, bf16[64,1024]{1,0:T(8,128)(2,1)S(1)}, u32[]{:S(2)}, u32[]{:S(2)}) collective-permute-start(bf16[64,1024]{1,0:T(8,128)(2,1)S(1)} %merge.1), channel_id=1, source_target_pairs={{0,4},{4,0},{8,12},{12,8},{1,5},{5,1},{9,13},{13,9},{2,6},{6,2},{1... | collective-permute-start | bytes 393224 | tf_op jit(solution)/shard_map/ppermute | solution.py:287
  35.1 5.3 %collective-permute-done.8 = bf16[64,1024]{1,0:T(8,128)(2,1)S(1)} collective-permute-done((bf16[64,1024]{1,0:T(8,128)(2,1)S(1)}, bf16[64,1024]{1,0:T(8,128)(2,1)S(1)}, u32[]{:S(2)}, u32[]{:S(2)}) %collective-permute-start.8) | collective-permute-done | bytes 131104 | tf_op jit(solution)/shard_map/ppermute | solution.py:287
  41.8 3.6 %collective-permute-done.9 = bf16[64,1024]{1,0:T(8,128)(2,1)S(1)} collective-permute-done((bf16[64,1024]{1,0:T(8,128)(2,1)S(1)}, bf16[64,1024]{1,0:T(8,128)(2,1)S(1)}, u32[]{:S(2)}, u32[]{:S(2)}) %collective-permute-start.9) | collective-permute-done | bytes 131104 | tf_op jit(solution)/shard_map/ppermute | solution.py:287
  46.4 0.8 %collective-permute-done.10 = bf16[64,1024]{1,0:T(8,128)(2,1)S(1)} collective-permute-done((bf16[64,1024]{1,0:T(8,128)(2,1)S(1)}, bf16[64,1024]{1,0:T(8,128)(2,1)S(1)}, u32[]{:S(2)}, u32[]{:S(2)}) %collective-permute-start.10) | collective-permute-done | bytes 131104 | tf_op jit(solution)/shard_map/ppermute | solution.py:287
  47.3 1.5 %collective-permute-start.11 = (bf16[64,1024]{1,0:T(8,128)(2,1)S(1)}, bf16[64,1024]{1,0:T(8,128)(2,1)S(1)}, u32[]{:S(2)}, u32[]{:S(2)}) collective-permute-start(bf16[64,1024]{1,0:T(8,128)(2,1)S(1)} %select_convert_fusion), channel_id=1, source_target_pairs={{0,2},{1,3},{2,0},{3,1},{4,6},{5,7},{6,4},{7,5},{8,10},{9,11},{10,... | collective-permute-start | bytes 393224 | tf_op jit(solution)/shard_map/ppermute | solution.py:287
  48.9 4.1 %collective-permute-done.11 = bf16[64,1024]{1,0:T(8,128)(2,1)S(1)} collective-permute-done((bf16[64,1024]{1,0:T(8,128)(2,1)S(1)}, bf16[64,1024]{1,0:T(8,128)(2,1)S(1)}, u32[]{:S(2)}, u32[]{:S(2)}) %collective-permute-start.11) | collective-permute-done | bytes 131104 | tf_op jit(solution)/shard_map/ppermute | solution.py:287
  53.0 0.8 %convert_add_fusion = f32[64,1024]{1,0:T(8,128)} fusion(bf16[64,1024]{1,0:T(8,128)(2,1)S(1)} %collective-permute-done.11, f32[64,1024]{1,0:T(8,128)S(1)} %fusion.3, bf16[64,1024]{1,0:T(8,128)(2,1)S(1)} %collective-permute-done.7, f32[64,1024]{1,0:T(8,128)S(1)} %fusion, bf16[64,1024]{1,0:T(8,128)(2,1)S(1)} %collective-permute-done.10, pred[]{:T(512)S(6)} %eq.13), kind=kLoop, calls=%fused_computation.2 | loop fusion | flops 458752 | bytes 1179649 | tf_op jit(solution)/shard_map/add | solution.py:347
  (25 shorter events, 2.9 us)
Async XLA Ops:
  0.0 40.7 %copy-start = (bf16[1024,1024]{1,0:T(8,128)(2,1)S(1)}, bf16[1024,1024]{1,0:T(8,128)(2,1)}, u32[]{:S(2)}) copy-start(bf16[1024,1024]{1,0:T(8,128)(2,1)} %param.15) | copy-start | bytes 6291460
  0.0 10.5 %collective-permute-start = (bf16[64,1024]{1,0:T(8,128)(2,1)}, bf16[64,1024]{1,0:T(8,128)(2,1)S(1)}, u32[]{:S(2)}, u32[]{:S(2)}) collective-permute-start(bf16[64,1024]{1,0:T(8,128)(2,1)} %refs_3_.1), channel_id=1, source_target_pairs={{0,8},{4,12},{8,0},{12,4},{1,9},{5,13},{9,1},{13,5},{2,10},{6,14},... | collective-permute-start | bytes 393224 | tf_op jit(solution)/shard_map/ppermute | solution.py:287
  6.0 2.2 %copy-start.2 = (bf16[4096,2,256]{2,1,0:T(2,128)(2,1)S(1)}, bf16[4096,2,256]{2,1,0:T(2,128)(2,1)}, u32[]{:S(2)}) copy-start(bf16[4096,2,256]{2,1,0:T(2,128)(2,1)} %cache_ref.3) | copy-start | bytes 12582916
  6.0 2.2 %copy-start.3 = (bf16[256,2,256]{2,1,0:T(2,128)(2,1)S(1)}, bf16[256,2,256]{2,1,0:T(2,128)(2,1)}, u32[]{:S(2)}) copy-start(bf16[256,2,256]{2,1,0:T(2,128)(2,1)} %fin_ref.3) | copy-start | bytes 786436
  6.0 2.2 %copy-start.4 = (bf16[64,2,256]{2,1,0:T(2,128)(2,1)S(1)}, bf16[64,2,256]{2,1,0:T(2,128)(2,1)}, u32[]{:S(2)}) copy-start(bf16[64,2,256]{2,1,0:T(2,128)(2,1)} %own_ref.3) | copy-start | bytes 196612
  8.2 3.2 %copy-start.1 = (bf16[64,1024]{1,0:T(8,128)(2,1)S(1)}, bf16[64,1024]{1,0:T(8,128)(2,1)}, u32[]{:S(2)}) copy-start(bf16[64,1024]{1,0:T(8,128)(2,1)} %refs_3_.1) | copy-start | bytes 393220
  10.6 6.3 %collective-permute-start.1 = (bf16[64,1024]{1,0:T(8,128)(2,1)S(1)}, bf16[64,1024]{1,0:T(8,128)(2,1)S(1)}, u32[]{:S(2)}, u32[]{:S(2)}) collective-permute-start(bf16[64,1024]{1,0:T(8,128)(2,1)S(1)} %collective-permute-done.refs_3_), channel_id=1, source_target_pairs={{0,4},{4,0},{8,12},{12,8},{1,5},{5,1},{9,13},{13,9},{2,6},{6,2},{1... | collective-permute-start | bytes 393224 | tf_op jit(solution)/shard_map/ppermute | solution.py:287
  11.4 11.5 %collective-permute-start.2 = (bf16[64,1024]{1,0:T(8,128)(2,1)S(1)}, bf16[64,1024]{1,0:T(8,128)(2,1)S(1)}, u32[]{:S(2)}, u32[]{:S(2)}) collective-permute-start(bf16[64,1024]{1,0:T(8,128)(2,1)S(1)} %copy-done.1), channel_id=1, source_target_pairs={{0,4},{4,0},{8,12},{12,8},{1,5},{5,1},{9,13},{13,9},{2,6},{6,2},{1... | collective-permute-start | bytes 393224 | tf_op jit(solution)/shard_map/ppermute | solution.py:287
  14.7 15.5 %collective-permute-start.4 = (bf16[64,1152]{1,0:T(8,128)(2,1)S(1)}, bf16[64,1152]{1,0:T(8,128)(2,1)S(1)}, u32[]{:S(2)}, u32[]{:S(2)}) collective-permute-start(bf16[64,1152]{1,0:T(8,128)(2,1)S(1)} %attend.4.refs_4_), channel_id=1, source_target_pairs={{0,8},{4,12},{8,0},{12,4},{1,9},{5,13},{9,1},{13,5},{2,10},{6,14},... | collective-permute-start | bytes 442376 | tf_op jit(solution)/shard_map/ppermute | solution.py:287
  19.0 11.2 %collective-permute-start.3 = (bf16[64,1152]{1,0:T(8,128)(2,1)S(1)}, bf16[64,1152]{1,0:T(8,128)(2,1)S(1)}, u32[]{:S(2)}, u32[]{:S(2)}) collective-permute-start(bf16[64,1152]{1,0:T(8,128)(2,1)S(1)} %attend.5.refs_0_.refs_4_), channel_id=1, source_target_pairs={{0,12},{4,8},{8,4},{12,0},{1,13},{5,9},{9,5},{13,1},{2,14},{6,10},... | collective-permute-start | bytes 442376 | tf_op jit(solution)/shard_map/ppermute | solution.py:287
  27.6 5.2 %collective-permute-start.5 = (bf16[64,1152]{1,0:T(8,128)(2,1)S(1)}, bf16[64,1152]{1,0:T(8,128)(2,1)S(1)}, u32[]{:S(2)}, u32[]{:S(2)}) collective-permute-start(bf16[64,1152]{1,0:T(8,128)(2,1)S(1)} %attend.6.refs_4_), channel_id=1, source_target_pairs={{0,4},{4,0},{8,12},{12,8},{1,5},{5,1},{9,13},{13,9},{2,6},{6,2},{1... | collective-permute-start | bytes 442376 | tf_op jit(solution)/shard_map/ppermute | solution.py:287
  33.3 7.1 %collective-permute-start.8 = (bf16[64,1024]{1,0:T(8,128)(2,1)S(1)}, bf16[64,1024]{1,0:T(8,128)(2,1)S(1)}, u32[]{:S(2)}, u32[]{:S(2)}) collective-permute-start(bf16[64,1024]{1,0:T(8,128)(2,1)S(1)} %merge.1), channel_id=1, source_target_pairs={{0,8},{4,12},{8,0},{12,4},{1,9},{5,13},{9,1},{13,5},{2,10},{6,14},... | collective-permute-start | bytes 393224 | tf_op jit(solution)/shard_map/ppermute | solution.py:287
  33.7 7.1 %collective-permute-start.6 = (bf16[64,1024]{1,0:T(8,128)(2,1)S(1)}, bf16[64,1024]{1,0:T(8,128)(2,1)S(1)}, u32[]{:S(2)}, u32[]{:S(2)}) collective-permute-start(bf16[64,1024]{1,0:T(8,128)(2,1)S(1)} %merge.1), channel_id=1, source_target_pairs={{0,4},{4,0},{8,12},{12,8},{1,5},{5,1},{9,13},{13,9},{2,6},{6,2},{1... | collective-permute-start | bytes 393224 | tf_op jit(solution)/shard_map/ppermute | solution.py:287
  40.4 5.0 %collective-permute-start.9 = (bf16[64,1024]{1,0:T(8,128)(2,1)S(1)}, bf16[64,1024]{1,0:T(8,128)(2,1)S(1)}, u32[]{:S(2)}, u32[]{:S(2)}) collective-permute-start(bf16[64,1024]{1,0:T(8,128)(2,1)S(1)} %collective-permute-done.8), channel_id=1, source_target_pairs={{0,4},{4,0},{8,12},{12,8},{1,5},{5,1},{9,13},{13,9},{2,6},{6,2},{1... | collective-permute-start | bytes 393224 | tf_op jit(solution)/shard_map/ppermute | solution.py:287
  41.7 5.6 %collective-permute-start.7 = (bf16[64,1024]{1,0:T(8,128)(2,1)S(1)}, bf16[64,1024]{1,0:T(8,128)(2,1)S(1)}, u32[]{:S(2)}, u32[]{:S(2)}) collective-permute-start(bf16[64,1024]{1,0:T(8,128)(2,1)S(1)} %convolution_convert_fusion.1), channel_id=1, source_target_pairs={{0,1},{1,0},{2,3},{3,2},{4,5},{5,4},{6,7},{7,6},{8,9},{9,8},{10,11... | collective-permute-start | bytes 393224 | tf_op jit(solution)/shard_map/ppermute | solution.py:287
  45.9 1.4 %collective-permute-start.10 = (bf16[64,1024]{1,0:T(8,128)(2,1)S(1)}, bf16[64,1024]{1,0:T(8,128)(2,1)S(1)}, u32[]{:S(2)}, u32[]{:S(2)}) collective-permute-start(bf16[64,1024]{1,0:T(8,128)(2,1)S(1)} %convolution_convert_fusion), channel_id=1, source_target_pairs={{0,1},{1,0},{2,3},{3,2},{4,5},{5,4},{6,7},{7,6},{8,9},{9,8},{10,11... | collective-permute-start | bytes 393224 | tf_op jit(solution)/shard_map/ppermute | solution.py:287
  47.3 5.6 %collective-permute-start.11 = (bf16[64,1024]{1,0:T(8,128)(2,1)S(1)}, bf16[64,1024]{1,0:T(8,128)(2,1)S(1)}, u32[]{:S(2)}, u32[]{:S(2)}) collective-permute-start(bf16[64,1024]{1,0:T(8,128)(2,1)S(1)} %select_convert_fusion), channel_id=1, source_target_pairs={{0,2},{1,3},{2,0},{3,1},{4,6},{5,7},{6,4},{7,5},{8,10},{9,11},{10,... | collective-permute-start | bytes 393224 | tf_op jit(solution)/shard_map/ppermute | solution.py:287

commit v8 on v7

--- a/solution.py
+++ b/solution.py
@@ -19,7 +19,7 @@
 
 
 VMEM_LIMIT = 26 << 20
-UNROLL = 6
+UNROLL = 8
 
 
 def params():

time: 53.4 us -> 53.1 us (level)
  starting transfers between devices: 16.1 us -> 17 us
  Pallas kernels: 15 us -> 14.2 us
  waiting for transfers between devices: 17.2 us -> 16.6 us
    ppermute x12, starting transfers between devices: 16.1 us -> 17 us  [swap(): return lax.ppermute(value, axis, [(i, i ^ k) for i in range(size)])]
    pallas_call x4, Pallas kernels: 9.32 us -> 8.51 us  [attend(): pl.pallas_call(functools.partial(attend_body, (kv, group, tokens, n)), in...]
    ppermute x12, waiting for transfers between devices: 17.2 us -> 16.6 us  [swap(): return lax.ppermute(value, axis, [(i, i ^ k) for i in range(size)])]
  transfers between devices with their start and end apart: 12 -> 12, of which waited for: 6 -> 6; matrix products, arithmetic and copies ran while one was open for 5% -> 5% of each run, Pallas kernels for 27% -> 26%
where the time goes in v8:
time: 53.1 us; the launch traced here: 53.2 us
  starting transfers between devices  17 us (32%)
  waiting for transfers between devices  16.6 us (31%)
  Pallas kernels  14.2 us (27%)
  matrix products  1.91 us (4%)
  other arithmetic  1.52 us (3%)
  between operations  1.45 us (3%)
  local copies, waits for them, and re-layouts  0.59 us (1%)
    ppermute x12, starting transfers between devices, swap(): return lax.ppermute(value, axis, [(i, i ^ k) for i in range(size)])  17 us
    ppermute x12, waiting for transfers between devices, swap(): return lax.ppermute(value, axis, [(i, i ^ k) for i in range(size)])  16.6 us
    pallas_call x4, Pallas kernels, attend(): pl.pallas_call(functools.partial(attend_body, (kv, group, tokens, n)), in...  8.51 us
    pallas_call x2, Pallas kernels, prepare(): pl.pallas_call(functools.partial(prepare_body, at), in_specs=[vmem_spec()...  3.51 us
    dot_general x4, matrix products, project(): return jnp.dot(rows, output_weight, preferred_element_type=F32)  1.91 us
    pallas_call x1, Pallas kernels, make_lists(): pl.pallas_call(functools.partial(list_body, axis, own_tokens, shards, fin...  1.61 us
  transfers between devices with their start and end apart: 12, of which 6 were waited for; matrix products, arithmetic and copies ran while one was open for 5% of the time, Pallas kernels for 26%

profile of v8, /device:TPU:0, one launch (start us, length us, event | category | flops | bytes accessed | tf_op | source)
XLA Modules:
  0.0 53.2 jit_solution(8066754355718133552)
XLA Ops:
  0.0 4.0 %collective-permute-start = (bf16[64,1024]{1,0:T(8,128)(2,1)}, bf16[64,1024]{1,0:T(8,128)(2,1)S(1)}, u32[]{:S(2)}, u32[]{:S(2)}) collective-permute-start(bf16[64,1024]{1,0:T(8,128)(2,1)} %refs_3_.1), channel_id=1, source_target_pairs={{0,8},{4,12},{8,0},{12,4},{1,9},{5,13},{9,1},{13,5},{2,10},{6,14},... | collective-permute-start | bytes 393224 | tf_op jit(solution)/shard_map/ppermute | solution.py:287
  5.3 0.7 %pad_add_fusion.meta_ref = s32[4,32]{1,0:T(4,128)S(1)} fusion(s32[1,1]{1,0:T(1,128)} %bitcast.7, s32[1,1]{1,0:T(1,128)} %bitcast.6, s32[2,32]{1,0:T(2,128)} %param.12), kind=kLoop, calls=%fused_computation.16 | loop fusion | flops 256 | bytes 776 | tf_op jit(solution)/shard_map/concatenate | solution.py:63
  6.0 1.6 %lists.1.lists_ref.refs_4_ = s32[2,43]{1,0:T(2,128)S(1)} custom-call(s32[4,32]{1,0:T(4,128)S(1)} %pad_add_fusion.meta_ref), custom_call_target="tpu_custom_call" | custom-call | flops 4294967296 | tf_op jit(solution)/shard_map/lists/pallas_call | solution.py:64
  7.7 0.5 %copy-done.2 = bf16[4096,2,256]{2,1,0:T(2,128)(2,1)S(1)} copy-done((bf16[4096,2,256]{2,1,0:T(2,128)(2,1)S(1)}, bf16[4096,2,256]{2,1,0:T(2,128)(2,1)}, u32[]{:S(2)}) %copy-start.2) | copy-done | bytes 4194328
  8.2 1.7 %prepare.2 = (bf16[5376,256]{1,0:T(8,128)(2,1)S(1)}, bf16[5376,256]{1,0:T(8,128)(2,1)S(1)}, f32[16,256]{1,0:T(8,128)S(1)}) custom-call(s32[2,43]{1,0:T(2,128)S(1)} %lists.1.lists_ref.refs_4_, bf16[4096,2,256]{2,1,0:T(2,128)(2,1)S(1)} %copy-done.2, bf16[256,2,256]{2,1,0:T(2,128)(2,1)S(1)} %copy-done.3, bf16[64,2,256]{2,1,0:T(2,128)(2,1)S(1)} %copy-done.4), custom_call_target="tpu_custom_call" | custom-call | flops 4294967296 | bytes 12582912 | tf_op jit(solution)/shard_map/prepare/pallas_call | solution.py:124
  10.0 0.6 %collective-permute-done.refs_3_ = bf16[64,1024]{1,0:T(8,128)(2,1)S(1)} collective-permute-done((bf16[64,1024]{1,0:T(8,128)(2,1)}, bf16[64,1024]{1,0:T(8,128)(2,1)S(1)}, u32[]{:S(2)}, u32[]{:S(2)}) %collective-permute-start) | collective-permute-done | bytes 131104 | tf_op jit(solution)/shard_map/ppermute | solution.py:287
  10.6 0.8 %collective-permute-start.1 = (bf16[64,1024]{1,0:T(8,128)(2,1)S(1)}, bf16[64,1024]{1,0:T(8,128)(2,1)S(1)}, u32[]{:S(2)}, u32[]{:S(2)}) collective-permute-start(bf16[64,1024]{1,0:T(8,128)(2,1)S(1)} %collective-permute-done.refs_3_), channel_id=1, source_target_pairs={{0,4},{4,0},{8,12},{12,8},{1,5},{5,1},{9,13},{13,9},{2,6},{6,2},{1... | collective-permute-start | bytes 393224 | tf_op jit(solution)/shard_map/ppermute | solution.py:287
  11.4 1.2 %collective-permute-start.2 = (bf16[64,1024]{1,0:T(8,128)(2,1)S(1)}, bf16[64,1024]{1,0:T(8,128)(2,1)S(1)}, u32[]{:S(2)}, u32[]{:S(2)}) collective-permute-start(bf16[64,1024]{1,0:T(8,128)(2,1)S(1)} %copy-done.1), channel_id=1, source_target_pairs={{0,4},{4,0},{8,12},{12,8},{1,5},{5,1},{9,13},{13,9},{2,6},{6,2},{1... | collective-permute-start | bytes 393224 | tf_op jit(solution)/shard_map/ppermute | solution.py:287
  12.6 1.8 %attend.4.refs_4_ = bf16[64,1152]{1,0:T(8,128)(2,1)S(1)} custom-call(f32[16,256]{1,0:T(8,128)S(1)} %get-tuple-element.22.refs_0_, bf16[5376,256]{1,0:T(8,128)(2,1)S(1)} %get-tuple-element.23.refs_1_, bf16[5376,256]{1,0:T(8,128)(2,1)S(1)} %get-tuple-element.24.refs_2_, bf16[64,1024]{1,0:T(8,128)(2,1)S(1)} %collective-permute-done.refs_3_, ...), custom_call_target="tpu_custom_call" | custom-call | flops 67108864 | tf_op jit(solution)/shard_map/attend/pallas_call | solution.py:223
  14.4 2.5 %collective-permute-start.4 = (bf16[64,1152]{1,0:T(8,128)(2,1)S(1)}, bf16[64,1152]{1,0:T(8,128)(2,1)S(1)}, u32[]{:S(2)}, u32[]{:S(2)}) collective-permute-start(bf16[64,1152]{1,0:T(8,128)(2,1)S(1)} %attend.4.refs_4_), channel_id=1, source_target_pairs={{0,8},{4,12},{8,0},{12,4},{1,9},{5,13},{9,1},{13,5},{2,10},{6,14},... | collective-permute-start | bytes 442376 | tf_op jit(solution)/shard_map/ppermute | solution.py:287
  16.9 1.8 %attend.5.refs_0_.refs_4_ = bf16[64,1152]{1,0:T(8,128)(2,1)S(1)} custom-call(f32[16,256]{1,0:T(8,128)S(1)} %get-tuple-element.22.refs_0_, bf16[5376,256]{1,0:T(8,128)(2,1)S(1)} %get-tuple-element.23.refs_1_, bf16[5376,256]{1,0:T(8,128)(2,1)S(1)} %get-tuple-element.24.refs_2_, bf16[64,1024]{1,0:T(8,128)(2,1)S(1)} %collective-permute-done.1.refs_3_, ...), custom_call_target="tpu_custom_call" | custom-call | flops 67108864 | tf_op jit(solution)/shard_map/attend/pallas_call | solution.py:223
  18.6 4.0 %collective-permute-start.3 = (bf16[64,1152]{1,0:T(8,128)(2,1)S(1)}, bf16[64,1152]{1,0:T(8,128)(2,1)S(1)}, u32[]{:S(2)}, u32[]{:S(2)}) collective-permute-start(bf16[64,1152]{1,0:T(8,128)(2,1)S(1)} %attend.5.refs_0_.refs_4_), channel_id=1, source_target_pairs={{0,12},{4,8},{8,4},{12,0},{1,13},{5,9},{9,5},{13,1},{2,14},{6,10},... | collective-permute-start | bytes 442376 | tf_op jit(solution)/shard_map/ppermute | solution.py:287
  22.6 1.8 %prepare.3 = (bf16[5376,256]{1,0:T(8,128)(2,1)S(1)}, bf16[5376,256]{1,0:T(8,128)(2,1)S(1)}, f32[16,256]{1,0:T(8,128)S(1)}) custom-call(s32[2,43]{1,0:T(2,128)S(1)} %lists.1.lists_ref.refs_4_, bf16[4096,2,256]{2,1,0:T(2,128)(2,1)S(1)} %copy-done.2, bf16[256,2,256]{2,1,0:T(2,128)(2,1)S(1)} %copy-done.3, bf16[64,2,256]{2,1,0:T(2,128)(2,1)S(1)} %copy-done.4, ...), custom_call_target="tpu_custom_call" | custom-call | flops 4294967296 | bytes 12582912 | tf_op jit(solution)/shard_map/prepare/pallas_call | solution.py:124
  24.4 2.6 %attend.6.refs_4_ = bf16[64,1152]{1,0:T(8,128)(2,1)S(1)} custom-call(f32[16,256]{1,0:T(8,128)S(1)} %get-tuple-element.26.refs_0_, bf16[5376,256]{1,0:T(8,128)(2,1)S(1)} %get-tuple-element.27.refs_1_, bf16[5376,256]{1,0:T(8,128)(2,1)S(1)} %get-tuple-element.28.refs_2_, bf16[64,1024]{1,0:T(8,128)(2,1)S(1)} %collective-permute-done.2.refs_1_.refs_3_, ...), custom_call_target="tpu_custom_call" | custom-call | flops 67108864 | tf_op jit(solution)/shard_map/attend/pallas_call | solution.py:223
  27.1 2.4 %attend.7.refs_0_ = bf16[64,1152]{1,0:T(8,128)(2,1)S(1)} custom-call(f32[16,256]{1,0:T(8,128)S(1)} %get-tuple-element.26.refs_0_, bf16[5376,256]{1,0:T(8,128)(2,1)S(1)} %get-tuple-element.27.refs_1_, bf16[5376,256]{1,0:T(8,128)(2,1)S(1)} %get-tuple-element.28.refs_2_, bf16[64,1024]{1,0:T(8,128)(2,1)S(1)} %copy-done.1, bf16[64,1152]{1,0:T(8,128)(2,1)S(1)} %attend.6.refs_4_), custom_call_target="tpu_custom_call" | custom-call | flops 67108864 | tf_op jit(solution)/shard_map/attend/pallas_call | solution.py:223
  29.5 2.7 %collective-permute-done.5.refs_3_ = bf16[64,1152]{1,0:T(8,128)(2,1)S(1)} collective-permute-done((bf16[64,1152]{1,0:T(8,128)(2,1)S(1)}, bf16[64,1152]{1,0:T(8,128)(2,1)S(1)}, u32[]{:S(2)}, u32[]{:S(2)}) %collective-permute-start.5) | collective-permute-done | bytes 147488 | tf_op jit(solution)/shard_map/ppermute | solution.py:287
  32.7 0.8 %collective-permute-start.8 = (bf16[64,1024]{1,0:T(8,128)(2,1)S(1)}, bf16[64,1024]{1,0:T(8,128)(2,1)S(1)}, u32[]{:S(2)}, u32[]{:S(2)}) collective-permute-start(bf16[64,1024]{1,0:T(8,128)(2,1)S(1)} %merge.1), channel_id=1, source_target_pairs={{0,8},{4,12},{8,0},{12,4},{1,9},{5,13},{9,1},{13,5},{2,10},{6,14},... | collective-permute-start | bytes 393224 | tf_op jit(solution)/shard_map/ppermute | solution.py:287
  33.5 1.4 %collective-permute-start.6 = (bf16[64,1024]{1,0:T(8,128)(2,1)S(1)}, bf16[64,1024]{1,0:T(8,128)(2,1)S(1)}, u32[]{:S(2)}, u32[]{:S(2)}) collective-permute-start(bf16[64,1024]{1,0:T(8,128)(2,1)S(1)} %merge.1), channel_id=1, source_target_pairs={{0,4},{4,0},{8,12},{12,8},{1,5},{5,1},{9,13},{13,9},{2,6},{6,2},{1... | collective-permute-start | bytes 393224 | tf_op jit(solution)/shard_map/ppermute | solution.py:287
  34.9 5.0 %collective-permute-done.8 = bf16[64,1024]{1,0:T(8,128)(2,1)S(1)} collective-permute-done((bf16[64,1024]{1,0:T(8,128)(2,1)S(1)}, bf16[64,1024]{1,0:T(8,128)(2,1)S(1)}, u32[]{:S(2)}, u32[]{:S(2)}) %collective-permute-start.8) | collective-permute-done | bytes 131104 | tf_op jit(solution)/shard_map/ppermute | solution.py:287
  41.4 3.4 %collective-permute-done.9 = bf16[64,1024]{1,0:T(8,128)(2,1)S(1)} collective-permute-done((bf16[64,1024]{1,0:T(8,128)(2,1)S(1)}, bf16[64,1024]{1,0:T(8,128)(2,1)S(1)}, u32[]{:S(2)}, u32[]{:S(2)}) %collective-permute-start.9) | collective-permute-done | bytes 131104 | tf_op jit(solution)/shard_map/ppermute | solution.py:287
  45.9 0.8 %collective-permute-done.10 = bf16[64,1024]{1,0:T(8,128)(2,1)S(1)} collective-permute-done((bf16[64,1024]{1,0:T(8,128)(2,1)S(1)}, bf16[64,1024]{1,0:T(8,128)(2,1)S(1)}, u32[]{:S(2)}, u32[]{:S(2)}) %collective-permute-start.10) | collective-permute-done | bytes 131104 | tf_op jit(solution)/shard_map/ppermute | solution.py:287
  46.8 1.6 %collective-permute-start.11 = (bf16[64,1024]{1,0:T(8,128)(2,1)S(1)}, bf16[64,1024]{1,0:T(8,128)(2,1)S(1)}, u32[]{:S(2)}, u32[]{:S(2)}) collective-permute-start(bf16[64,1024]{1,0:T(8,128)(2,1)S(1)} %select_convert_fusion), channel_id=1, source_target_pairs={{0,2},{1,3},{2,0},{3,1},{4,6},{5,7},{6,4},{7,5},{8,10},{9,11},{10,... | collective-permute-start | bytes 393224 | tf_op jit(solution)/shard_map/ppermute | solution.py:287
  48.4 4.1 %collective-permute-done.11 = bf16[64,1024]{1,0:T(8,128)(2,1)S(1)} collective-permute-done((bf16[64,1024]{1,0:T(8,128)(2,1)S(1)}, bf16[64,1024]{1,0:T(8,128)(2,1)S(1)}, u32[]{:S(2)}, u32[]{:S(2)}) %collective-permute-start.11) | collective-permute-done | bytes 131104 | tf_op jit(solution)/shard_map/ppermute | solution.py:287
  52.4 0.8 %convert_add_fusion = f32[64,1024]{1,0:T(8,128)} fusion(bf16[64,1024]{1,0:T(8,128)(2,1)S(1)} %collective-permute-done.11, f32[64,1024]{1,0:T(8,128)S(1)} %fusion.3, bf16[64,1024]{1,0:T(8,128)(2,1)S(1)} %collective-permute-done.7, f32[64,1024]{1,0:T(8,128)S(1)} %fusion, bf16[64,1024]{1,0:T(8,128)(2,1)S(1)} %collective-permute-done.10, pred[]{:T(512)S(6)} %eq.13), kind=kLoop, calls=%fused_computation.2 | loop fusion | flops 458752 | bytes 1179649 | tf_op jit(solution)/shard_map/add | solution.py:347
  (25 shorter events, 3.3 us)
Async XLA Ops:
  0.0 40.4 %copy-start = (bf16[1024,1024]{1,0:T(8,128)(2,1)S(1)}, bf16[1024,1024]{1,0:T(8,128)(2,1)}, u32[]{:S(2)}) copy-start(bf16[1024,1024]{1,0:T(8,128)(2,1)} %param.15) | copy-start | bytes 6291460
  0.0 10.5 %collective-permute-start = (bf16[64,1024]{1,0:T(8,128)(2,1)}, bf16[64,1024]{1,0:T(8,128)(2,1)S(1)}, u32[]{:S(2)}, u32[]{:S(2)}) collective-permute-start(bf16[64,1024]{1,0:T(8,128)(2,1)} %refs_3_.1), channel_id=1, source_target_pairs={{0,8},{4,12},{8,0},{12,4},{1,9},{5,13},{9,1},{13,5},{2,10},{6,14},... | collective-permute-start | bytes 393224 | tf_op jit(solution)/shard_map/ppermute | solution.py:287
  6.0 2.2 %copy-start.2 = (bf16[4096,2,256]{2,1,0:T(2,128)(2,1)S(1)}, bf16[4096,2,256]{2,1,0:T(2,128)(2,1)}, u32[]{:S(2)}) copy-start(bf16[4096,2,256]{2,1,0:T(2,128)(2,1)} %cache_ref.3) | copy-start | bytes 12582916
  6.0 2.2 %copy-start.3 = (bf16[256,2,256]{2,1,0:T(2,128)(2,1)S(1)}, bf16[256,2,256]{2,1,0:T(2,128)(2,1)}, u32[]{:S(2)}) copy-start(bf16[256,2,256]{2,1,0:T(2,128)(2,1)} %fin_ref.3) | copy-start | bytes 786436
  6.0 2.2 %copy-start.4 = (bf16[64,2,256]{2,1,0:T(2,128)(2,1)S(1)}, bf16[64,2,256]{2,1,0:T(2,128)(2,1)}, u32[]{:S(2)}) copy-start(bf16[64,2,256]{2,1,0:T(2,128)(2,1)} %own_ref.3) | copy-start | bytes 196612
  8.2 3.1 %copy-start.1 = (bf16[64,1024]{1,0:T(8,128)(2,1)S(1)}, bf16[64,1024]{1,0:T(8,128)(2,1)}, u32[]{:S(2)}) copy-start(bf16[64,1024]{1,0:T(8,128)(2,1)} %refs_3_.1) | copy-start | bytes 393220
  10.6 6.3 %collective-permute-start.1 = (bf16[64,1024]{1,0:T(8,128)(2,1)S(1)}, bf16[64,1024]{1,0:T(8,128)(2,1)S(1)}, u32[]{:S(2)}, u32[]{:S(2)}) collective-permute-start(bf16[64,1024]{1,0:T(8,128)(2,1)S(1)} %collective-permute-done.refs_3_), channel_id=1, source_target_pairs={{0,4},{4,0},{8,12},{12,8},{1,5},{5,1},{9,13},{13,9},{2,6},{6,2},{1... | collective-permute-start | bytes 393224 | tf_op jit(solution)/shard_map/ppermute | solution.py:287
  11.4 11.2 %collective-permute-start.2 = (bf16[64,1024]{1,0:T(8,128)(2,1)S(1)}, bf16[64,1024]{1,0:T(8,128)(2,1)S(1)}, u32[]{:S(2)}, u32[]{:S(2)}) collective-permute-start(bf16[64,1024]{1,0:T(8,128)(2,1)S(1)} %copy-done.1), channel_id=1, source_target_pairs={{0,4},{4,0},{8,12},{12,8},{1,5},{5,1},{9,13},{13,9},{2,6},{6,2},{1... | collective-permute-start | bytes 393224 | tf_op jit(solution)/shard_map/ppermute | solution.py:287
  14.4 15.1 %collective-permute-start.4 = (bf16[64,1152]{1,0:T(8,128)(2,1)S(1)}, bf16[64,1152]{1,0:T(8,128)(2,1)S(1)}, u32[]{:S(2)}, u32[]{:S(2)}) collective-permute-start(bf16[64,1152]{1,0:T(8,128)(2,1)S(1)} %attend.4.refs_4_), channel_id=1, source_target_pairs={{0,8},{4,12},{8,0},{12,4},{1,9},{5,13},{9,1},{13,5},{2,10},{6,14},... | collective-permute-start | bytes 442376 | tf_op jit(solution)/shard_map/ppermute | solution.py:287
  18.6 10.8 %collective-permute-start.3 = (bf16[64,1152]{1,0:T(8,128)(2,1)S(1)}, bf16[64,1152]{1,0:T(8,128)(2,1)S(1)}, u32[]{:S(2)}, u32[]{:S(2)}) collective-permute-start(bf16[64,1152]{1,0:T(8,128)(2,1)S(1)} %attend.5.refs_0_.refs_4_), channel_id=1, source_target_pairs={{0,12},{4,8},{8,4},{12,0},{1,13},{5,9},{9,5},{13,1},{2,14},{6,10},... | collective-permute-start | bytes 442376 | tf_op jit(solution)/shard_map/ppermute | solution.py:287
  27.0 5.2 %collective-permute-start.5 = (bf16[64,1152]{1,0:T(8,128)(2,1)S(1)}, bf16[64,1152]{1,0:T(8,128)(2,1)S(1)}, u32[]{:S(2)}, u32[]{:S(2)}) collective-permute-start(bf16[64,1152]{1,0:T(8,128)(2,1)S(1)} %attend.6.refs_4_), channel_id=1, source_target_pairs={{0,4},{4,0},{8,12},{12,8},{1,5},{5,1},{9,13},{13,9},{2,6},{6,2},{1... | collective-permute-start | bytes 442376 | tf_op jit(solution)/shard_map/ppermute | solution.py:287
  32.7 7.2 %collective-permute-start.8 = (bf16[64,1024]{1,0:T(8,128)(2,1)S(1)}, bf16[64,1024]{1,0:T(8,128)(2,1)S(1)}, u32[]{:S(2)}, u32[]{:S(2)}) collective-permute-start(bf16[64,1024]{1,0:T(8,128)(2,1)S(1)} %merge.1), channel_id=1, source_target_pairs={{0,8},{4,12},{8,0},{12,4},{1,9},{5,13},{9,1},{13,5},{2,10},{6,14},... | collective-permute-start | bytes 393224 | tf_op jit(solution)/shard_map/ppermute | solution.py:287
  33.5 6.9 %collective-permute-start.6 = (bf16[64,1024]{1,0:T(8,128)(2,1)S(1)}, bf16[64,1024]{1,0:T(8,128)(2,1)S(1)}, u32[]{:S(2)}, u32[]{:S(2)}) collective-permute-start(bf16[64,1024]{1,0:T(8,128)(2,1)S(1)} %merge.1), channel_id=1, source_target_pairs={{0,4},{4,0},{8,12},{12,8},{1,5},{5,1},{9,13},{13,9},{2,6},{6,2},{1... | collective-permute-start | bytes 393224 | tf_op jit(solution)/shard_map/ppermute | solution.py:287
  39.9 5.0 %collective-permute-start.9 = (bf16[64,1024]{1,0:T(8,128)(2,1)S(1)}, bf16[64,1024]{1,0:T(8,128)(2,1)S(1)}, u32[]{:S(2)}, u32[]{:S(2)}) collective-permute-start(bf16[64,1024]{1,0:T(8,128)(2,1)S(1)} %collective-permute-done.8), channel_id=1, source_target_pairs={{0,4},{4,0},{8,12},{12,8},{1,5},{5,1},{9,13},{13,9},{2,6},{6,2},{1... | collective-permute-start | bytes 393224 | tf_op jit(solution)/shard_map/ppermute | solution.py:287
  41.4 5.4 %collective-permute-start.7 = (bf16[64,1024]{1,0:T(8,128)(2,1)S(1)}, bf16[64,1024]{1,0:T(8,128)(2,1)S(1)}, u32[]{:S(2)}, u32[]{:S(2)}) collective-permute-start(bf16[64,1024]{1,0:T(8,128)(2,1)S(1)} %convolution_convert_fusion.1), channel_id=1, source_target_pairs={{0,1},{1,0},{2,3},{3,2},{4,5},{5,4},{6,7},{7,6},{8,9},{9,8},{10,11... | collective-permute-start | bytes 393224 | tf_op jit(solution)/shard_map/ppermute | solution.py:287
  45.4 1.4 %collective-permute-start.10 = (bf16[64,1024]{1,0:T(8,128)(2,1)S(1)}, bf16[64,1024]{1,0:T(8,128)(2,1)S(1)}, u32[]{:S(2)}, u32[]{:S(2)}) collective-permute-start(bf16[64,1024]{1,0:T(8,128)(2,1)S(1)} %convolution_convert_fusion), channel_id=1, source_target_pairs={{0,1},{1,0},{2,3},{3,2},{4,5},{5,4},{6,7},{7,6},{8,9},{9,8},{10,11... | collective-permute-start | bytes 393224 | tf_op jit(solution)/shard_map/ppermute | solution.py:287
  46.8 5.6 %collective-permute-start.11 = (bf16[64,1024]{1,0:T(8,128)(2,1)S(1)}, bf16[64,1024]{1,0:T(8,128)(2,1)S(1)}, u32[]{:S(2)}, u32[]{:S(2)}) collective-permute-start(bf16[64,1024]{1,0:T(8,128)(2,1)S(1)} %select_convert_fusion), channel_id=1, source_target_pairs={{0,2},{1,3},{2,0},{3,1},{4,6},{5,7},{6,4},{7,5},{8,10},{9,11},{10,... | collective-permute-start | bytes 393224 | tf_op jit(solution)/shard_map/ppermute | solution.py:287
